TPU v7x, 32 devices: a whole 2x2x4 slice. The times are simulated.
32 devices in a mesh: dp: 8 (over y, x, core), mp: 4 (over z).
Axes of the slice: x: 2, y: 2, z: 4, core: 2. Of those that a mesh axis runs over, the one named last changes fastest.
Arguments:
- text_tokens: bfloat16 [64, 128, 768], P(('dp', 'mp')), may hold values from -6 to 6
- image_regions: bfloat16 [64, 36, 1024], P(('dp', 'mp')), may hold values from -6 to 6
- lengths: int32 [64], P(('dp', 'mp')), may hold values from 8 to 128
- region_counts: int32 [64], P(('dp', 'mp')), may hold values from 10 to 36
- text_cross: bfloat16 [3, 768, 1024], P(None, None, 'mp'), may hold values from -0.21875 to 0.21875
- image_cross: bfloat16 [3, 1024, 1024], P(None, None, 'mp'), may hold values from -0.1875 to 0.1875
- text_cross_out: bfloat16 [1024, 768], P('mp'), may hold values from -0.5 to 0.5
- image_cross_out: bfloat16 [1024, 1024], P('mp'), may hold values from -0.5 to 0.5
- text_up: bfloat16 [768, 3072], P(None, 'mp'), may hold values from -0.21875 to 0.21875
- text_down: bfloat16 [3072, 768], P('mp'), may hold values from -0.15625 to 0.15625
- image_up: bfloat16 [1024, 1024], P(None, 'mp'), may hold values from -0.1875 to 0.1875
- image_down: bfloat16 [1024, 1024], P('mp'), may hold values from -0.25 to 0.25
- text_self: bfloat16 [3, 768, 768], P(None, None, 'mp'), may hold values from -0.21875 to 0.21875
- text_self_out: bfloat16 [768, 768], P('mp'), may hold values from -0.625 to 0.625
- image_self: bfloat16 [3, 1024, 1024], P(None, None, 'mp'), may hold values from -0.1875 to 0.1875
- image_self_out: bfloat16 [1024, 1024], P('mp'), may hold values from -0.5 to 0.5
- text_gains: float32 [3, 768], replicated, may hold values from 0.5 to 1.5
- text_shifts: float32 [3, 768], replicated, may hold values from -1.75 to 1.75
- image_gains: float32 [3, 1024], replicated, may hold values from 0.5 to 1.5
- image_shifts: float32 [3, 1024], replicated, may hold values from -1.75 to 1.75
- text_cotangent: bfloat16 [64, 128, 768], P(('dp', 'mp')), may hold values from -6 to 6
- image_cotangent: bfloat16 [64, 36, 1024], P(('dp', 'mp')), may hold values from -6 to 6
Outputs:
- text_output: float32 [64, 128, 768], P(('dp', 'mp'))
- image_output: float32 [64, 36, 1024], P(('dp', 'mp'))
- text_grad: float32 [64, 128, 768], P(('dp', 'mp'))
- image_grad: float32 [64, 36, 1024], P(('dp', 'mp'))
- text_cross_grad: float32 [3, 768, 1024], P(None, 'dp', 'mp')
- image_cross_grad: float32 [3, 1024, 1024], P(None, 'dp', 'mp')
- text_cross_out_grad: float32 [1024, 768], P('mp', 'dp')
- image_cross_out_grad: float32 [1024, 1024], P('mp', 'dp')
- text_up_grad: float32 [768, 3072], P('dp', 'mp')
- text_down_grad: float32 [3072, 768], P('mp', 'dp')
- image_up_grad: float32 [1024, 1024], P('dp', 'mp')
- image_down_grad: float32 [1024, 1024], P('mp', 'dp')
- text_self_grad: float32 [3, 768, 768], P(None, 'dp', 'mp')
- text_self_out_grad: float32 [768, 768], P('mp', 'dp')
- image_self_grad: float32 [3, 1024, 1024], P(None, 'dp', 'mp')
- image_self_out_grad: float32 [1024, 1024], P('mp', 'dp')
- text_gains_grad: float32 [3, 768], replicated
- text_shifts_grad: float32 [3, 768], replicated
- image_gains_grad: float32 [3, 1024], replicated
- image_shifts_grad: float32 [3, 1024], replicated
Inputs may be any that keep to these rules, and one draw needn't show every extreme that they name: `lengths`: text slots at or beyond a pair's length are padding and are never attended to. `region_counts`: image regions at or beyond a pair's count are padding and are never attended to.
All inputs are finite; a program needn't handle non-finite values.
Results may differ from a plain program's by a relative error of at most 0.039.
Values may be sent and summed in bfloat16 or wider, within the bound.
A program may use at most 192 MiB of HBM per device.

v0:
```python
import math

import jax
import jax.numpy as jnp
from jax import lax
from jax.sharding import PartitionSpec as P

TEXT_HEAD = 64
CROSS_HEAD = 128
IMAGE_HEAD = 128


EPSILON = 1e-05
MASKED = -1e30


def project(inputs, weight):
    return jnp.dot(inputs, weight, preferred_element_type=jnp.float32)


def project_back(gradient, weight):
    return lax.dot_general(
        gradient,
        weight,
        (((gradient.ndim - 1,), (1,)), ((), ())),
        preferred_element_type=jnp.float32,
    )


def weight_grad(inputs, gradient):
    flat_in = inputs.reshape(-1, inputs.shape[-1])
    flat_grad = gradient.reshape(-1, gradient.shape[-1])
    return lax.dot_general(
        flat_in, flat_grad, (((0,), (0,)), ((), ())), preferred_element_type=jnp.float32
    )


def layer_norm(hidden, scales, offsets):
    average = jnp.mean(hidden, -1, keepdims=True)
    centred = hidden - average
    spread = jnp.mean(centred * centred, -1, keepdims=True)
    return centred * lax.rsqrt(spread + EPSILON) * scales + offsets


def norm_back(hidden, scales, offsets, gradient):
    unused, pullback = jax.vjp(layer_norm, hidden, scales, offsets)
    return pullback(gradient)


def gelu_exact(values):
    return jax.nn.gelu(values, approximate=False)


def split_heads(rows, head_size):
    return rows.reshape(rows.shape[0], rows.shape[1], rows.shape[2] // head_size, head_size)


def scores_of(query_heads, key_heads, visible, head_size):
    scores = jnp.einsum(
        "plhe,pmhe->phlm", query_heads, key_heads, preferred_element_type=jnp.float32
    ) / math.sqrt(head_size)
    return jnp.where(visible[:, None, None, :], scores, MASKED)


def attend(queries, key_rows, value_rows, visible, head_size):
    scores = scores_of(
        split_heads(queries, head_size), split_heads(key_rows, head_size), visible, head_size
    )
    highest = jnp.max(scores, -1, keepdims=True)
    log_total = highest + jnp.log(jnp.sum(jnp.exp(scores - highest), -1, keepdims=True))
    probs = jnp.exp(scores - log_total).astype(jnp.bfloat16)
    context = jnp.einsum(
        "phlm,pmhe->plhe",
        probs,
        split_heads(value_rows, head_size),
        preferred_element_type=jnp.float32,
    )
    return (context.reshape(queries.shape).astype(jnp.bfloat16), log_total)


def attend_back(queries, key_rows, value_rows, visible, head_size, log_total, context_grad):
    query_heads = split_heads(queries, head_size)
    key_heads = split_heads(key_rows, head_size)
    value_heads = split_heads(value_rows, head_size)
    grad_heads = split_heads(context_grad, head_size)
    probs = jnp.exp(scores_of(query_heads, key_heads, visible, head_size) - log_total)
    value_grad = jnp.einsum(
        "phlm,plhe->pmhe",
        probs.astype(jnp.bfloat16),
        grad_heads,
        preferred_element_type=jnp.float32,
    )
    prob_grad = jnp.einsum(
        "plhe,pmhe->phlm", grad_heads, value_heads, preferred_element_type=jnp.float32
    )
    inner = jnp.sum(probs * prob_grad, -1, keepdims=True)
    score_grad = (probs * (prob_grad - inner)).astype(jnp.bfloat16)
    query_grad = jnp.einsum(
        "phlm,pmhe->plhe", score_grad, key_heads, preferred_element_type=jnp.float32
    ) / math.sqrt(head_size)
    key_grad = jnp.einsum(
        "phlm,plhe->pmhe", score_grad, query_heads, preferred_element_type=jnp.float32
    ) / math.sqrt(head_size)
    return (
        query_grad.reshape(queries.shape).astype(jnp.bfloat16),
        key_grad.reshape(key_rows.shape).astype(jnp.bfloat16),
        value_grad.reshape(value_rows.shape).astype(jnp.bfloat16),
    )


def project_three(group_rows, weights):
    return tuple((project(group_rows, weights[number]).astype(jnp.bfloat16) for number in range(3)))


def stacked_grads(group_rows, grads):
    return jnp.stack(
        [
            weight_grad(group_rows, grads[0]),
            weight_grad(group_rows, grads[1]),
            weight_grad(group_rows, grads[2]),
        ]
    )


def input_part(grads, weights):
    return (
        project_back(grads[0], weights[0])
        + project_back(grads[1], weights[1])
        + project_back(grads[2], weights[2])
    )


def cross_forward(text_group, image_group, text_cross, image_cross, text_mask, image_mask):
    text_proj = project_three(text_group, text_cross)
    image_proj = project_three(image_group, image_cross)
    text_context, text_total = attend(
        text_proj[0], image_proj[1], image_proj[2], image_mask, CROSS_HEAD
    )
    image_context, image_total = attend(
        image_proj[0], text_proj[1], text_proj[2], text_mask, CROSS_HEAD
    )
    return (text_proj, image_proj, (text_context, image_context), (text_total, image_total))


def cross_back(
    text_group,
    image_group,
    text_cross,
    image_cross,
    text_cross_out,
    image_cross_out,
    text_mask,
    image_mask,
    text_coming,
    image_coming,
):
    text_proj, image_proj, contexts, totals = cross_forward(
        text_group, image_group, text_cross, image_cross, text_mask, image_mask
    )
    text_out_grad = weight_grad(contexts[0], text_coming)
    image_out_grad = weight_grad(contexts[1], image_coming)
    text_ctx_grad = project_back(text_coming, text_cross_out).astype(jnp.bfloat16)
    image_ctx_grad = project_back(image_coming, image_cross_out).astype(jnp.bfloat16)
    text_query_grad, image_key_grad, image_value_grad = attend_back(
        text_proj[0], image_proj[1], image_proj[2], image_mask, CROSS_HEAD, totals[0], text_ctx_grad
    )
    image_query_grad, text_key_grad, text_value_grad = attend_back(
        image_proj[0], text_proj[1], text_proj[2], text_mask, CROSS_HEAD, totals[1], image_ctx_grad
    )
    text_grads = (text_query_grad, text_key_grad, text_value_grad)
    image_grads = (image_query_grad, image_key_grad, image_value_grad)
    return (
        stacked_grads(text_group, text_grads),
        stacked_grads(image_group, image_grads),
        text_out_grad,
        image_out_grad,
        input_part(text_grads, text_cross),
        input_part(image_grads, image_cross),
    )


def ffn_forward(group_rows, up_weight, down_weight):
    upper = project(group_rows, up_weight)
    middle = gelu_exact(upper).astype(jnp.bfloat16)
    return (upper, middle, project(middle, down_weight))


def ffn_back(group_rows, upper, middle, up_weight, down_weight, coming):
    down_grad = weight_grad(middle, coming)
    middle_grad = project_back(coming, down_weight)
    unused, pullback = jax.vjp(gelu_exact, upper)
    upper_grad = pullback(middle_grad)[0].astype(jnp.bfloat16)
    return (weight_grad(group_rows, upper_grad), down_grad, project_back(upper_grad, up_weight))


def self_forward(group_rows, weights, out_weight, visible, head_size):
    proj = project_three(group_rows, weights)
    context, log_total = attend(proj[0], proj[1], proj[2], visible, head_size)
    return (proj, context, log_total, project(context, out_weight))


def self_back(group_rows, saved, weights, out_weight, visible, head_size, coming):
    proj, context, log_total = (saved[0], saved[1], saved[2])
    out_grad = weight_grad(context, coming)
    context_grad = project_back(coming, out_weight).astype(jnp.bfloat16)
    grads = attend_back(proj[0], proj[1], proj[2], visible, head_size, log_total, context_grad)
    return (stacked_grads(group_rows, grads), out_grad, input_part(grads, weights))


def gather_pairs(text_tokens, image_regions, seen_local):
    return (
        lax.all_gather(text_tokens, "mp", axis=0, tiled=True),
        lax.all_gather(image_regions, "mp", axis=0, tiled=True),
        lax.all_gather(seen_local, "mp", axis=0, tiled=True),
    )


def gather_layer(text_low, image_low):
    return (
        lax.all_gather(text_low, "mp", axis=0, tiled=True),
        lax.all_gather(image_low, "mp", axis=0, tiled=True),
    )


def sum_branch(text_part, image_part):
    return (
        lax.psum_scatter(
            text_part.astype(jnp.bfloat16), "mp", scatter_dimension=0, tiled=True
        ).astype(jnp.float32),
        lax.psum_scatter(
            image_part.astype(jnp.bfloat16), "mp", scatter_dimension=0, tiled=True
        ).astype(jnp.float32),
    )


def gather_grads(text_grad, image_grad):
    return (
        lax.all_gather(text_grad, "mp", axis=0, tiled=True),
        lax.all_gather(image_grad, "mp", axis=0, tiled=True),
    )


def sum_inputs(text_part, image_part):
    return (
        lax.psum_scatter(
            text_part.astype(jnp.bfloat16), "mp", scatter_dimension=0, tiled=True
        ).astype(jnp.float32),
        lax.psum_scatter(
            image_part.astype(jnp.bfloat16), "mp", scatter_dimension=0, tiled=True
        ).astype(jnp.float32),
    )


def shards(
    text_tokens,
    image_regions,
    lengths,
    region_counts,
    text_cross,
    image_cross,
    text_cross_out,
    image_cross_out,
    text_up,
    text_down,
    image_up,
    image_down,
    text_self,
    text_self_out,
    image_self,
    image_self_out,
    text_gains,
    text_shifts,
    image_gains,
    image_shifts,
    text_cotangent,
    image_cotangent,
):
    slot_count = text_tokens.shape[1]
    region_total = image_regions.shape[1]
    text_seen = jnp.arange(slot_count, dtype=jnp.int32)[None, :] < lengths[:, None]
    image_seen = jnp.arange(region_total, dtype=jnp.int32)[None, :] < region_counts[:, None]
    seen_local = jnp.concatenate([text_seen, image_seen], 1).astype(jnp.bfloat16)
    text_first, image_first, seen_group = gather_pairs(text_tokens, image_regions, seen_local)
    text_mask = seen_group[:, :slot_count] > 0.5
    image_mask = seen_group[:, slot_count:] > 0.5
    text_input = text_tokens.astype(jnp.float32)
    image_input = image_regions.astype(jnp.float32)
    unused_text, unused_image, contexts, unused_totals = cross_forward(
        text_first, image_first, text_cross, image_cross, text_mask, image_mask
    )
    text_branch, image_branch = sum_branch(
        project(contexts[0], text_cross_out), project(contexts[1], image_cross_out)
    )
    text_hidden_a = text_input + text_branch
    image_hidden_a = image_input + image_branch
    text_mid = layer_norm(text_hidden_a, text_gains[0], text_shifts[0])
    image_mid = layer_norm(image_hidden_a, image_gains[0], image_shifts[0])
    text_second, image_second = gather_layer(
        text_mid.astype(jnp.bfloat16), image_mid.astype(jnp.bfloat16)
    )
    text_upper, text_middle, text_part = ffn_forward(text_second, text_up, text_down)
    image_upper, image_middle, image_part = ffn_forward(image_second, image_up, image_down)
    text_branch, image_branch = sum_branch(text_part, image_part)
    text_hidden_b = text_mid + text_branch
    image_hidden_b = image_mid + image_branch
    text_mixed = layer_norm(text_hidden_b, text_gains[1], text_shifts[1])
    image_mixed = layer_norm(image_hidden_b, image_gains[1], image_shifts[1])
    text_third, image_third = gather_layer(
        text_mixed.astype(jnp.bfloat16), image_mixed.astype(jnp.bfloat16)
    )
    text_saved = self_forward(text_third, text_self, text_self_out, text_mask, TEXT_HEAD)
    image_saved = self_forward(image_third, image_self, image_self_out, image_mask, IMAGE_HEAD)
    text_branch, image_branch = sum_branch(text_saved[3], image_saved[3])
    text_hidden_c = text_mixed + text_branch
    image_hidden_c = image_mixed + image_branch
    text_result = layer_norm(text_hidden_c, text_gains[2], text_shifts[2])
    image_result = layer_norm(image_hidden_c, image_gains[2], image_shifts[2])
    text_grad_c, text_gain_c, text_shift_c = norm_back(
        text_hidden_c, text_gains[2], text_shifts[2], text_cotangent.astype(jnp.float32)
    )
    image_grad_c, image_gain_c, image_shift_c = norm_back(
        image_hidden_c, image_gains[2], image_shifts[2], image_cotangent.astype(jnp.float32)
    )
    text_coming, image_coming = gather_grads(
        text_grad_c.astype(jnp.bfloat16), image_grad_c.astype(jnp.bfloat16)
    )
    text_self_w, text_self_o, text_part = self_back(
        text_third, text_saved, text_self, text_self_out, text_mask, TEXT_HEAD, text_coming
    )
    image_self_w, image_self_o, image_part = self_back(
        image_third, image_saved, image_self, image_self_out, image_mask, IMAGE_HEAD, image_coming
    )
    text_inner, image_inner = sum_inputs(text_part, image_part)
    text_mixed_grad = text_grad_c + text_inner
    image_mixed_grad = image_grad_c + image_inner
    text_grad_b, text_gain_b, text_shift_b = norm_back(
        text_hidden_b, text_gains[1], text_shifts[1], text_mixed_grad
    )
    image_grad_b, image_gain_b, image_shift_b = norm_back(
        image_hidden_b, image_gains[1], image_shifts[1], image_mixed_grad
    )
    text_coming, image_coming = gather_grads(
        text_grad_b.astype(jnp.bfloat16), image_grad_b.astype(jnp.bfloat16)
    )
    text_up_w, text_down_w, text_part = ffn_back(
        text_second, text_upper, text_middle, text_up, text_down, text_coming
    )
    image_up_w, image_down_w, image_part = ffn_back(
        image_second, image_upper, image_middle, image_up, image_down, image_coming
    )
    text_inner, image_inner = sum_inputs(text_part, image_part)
    text_mid_grad = text_grad_b + text_inner
    image_mid_grad = image_grad_b + image_inner
    text_grad_a, text_gain_a, text_shift_a = norm_back(
        text_hidden_a, text_gains[0], text_shifts[0], text_mid_grad
    )
    image_grad_a, image_gain_a, image_shift_a = norm_back(
        image_hidden_a, image_gains[0], image_shifts[0], image_mid_grad
    )
    text_coming, image_coming = gather_grads(
        text_grad_a.astype(jnp.bfloat16), image_grad_a.astype(jnp.bfloat16)
    )
    cross_grads = cross_back(
        text_first,
        image_first,
        text_cross,
        image_cross,
        text_cross_out,
        image_cross_out,
        text_mask,
        image_mask,
        text_coming,
        image_coming,
    )
    text_inner, image_inner = sum_inputs(cross_grads[4], cross_grads[5])
    text_input_grad = text_grad_a + text_inner
    image_input_grad = image_grad_a + image_inner
    shares = (
        lax.psum_scatter(cross_grads[0], "dp", scatter_dimension=1, tiled=True),
        lax.psum_scatter(cross_grads[1], "dp", scatter_dimension=1, tiled=True),
        lax.psum_scatter(cross_grads[2], "dp", scatter_dimension=1, tiled=True),
        lax.psum_scatter(cross_grads[3], "dp", scatter_dimension=1, tiled=True),
        lax.psum_scatter(text_up_w, "dp", scatter_dimension=0, tiled=True),
        lax.psum_scatter(text_down_w, "dp", scatter_dimension=1, tiled=True),
        lax.psum_scatter(image_up_w, "dp", scatter_dimension=0, tiled=True),
        lax.psum_scatter(image_down_w, "dp", scatter_dimension=1, tiled=True),
        lax.psum_scatter(text_self_w, "dp", scatter_dimension=1, tiled=True),
        lax.psum_scatter(text_self_o, "dp", scatter_dimension=1, tiled=True),
        lax.psum_scatter(image_self_w, "dp", scatter_dimension=1, tiled=True),
        lax.psum_scatter(image_self_o, "dp", scatter_dimension=1, tiled=True),
    )
    norm_totals = lax.psum(
        (
            jnp.stack([text_gain_a, text_gain_b, text_gain_c]),
            jnp.stack([text_shift_a, text_shift_b, text_shift_c]),
            jnp.stack([image_gain_a, image_gain_b, image_gain_c]),
            jnp.stack([image_shift_a, image_shift_b, image_shift_c]),
        ),
        ("dp", "mp"),
    )
    return (
        text_result,
        image_result,
        text_input_grad,
        image_input_grad,
        shares[0],
        shares[1],
        shares[2],
        shares[3],
        shares[4],
        shares[5],
        shares[6],
        shares[7],
        shares[8],
        shares[9],
        shares[10],
        shares[11],
        norm_totals[0],
        norm_totals[1],
        norm_totals[2],
        norm_totals[3],
    )


def solution(mesh):
    in_specs = (
        P(("dp", "mp"), None, None),
        P(("dp", "mp"), None, None),
        P(("dp", "mp")),
        P(("dp", "mp")),
        P(None, None, "mp"),
        P(None, None, "mp"),
        P("mp", None),
        P("mp", None),
        P(None, "mp"),
        P("mp", None),
        P(None, "mp"),
        P("mp", None),
        P(None, None, "mp"),
        P("mp", None),
        P(None, None, "mp"),
        P("mp", None),
        P(),
        P(),
        P(),
        P(),
        P(("dp", "mp"), None, None),
        P(("dp", "mp"), None, None),
    )
    out_specs = (
        P(("dp", "mp"), None, None),
        P(("dp", "mp"), None, None),
        P(("dp", "mp"), None, None),
        P(("dp", "mp"), None, None),
        P(None, "dp", "mp"),
        P(None, "dp", "mp"),
        P("mp", "dp"),
        P("mp", "dp"),
        P("dp", "mp"),
        P("mp", "dp"),
        P("dp", "mp"),
        P("mp", "dp"),
        P(None, "dp", "mp"),
        P("mp", "dp"),
        P(None, "dp", "mp"),
        P("mp", "dp"),
        P(),
        P(),
        P(),
        P(),
    )
    return jax.shard_map(shards, mesh=mesh, in_specs=in_specs, out_specs=out_specs, check_vma=False)
```

profile of v0, /device:TPU:0, one launch (start us, length us, event | category | flops | bytes accessed | tf_op | source)
XLA Modules:
  0.0 1196.2 jit_solution(5372635378197834408)
XLA Ops:
  9.5 12.7 %all-gather = bf16[4,2,164]{2,1,0:T(2,128)(2,1)S(1)} all-gather(bf16[1,2,164]{2,1,0:T(2,128)(2,1)S(1)} %fusion.195), channel_id=1, replica_groups=mesh['dp'=8,'mp'=4] {'mp'}, dimensions={0}, use_global_device_ids=true | all-gather | bytes 3280 | tf_op jit(solution)/shard_map/all_gather | solution.py:214
  23.1 25.7 %all_gather.39 = bf16[8,36,1024]{2,1,0:T(8,128)(2,1)S(1)} all-gather(bf16[2,36,1024]{2,1,0:T(8,128)(2,1)S(1)} %copy.166), channel_id=1, replica_groups=mesh['dp'=8,'mp'=4] {'mp'}, dimensions={0}, use_global_device_ids=true | all-gather | bytes 737280 | tf_op jit(solution)/shard_map/all_gather | solution.py:213
  51.9 6.9 all-gather.8.cloned.1.call-done
  58.8 2.0 fusion.12
  63.0 1.8 convolution_convert_fusion.3
  65.5 34.8 %reduce-scatter.31.cloned.1.call-done = bf16[2,128,768]{2,1,0:T(8,128)(2,1)} async-done(((bf16[8,128,768]{2,1,0:T(8,128)(2,1)}), bf16[2,128,768]{2,1,0:T(8,128)(2,1)}) %reduce-scatter.31.cloned.1.call-update) | async-done | bytes 393232 | tf_op jit(solution)/shard_map/reduce_scatter | solution.py:227
  103.9 36.0 %all-gather.10.cloned.1.call-done = bf16[8,128,768]{2,1,0:T(8,128)(2,1)} async-done(((bf16[2,128,768]{2,1,0:T(8,128)(2,1)}), bf16[8,128,768]{2,1,0:T(8,128)(2,1)}) %all-gather.10.cloned.1.call-update) | async-done | bytes 1572880 | tf_op jit(solution)/shard_map/all_gather | solution.py:220
  139.9 3.4 fusion.42
  143.4 7.9 multiply_convert_fusion
  152.4 2.5 convolution_convert_fusion.2
  156.5 2.2 fusion.14
  164.4 25.0 %reduce-scatter.33.cloned.1.call-done = bf16[2,128,768]{2,1,0:T(8,128)(2,1)} async-done(((bf16[8,128,768]{2,1,0:T(8,128)(2,1)}), bf16[2,128,768]{2,1,0:T(8,128)(2,1)}) %reduce-scatter.33.cloned.1.call-update) | async-done | bytes 393232 | tf_op jit(solution)/shard_map/reduce_scatter | solution.py:227
  193.9 19.6 %reduce-scatter.37.cloned.1.call-done = bf16[2,36,1024]{2,1,0:T(8,128)(2,1)} async-done(((bf16[8,36,1024]{2,1,0:T(8,128)(2,1)}), bf16[2,36,1024]{2,1,0:T(8,128)(2,1)}) %reduce-scatter.37.cloned.1.call-update) | async-done | bytes 147472 | tf_op jit(solution)/shard_map/reduce_scatter | solution.py:230
  217.3 21.4 %all_gather.44 = bf16[8,36,1024]{2,1,0:T(8,128)(2,1)S(1)} all-gather(bf16[2,36,1024]{2,1,0:T(8,128)(2,1)S(1)} %fusion.146), channel_id=1, replica_groups=mesh['dp'=8,'mp'=4] {'mp'}, dimensions={0}, use_global_device_ids=true | all-gather | bytes 737280 | tf_op jit(solution)/shard_map/all_gather | solution.py:221
  244.2 12.9 %all-gather.12.cloned.1.call-done = bf16[8,128,768]{2,1,0:T(8,128)(2,1)} async-done(((bf16[2,128,768]{2,1,0:T(8,128)(2,1)}), bf16[8,128,768]{2,1,0:T(8,128)(2,1)}) %all-gather.12.cloned.1.call-update) | async-done | bytes 1572880 | tf_op jit(solution)/shard_map/all_gather | solution.py:220
  257.1 2.2 convolution_convert_fusion.17
  264.4 1.8 convolution_convert_fusion.1
  266.2 15.3 %reduce-scatter.39.cloned.1.call-done = bf16[2,36,1024]{2,1,0:T(8,128)(2,1)} async-done(((bf16[8,36,1024]{2,1,0:T(8,128)(2,1)}), bf16[2,36,1024]{2,1,0:T(8,128)(2,1)}) %reduce-scatter.39.cloned.1.call-update) | async-done | bytes 147472 | tf_op jit(solution)/shard_map/reduce_scatter | solution.py:230
  284.6 22.8 %all_gather.45 = bf16[8,36,1024]{2,1,0:T(8,128)(2,1)S(1)} all-gather(bf16[2,36,1024]{2,1,0:T(8,128)(2,1)S(1)} %fusion.147), channel_id=1, replica_groups=mesh['dp'=8,'mp'=4] {'mp'}, dimensions={0}, use_global_device_ids=true | all-gather | bytes 737280 | tf_op jit(solution)/shard_map/all_gather | solution.py:221
  312.0 12.9 %reduce-scatter.35.cloned.1.call-done = bf16[2,128,768]{2,1,0:T(8,128)(2,1)} async-done(((bf16[8,128,768]{2,1,0:T(8,128)(2,1)}), bf16[2,128,768]{2,1,0:T(8,128)(2,1)}) %reduce-scatter.35.cloned.1.call-update) | async-done | bytes 393232 | tf_op jit(solution)/shard_map/reduce_scatter | solution.py:227
  331.0 18.5 %reduce-scatter.41.cloned.1.call-done = bf16[2,36,1024]{2,1,0:T(8,128)(2,1)} async-done(((bf16[8,36,1024]{2,1,0:T(8,128)(2,1)}), bf16[2,36,1024]{2,1,0:T(8,128)(2,1)}) %reduce-scatter.41.cloned.1.call-update) | async-done | bytes 147472 | tf_op jit(solution)/shard_map/reduce_scatter | solution.py:230
  351.6 1.7 fusion.126
  353.9 33.3 %all-gather.14.cloned.1.call-done = bf16[8,128,768]{2,1,0:T(8,128)(2,1)} async-done(((bf16[2,128,768]{2,1,0:T(8,128)(2,1)}), bf16[8,128,768]{2,1,0:T(8,128)(2,1)}) %all-gather.14.cloned.1.call-update) | async-done | bytes 1572880 | tf_op jit(solution)/shard_map/all_gather | solution.py:238
  387.2 2.1 convolution_convert_fusion.15
  394.6 1.8 add_convert_fusion.2
  398.4 23.5 %all_gather.49 = bf16[8,36,1024]{2,1,0:T(8,128)(2,1)S(1)} all-gather(bf16[2,36,1024]{2,1,0:T(8,128)(2,1)S(1)} %add_convert_fusion.9), channel_id=1, replica_groups=mesh['dp'=8,'mp'=4] {'mp'}, dimensions={0}, use_global_device_ids=true | all-gather | bytes 737280 | tf_op jit(solution)/shard_map/all_gather | solution.py:239
  426.4 12.4 %reduce-scatter.43.cloned.1.call-done = bf16[2,128,768]{2,1,0:T(8,128)(2,1)} async-done(((bf16[8,128,768]{2,1,0:T(8,128)(2,1)}), bf16[2,128,768]{2,1,0:T(8,128)(2,1)}) %reduce-scatter.43.cloned.1.call-update) | async-done | bytes 393232 | tf_op jit(solution)/shard_map/reduce_scatter | solution.py:245
  438.8 2.1 multiply_reduce_fusion.1
  443.1 21.1 %reduce-scatter.47.cloned.1.call-done = bf16[2,36,1024]{2,1,0:T(8,128)(2,1)} async-done(((bf16[8,36,1024]{2,1,0:T(8,128)(2,1)}), bf16[2,36,1024]{2,1,0:T(8,128)(2,1)}) %reduce-scatter.47.cloned.1.call-update) | async-done | bytes 147472 | tf_op jit(solution)/shard_map/reduce_scatter | solution.py:248
  464.2 1.8 multiply_reduce_fusion.8
  467.3 21.2 %all_gather.50 = bf16[8,36,1024]{2,1,0:T(8,128)(2,1)S(1)} all-gather(bf16[2,36,1024]{2,1,0:T(8,128)(2,1)S(1)} %add_convert_fusion.8), channel_id=1, replica_groups=mesh['dp'=8,'mp'=4] {'mp'}, dimensions={0}, use_global_device_ids=true | all-gather | bytes 737280 | tf_op jit(solution)/shard_map/all_gather | solution.py:239
  492.5 14.9 %all-gather.16.cloned.1.call-done = bf16[8,128,768]{2,1,0:T(8,128)(2,1)} async-done(((bf16[2,128,768]{2,1,0:T(8,128)(2,1)}), bf16[8,128,768]{2,1,0:T(8,128)(2,1)}) %all-gather.16.cloned.1.call-update) | async-done | bytes 1572880 | tf_op jit(solution)/shard_map/all_gather | solution.py:238
  507.4 5.6 add_convert_fusion.1
  514.2 2.6 convolution_convert_fusion
  516.9 14.7 %reduce-scatter.49.cloned.1.call-done = bf16[2,36,1024]{2,1,0:T(8,128)(2,1)} async-done(((bf16[8,36,1024]{2,1,0:T(8,128)(2,1)}), bf16[2,36,1024]{2,1,0:T(8,128)(2,1)}) %reduce-scatter.49.cloned.1.call-update) | async-done | bytes 147472 | tf_op jit(solution)/shard_map/reduce_scatter | solution.py:248
  532.9 35.1 %reduce-scatter.45.cloned.1.call-done = bf16[2,128,768]{2,1,0:T(8,128)(2,1)} async-done(((bf16[8,128,768]{2,1,0:T(8,128)(2,1)}), bf16[2,128,768]{2,1,0:T(8,128)(2,1)}) %reduce-scatter.45.cloned.1.call-update) | async-done | bytes 393232 | tf_op jit(solution)/shard_map/reduce_scatter | solution.py:245
  568.0 2.1 multiply_reduce_fusion.2
  572.9 21.2 %all_gather.51 = bf16[8,36,1024]{2,1,0:T(8,128)(2,1)S(1)} all-gather(bf16[2,36,1024]{2,1,0:T(8,128)(2,1)S(1)} %add_convert_fusion.7), channel_id=1, replica_groups=mesh['dp'=8,'mp'=4] {'mp'}, dimensions={0}, use_global_device_ids=true | all-gather | bytes 737280 | tf_op jit(solution)/shard_map/all_gather | solution.py:239
  600.8 2.8 copy.260
  603.6 4.7 reshape.500
  611.0 3.3 fusion.103
  614.3 2.1 fusion.15
  623.5 1.8 add_convert_fusion
  628.7 2.8 copy.258
  631.4 3.9 copy.270
  638.8 1.9 pad_maximum_fusion
  651.0 2.0 pad_maximum_fusion.1
  654.3 4.2 convolution_bitcast_fusion
  660.0 4.4 convolution_bitcast_fusion.1
  670.5 23.3 %reduce-scatter.75.cloned.1.call-done = f32[96,576]{1,0:T(8,128)} async-done(((f32[768,576]{1,0:T(8,128)}), f32[96,576]{1,0:T(8,128)}) %reduce-scatter.75.cloned.1.call-update) | async-done | bytes 221200
  695.8 41.0 %all-reduce = (f32[3,768]{1,0:T(4,128)}, f32[3,768]{1,0:T(4,128)}, f32[3,1024]{1,0:T(4,128)}, f32[3,1024]{1,0:T(4,128)}) all-reduce(f32[3,768]{1,0:T(4,128)S(1)} %pad_maximum_fusion.6, f32[3,768]{1,0:T(4,128)S(1)} %pad_maximum_fusion.7, f32[3,1024]{1,0:T(4,128)S(1)} %pad_maximum_fusion.4, ...), channel_id=1, replica_groups=mesh['dp'=8,'mp'=4] {'dp','mp'}, use_global_device_ids=true, to_apply=%region_63.64 | all-reduce | flops 10752 | bytes 86016 | tf_op jit(solution)/shard_map/psum | solution.py:392
  738.8 16.3 %reduce-scatter.51.cloned.1.call-done = bf16[2,128,768]{2,1,0:T(8,128)(2,1)} async-done(((bf16[8,128,768]{2,1,0:T(8,128)(2,1)}), bf16[2,128,768]{2,1,0:T(8,128)(2,1)}) %reduce-scatter.51.cloned.1.call-update) | async-done | bytes 393232 | tf_op jit(solution)/shard_map/reduce_scatter | solution.py:245
  755.1 2.1 convert_add_fusion
  757.2 42.5 %reduce-scatter.73.cloned.1.call-done = f32[96,768]{1,0:T(8,128)} async-done(((f32[768,768]{1,0:T(8,128)}), f32[96,768]{1,0:T(8,128)}) %reduce-scatter.73.cloned.1.call-update) | async-done | bytes 294928
  801.5 47.6 %reduce-scatter.55.cloned.1.call-done = f32[3,128,256]{1,2,0:T(8,128)} async-done(((f32[3,1024,256]{1,2,0:T(8,128)}), f32[3,128,256]{1,2,0:T(8,128)}) %reduce-scatter.55.cloned.1.call-update) | async-done | bytes 393232 | tf_op jit(solution)/shard_map/reduce_scatter | solution.py:380
  849.1 1.9 copy.242
  851.0 37.8 %reduce-scatter.71.cloned.1.call-done = f32[256,128]{1,0:T(8,128)} async-done(((f32[256,1024]{1,0:T(8,128)}), f32[256,128]{1,0:T(8,128)}) %reduce-scatter.71.cloned.1.call-update) | async-done | bytes 131088 | tf_op jit(solution)/shard_map/reduce_scatter | solution.py:390
  888.9 39.6 %reduce-scatter.67.cloned.1.call-done = f32[256,128]{1,0:T(8,128)} async-done(((f32[256,1024]{1,0:T(8,128)}), f32[256,128]{1,0:T(8,128)}) %reduce-scatter.67.cloned.1.call-update) | async-done | bytes 131088 | tf_op jit(solution)/shard_map/reduce_scatter | solution.py:386
  928.5 39.7 %reduce-scatter.65.cloned.1.call-done = f32[128,256]{1,0:T(8,128)} async-done(((f32[1024,256]{1,0:T(8,128)}), f32[128,256]{1,0:T(8,128)}) %reduce-scatter.65.cloned.1.call-update) | async-done | bytes 131088 | tf_op jit(solution)/shard_map/reduce_scatter | solution.py:385
  968.2 39.6 %reduce-scatter.59.cloned.1.call-done = f32[256,128]{1,0:T(8,128)} async-done(((f32[256,1024]{1,0:T(8,128)}), f32[256,128]{1,0:T(8,128)}) %reduce-scatter.59.cloned.1.call-update) | async-done | bytes 131088 | tf_op jit(solution)/shard_map/reduce_scatter | solution.py:382
  1007.8 49.9 %reduce-scatter.69.cloned.1.call-done = f32[3,128,256]{2,1,0:T(8,128)} async-done(((f32[3,1024,256]{2,1,0:T(8,128)}), f32[3,128,256]{2,1,0:T(8,128)}) %reduce-scatter.69.cloned.1.call-update) | async-done | bytes 393232 | tf_op jit(solution)/shard_map/reduce_scatter | solution.py:389
  1057.7 46.3 %reduce-scatter.63.cloned.1.call-done = f32[768,96]{0,1:T(8,128)} async-done(((f32[768,768]{0,1:T(8,128)}), f32[768,96]{0,1:T(8,128)}) %reduce-scatter.63.cloned.1.call-update) | async-done | bytes 294928 | tf_op jit(solution)/shard_map/reduce_scatter | solution.py:384
  1104.0 46.3 %reduce-scatter.61.cloned.1.call-done = f32[96,768]{1,0:T(8,128)} async-done(((f32[768,768]{1,0:T(8,128)}), f32[96,768]{1,0:T(8,128)}) %reduce-scatter.61.cloned.1.call-update) | async-done | bytes 294928 | tf_op jit(solution)/shard_map/reduce_scatter | solution.py:383
  1150.4 38.5 %reduce-scatter.57.cloned.1.call-done = f32[256,96]{0,1:T(8,128)} async-done(((f32[256,768]{0,1:T(8,128)}), f32[256,96]{0,1:T(8,128)}) %reduce-scatter.57.cloned.1.call-update) | async-done | bytes 98320 | tf_op jit(solution)/shard_map/reduce_scatter | solution.py:381
  (651 shorter events, 126.7 us)
Async XLA Ops:
  7.2 132.7 %copy-start = (bf16[768,768]{1,0:T(8,128)(2,1)S(1)}, bf16[768,768]{1,0:T(8,128)(2,1)}, u32[]{:S(2)}) copy-start(bf16[768,768]{1,0:T(8,128)(2,1)} %param.30) | copy-start | bytes 3538948
  7.2 51.6 %all-gather.8.cloned.1.call-start = ((), (), s32[]{:S(2)}) async-start(), calls=%async_computation.24 | async-start | bytes 1966080 | tf_op jit(solution)/shard_map/all_gather | solution.py:212
  7.9 92.4 %reduce-scatter.31.cloned.1.call-start = ((), (), s32[]{:S(2)}) async-start(), calls=%async_computation.25 | async-start | bytes 1966080 | tf_op jit(solution)/shard_map/reduce_scatter | solution.py:227
  48.7 106.3 %copy-start.99 = (bf16[8,36,1024]{2,1,0:T(8,128)(2,1)}, bf16[8,36,1024]{2,1,0:T(8,128)(2,1)S(1)}, u32[]{:S(2)}) copy-start(bf16[8,36,1024]{2,1,0:T(8,128)(2,1)S(1)} %all_gather.39) | copy-start | bytes 1769476
  63.0 37.4 %copy-start.2 = (bf16[2,128,768]{2,1,0:T(8,128)(2,1)S(1)}, bf16[2,128,768]{2,1,0:T(8,128)(2,1)}, u32[]{:S(2)}) copy-start(bf16[2,128,768]{2,1,0:T(8,128)(2,1)} %param.22) | copy-start | bytes 1179652
  64.8 75.1 %all-gather.10.cloned.1.call-start = ((), (), s32[]{:S(2)}) async-start(), calls=%async_computation.26 | async-start | bytes 1966080 | tf_op jit(solution)/shard_map/all_gather | solution.py:220
  65.5 123.9 %copy-start.135 = (f32[768]{0:T(1024)}, f32[768]{0:T(1024)S(1)}, u32[]{:S(2)}) copy-start(f32[768]{0:T(1024)S(1)} %get-tuple-element.163) | copy-start | bytes 9220
  65.5 126.2 %copy-start.137 = (f32[768]{0:T(1024)}, f32[768]{0:T(1024)S(1)}, u32[]{:S(2)}) copy-start(f32[768]{0:T(1024)S(1)} %get-tuple-element.162) | copy-start | bytes 9220
  65.5 126.2 %copy-start.146 = (f32[768]{0:T(1024)}, f32[768]{0:T(1024)S(1)}, u32[]{:S(2)}) copy-start(f32[768]{0:T(1024)S(1)} %get-tuple-element.107) | copy-start | bytes 9220
  101.6 87.8 %copy-start.139 = (f32[2,128]{1,0:T(2,128)}, f32[2,128]{1,0:T(2,128)S(1)}, u32[]{:S(2)}) copy-start(f32[2,128]{1,0:T(2,128)S(1)} %broadcast_multiply_fusion.5) | copy-start | bytes 3076
  102.8 40.5 %copy-start.182 = (f32[2,128]{1,0:T(2,128)}, f32[2,128]{1,0:T(2,128)S(1)}, u32[]{:S(2)}) copy-start(f32[2,128]{1,0:T(2,128)S(1)} %multiply_reduce_fusion.7) | copy-start | bytes 3076
  102.9 86.6 %copy-start.151 = (f32[2,128]{1,0:T(2,128)}, f32[2,128]{1,0:T(2,128)S(1)}, u32[]{:S(2)}) copy-start(f32[2,128]{1,0:T(2,128)S(1)} %fusion.196) | copy-start | bytes 3076
  103.9 85.6 %reduce-scatter.33.cloned.1.call-start = ((), (), s32[]{:S(2)}) async-start(), calls=%async_computation.27 | async-start | bytes 1966080 | tf_op jit(solution)/shard_map/reduce_scatter | solution.py:227
  155.0 58.6 %reduce-scatter.37.cloned.1.call-start = ((), (), s32[]{:S(2)}) async-start(), calls=%async_computation.30 | async-start | bytes 819200 | tf_op jit(solution)/shard_map/reduce_scatter | solution.py:230
  164.1 92.9 %all-gather.12.cloned.1.call-start = ((), (), s32[]{:S(2)}) async-start(), calls=%async_computation.28 | async-start | bytes 1966080 | tf_op jit(solution)/shard_map/all_gather | solution.py:220
  191.1 47.6 %copy-start.153 = (f32[2,128]{1,0:T(2,128)}, f32[2,128]{1,0:T(2,128)S(1)}, u32[]{:S(2)}) copy-start(f32[2,128]{1,0:T(2,128)S(1)} %fusion.197) | copy-start | bytes 3076
  191.7 48.0 %copy-start.116 = (bf16[1024,256]{1,0:T(8,128)(2,1)S(1)}, bf16[1024,256]{1,0:T(8,128)(2,1)}, u32[]{:S(2)}) copy-start(bf16[1024,256]{1,0:T(8,128)(2,1)} %param.32) | copy-start | bytes 1572868
  192.7 88.9 %reduce-scatter.39.cloned.1.call-start = ((), (), s32[]{:S(2)}) async-start(), calls=%async_computation.31 | async-start | bytes 819200 | tf_op jit(solution)/shard_map/reduce_scatter | solution.py:230
  193.3 45.4 %copy-start.132 = (f32[1,1024]{1,0:T(1,128)}, f32[1,1024]{1,0:T(1,128)S(1)}, u32[]{:S(2)}) copy-start(f32[1,1024]{1,0:T(1,128)S(1)} %get-tuple-element.139) | copy-start | bytes 12292
  193.9 44.8 %copy-start.144 = (f32[1,1024]{1,0:T(1,128)}, f32[1,1024]{1,0:T(1,128)S(1)}, u32[]{:S(2)}) copy-start(f32[1,1024]{1,0:T(1,128)S(1)} %get-tuple-element.142) | copy-start | bytes 12292
  244.1 80.8 %reduce-scatter.35.cloned.1.call-start = ((), (), s32[]{:S(2)}) async-start(), calls=%async_computation.29 | async-start | bytes 1966080 | tf_op jit(solution)/shard_map/reduce_scatter | solution.py:227
  266.2 83.4 %reduce-scatter.41.cloned.1.call-start = ((), (), s32[]{:S(2)}) async-start(), calls=%async_computation.32 | async-start | bytes 819200 | tf_op jit(solution)/shard_map/reduce_scatter | solution.py:230
  281.6 25.8 %copy-start.51 = (bf16[3,1024,256]{2,1,0:T(8,128)(2,1)S(1)}, bf16[3,1024,256]{2,1,0:T(8,128)(2,1)}, u32[]{:S(2)}) copy-start(bf16[3,1024,256]{2,1,0:T(8,128)(2,1)} %param.36) | copy-start | bytes 4718596
  283.0 24.7 %copy-start.13 = (f32[2,36,1024]{2,1,0:T(8,128)}, f32[2,36,1024]{2,1,0:T(8,128)S(1)}, u32[]{:S(2)}) copy-start(f32[2,36,1024]{2,1,0:T(8,128)S(1)} %get-tuple-element.127) | copy-start | bytes 884740
  312.0 75.2 %all-gather.14.cloned.1.call-start = ((), (), s32[]{:S(2)}) async-start(), calls=%async_computation.33 | async-start | bytes 1966080 | tf_op jit(solution)/shard_map/all_gather | solution.py:238
  330.5 108.2 %reduce-scatter.43.cloned.1.call-start = ((), (), s32[]{:S(2)}) async-start(), calls=%async_computation.34 | async-start | bytes 1966080 | tf_op jit(solution)/shard_map/reduce_scatter | solution.py:245
  396.4 25.5 %copy-start.48 = (bf16[256,1024]{1,0:T(8,128)(2,1)S(1)}, bf16[256,1024]{1,0:T(8,128)(2,1)}, u32[]{:S(2)}) copy-start(bf16[256,1024]{1,0:T(8,128)(2,1)} %param.37) | copy-start | bytes 1572868
  396.5 67.8 %reduce-scatter.47.cloned.1.call-start = ((), (), s32[]{:S(2)}) async-start(), calls=%async_computation.38 | async-start | bytes 819200 | tf_op jit(solution)/shard_map/reduce_scatter | solution.py:248
  398.3 24.4 %copy-start.28 = (f32[2,36,1024]{2,1,0:T(8,128)}, f32[2,36,1024]{2,1,0:T(8,128)S(1)}, u32[]{:S(2)}) copy-start(f32[2,36,1024]{2,1,0:T(8,128)S(1)} %get-tuple-element.117) | copy-start | bytes 884740
  398.3 24.4 %copy-start.174 = (f32[2,36]{1,0:T(2,128)}, f32[2,36]{1,0:T(2,128)S(1)}, u32[]{:S(2)}) copy-start(f32[2,36]{1,0:T(2,128)S(1)} %negate_multiply_fusion.4) | copy-start | bytes 868
  398.4 24.3 %copy-start.70 = (bf16[8,36,256]{2,0,1:T(8,128)(2,1)S(1)}, bf16[8,36,256]{2,0,1:T(8,128)(2,1)}, u32[]{:S(2)}) copy-start(bf16[8,36,256]{2,0,1:T(8,128)(2,1)} %copy-done.69) | copy-start | bytes 442372
  426.4 81.0 %all-gather.16.cloned.1.call-start = ((), (), s32[]{:S(2)}) async-start(), calls=%async_computation.35 | async-start | bytes 1966080 | tf_op jit(solution)/shard_map/all_gather | solution.py:238
  443.0 46.4 %copy-start.122 = (f32[8,36,256]{2,1,0:T(8,128)S(1)}, f32[8,36,256]{2,1,0:T(8,128)}, u32[]{:S(2)}) copy-start(f32[8,36,256]{2,1,0:T(8,128)} %copy-done.121) | copy-start | bytes 884740
  443.0 88.6 %reduce-scatter.49.cloned.1.call-start = ((), (), s32[]{:S(2)}) async-start(), calls=%async_computation.39 | async-start | bytes 819200 | tf_op jit(solution)/shard_map/reduce_scatter | solution.py:248
  492.3 75.7 %reduce-scatter.45.cloned.1.call-start = ((), (), s32[]{:S(2)}) async-start(), calls=%async_computation.36 | async-start | bytes 1966080 | tf_op jit(solution)/shard_map/reduce_scatter | solution.py:245
  516.8 51.2 %copy-start.3 = (bf16[2,128,768]{2,1,0:T(8,128)(2,1)S(1)}, bf16[2,128,768]{2,1,0:T(8,128)(2,1)}, u32[]{:S(2)}) copy-start(bf16[2,128,768]{2,1,0:T(8,128)(2,1)} %param.22) | copy-start | bytes 1179652
  516.8 51.2 %copy-start.7 = (bf16[2,128,768]{2,1,0:T(8,128)(2,1)S(1)}, bf16[2,128,768]{2,1,0:T(8,128)(2,1)}, u32[]{:S(2)}) copy-start(bf16[2,128,768]{2,1,0:T(8,128)(2,1)} %reduce-scatter.31.cloned.1.call-done) | copy-start | bytes 1179652
  516.8 51.2 %copy-start.136 = (f32[768]{0:T(1024)S(1)}, f32[768]{0:T(1024)}, u32[]{:S(2)}) copy-start(f32[768]{0:T(1024)} %copy-done.135) | copy-start | bytes 9220
  516.8 51.2 %copy-start.140 = (f32[2,128]{1,0:T(2,128)S(1)}, f32[2,128]{1,0:T(2,128)}, u32[]{:S(2)}) copy-start(f32[2,128]{1,0:T(2,128)} %copy-done.139) | copy-start | bytes 3076
  516.8 51.1 %copy-start.152 = (f32[2,128]{1,0:T(2,128)S(1)}, f32[2,128]{1,0:T(2,128)}, u32[]{:S(2)}) copy-start(f32[2,128]{1,0:T(2,128)} %copy-done.151) | copy-start | bytes 3076
  516.9 53.3 %copy-start.183 = (f32[2,128]{1,0:T(2,128)S(1)}, f32[2,128]{1,0:T(2,128)}, u32[]{:S(2)}) copy-start(f32[2,128]{1,0:T(2,128)} %copy-done.182) | copy-start | bytes 3076
  516.9 97.4 %all-gather.18.cloned.1.call-start = ((), (), s32[]{:S(2)}) async-start(), calls=%async_computation.37 | async-start | bytes 1966080 | tf_op jit(solution)/shard_map/all_gather | solution.py:238
  572.4 96.4 %reduce-scatter.77.cloned.1.call-start = ((), (), s32[]{:S(2)}) async-start(), calls=%async_computation.53 | async-start | bytes 884736
  598.2 95.6 %reduce-scatter.75.cloned.1.call-start = ((), (), s32[]{:S(2)}) async-start(), calls=%async_computation.52 | async-start | bytes 2211840
  608.3 128.6 %reduce-scatter.53.cloned.1.call-start = ((), (), s32[]{:S(2)}) async-start(), calls=%async_computation.41 | async-start | bytes 819200 | tf_op jit(solution)/shard_map/reduce_scatter | solution.py:248
  620.3 134.8 %reduce-scatter.51.cloned.1.call-start = ((), (), s32[]{:S(2)}) async-start(), calls=%async_computation.40 | async-start | bytes 1966080 | tf_op jit(solution)/shard_map/reduce_scatter | solution.py:245
  625.3 174.3 %reduce-scatter.73.cloned.1.call-start = ((), (), s32[]{:S(2)}) async-start(), calls=%async_computation.51 | async-start | bytes 2654208
  635.4 213.7 %reduce-scatter.55.cloned.1.call-start = ((), (), s32[]{:S(2)}) async-start(), calls=%async_computation.42 | async-start | bytes 3538944 | tf_op jit(solution)/shard_map/reduce_scatter | solution.py:380
  640.7 248.2 %reduce-scatter.71.cloned.1.call-start = ((), (), s32[]{:S(2)}) async-start(), calls=%async_computation.50 | async-start | bytes 1179648 | tf_op jit(solution)/shard_map/reduce_scatter | solution.py:390
  643.5 285.0 %reduce-scatter.67.cloned.1.call-start = ((), (), s32[]{:S(2)}) async-start(), calls=%async_computation.48 | async-start | bytes 1179648 | tf_op jit(solution)/shard_map/reduce_scatter | solution.py:386
  645.0 323.2 %reduce-scatter.65.cloned.1.call-start = ((), (), s32[]{:S(2)}) async-start(), calls=%async_computation.47 | async-start | bytes 1179648 | tf_op jit(solution)/shard_map/reduce_scatter | solution.py:385
  646.7 361.2 %reduce-scatter.59.cloned.1.call-start = ((), (), s32[]{:S(2)}) async-start(), calls=%async_computation.44 | async-start | bytes 1179648 | tf_op jit(solution)/shard_map/reduce_scatter | solution.py:382
  648.7 409.1 %reduce-scatter.69.cloned.1.call-start = ((), (), s32[]{:S(2)}) async-start(), calls=%async_computation.49 | async-start | bytes 3538944 | tf_op jit(solution)/shard_map/reduce_scatter | solution.py:389
  653.0 451.1 %reduce-scatter.63.cloned.1.call-start = ((), (), s32[]{:S(2)}) async-start(), calls=%async_computation.46 | async-start | bytes 2654208 | tf_op jit(solution)/shard_map/reduce_scatter | solution.py:384
  658.6 491.8 %reduce-scatter.61.cloned.1.call-start = ((), (), s32[]{:S(2)}) async-start(), calls=%async_computation.45 | async-start | bytes 2654208 | tf_op jit(solution)/shard_map/reduce_scatter | solution.py:383
  664.5 524.4 %reduce-scatter.57.cloned.1.call-start = ((), (), s32[]{:S(2)}) async-start(), calls=%async_computation.43 | async-start | bytes 884736 | tf_op jit(solution)/shard_map/reduce_scatter | solution.py:381
  667.7 28.0 %copy-start.170 = (f32[768]{0:T(1024)S(1)}, f32[768]{0:T(1024)}, u32[]{:S(2)}) copy-start(f32[768]{0:T(1024)} %get-tuple-element.84) | copy-start | bytes 9220
  667.7 28.0 %copy-start.169 = (f32[768]{0:T(1024)S(1)}, f32[768]{0:T(1024)}, u32[]{:S(2)}) copy-start(f32[768]{0:T(1024)} %get-tuple-element.87) | copy-start | bytes 9220
  667.7 28.0 %copy-start.171 = (f32[768]{0:T(1024)S(1)}, f32[768]{0:T(1024)}, u32[]{:S(2)}) copy-start(f32[768]{0:T(1024)} %get-tuple-element.82) | copy-start | bytes 9220
  667.7 69.1 %copy-start.42 = (f32[2,36,1024]{2,1,0:T(8,128)S(1)}, f32[2,36,1024]{2,1,0:T(8,128)}, u32[]{:S(2)}) copy-start(f32[2,36,1024]{2,1,0:T(8,128)} %copy-done.41) | copy-start | bytes 884740
  667.7 69.1 %copy-start.179 = (f32[2,36]{1,0:T(2,128)S(1)}, f32[2,36]{1,0:T(2,128)}, u32[]{:S(2)}) copy-start(f32[2,36]{1,0:T(2,128)} %copy-done.178) | copy-start | bytes 868
  668.7 86.3 %copy-start.22 = (f32[2,128,768]{2,1,0:T(8,128)S(1)}, f32[2,128,768]{2,1,0:T(8,128)}, u32[]{:S(2)}) copy-start(f32[2,128,768]{2,1,0:T(8,128)} %copy-done.21) | copy-start | bytes 2359300
  668.8 86.3 %copy-start.177 = (f32[2,128]{1,0:T(2,128)S(1)}, f32[2,128]{1,0:T(2,128)}, u32[]{:S(2)}) copy-start(f32[2,128]{1,0:T(2,128)} %copy-done.176) | copy-start | bytes 3076
  755.1 433.8 %copy-start.1 = (bf16[768,768]{1,0:T(8,128)(2,1)S(1)}, bf16[768,768]{1,0:T(8,128)(2,1)}, u32[]{:S(2)}) copy-start(bf16[768,768]{1,0:T(8,128)(2,1)} %param.30) | copy-start | bytes 3538948
  (170 other events, 883.9 us)
Sparse Core Ops, SparseCore 0:
  9.6 49.1 all-gather.7
  64.9 35.3 reduce-scatter.30
  104.0 35.8 all-gather.9
  155.1 34.2 reduce-scatter.32
  192.1 21.3 reduce-scatter.36
  215.6 41.4 all-gather.11
  259.9 21.5 reduce-scatter.38
  283.9 41.0 reduce-scatter.34
  327.2 22.2 reduce-scatter.40
  351.5 35.6 all-gather.13
  396.6 42.1 reduce-scatter.42
  440.9 23.2 reduce-scatter.46
  466.3 40.9 all-gather.15
  510.1 21.4 reduce-scatter.48
  533.8 34.1 reduce-scatter.44
  572.6 40.6 all-gather.17
  616.3 34.0 reduce-scatter.76
  653.6 40.1 reduce-scatter.74
  696.1 22.7 reduce-scatter.52
  721.0 34.0 reduce-scatter.50
  758.4 41.1 reduce-scatter.72
  803.0 46.0 reduce-scatter.54
  852.9 35.9 reduce-scatter.70
  892.5 35.9 reduce-scatter.66
  932.2 35.9 reduce-scatter.64
  971.8 35.9 reduce-scatter.58
  1011.6 46.0 reduce-scatter.68
  1061.6 42.3 reduce-scatter.62
  1108.0 42.3 reduce-scatter.60
  1153.9 34.9 reduce-scatter.56
where the time goes:
time: 1210 us; the launch traced here: 1200 us
  waiting for transfers between devices  782 us (65%)
  blocking collectives  189 us (16%)
  matrix products  93 us (8%)
  local copies, waits for them, and re-layouts  58.4 us (5%)
  other arithmetic  53.1 us (4%)
  between operations  17.6 us (1%)
    reduce_scatter x3, waiting for transfers between devices, sum_branch(): lax.psum_scatter(text_part.astype(jnp.bfloat16), 'mp', scatter_dimension=...  72.8 us
    unnamed x33, waiting for transfers between devices  66.9 us
    all_gather x3, blocking collectives, gather_grads(): lax.all_gather(image_grad, 'mp', axis=0, tiled=True)  65.9 us
    reduce_scatter x3, waiting for transfers between devices, sum_inputs(): lax.psum_scatter(text_part.astype(jnp.bfloat16), 'mp', scatter_dimension=...  63.7 us
    unnamed x422, local copies, waits for them, and re-layouts  56 us
    reduce_scatter x3, waiting for transfers between devices, sum_branch(): lax.psum_scatter(image_part.astype(jnp.bfloat16), 'mp', scatter_dimension...  53.5 us
    reduce_scatter x1, waiting for transfers between devices, shards(): lax.psum_scatter(image_self_w, 'dp', scatter_dimension=1, tiled=True)  49.9 us
    all_gather x2, waiting for transfers between devices, gather_layer(): lax.all_gather(text_low, 'mp', axis=0, tiled=True)  48.9 us
  transfers between devices with their start and end apart: 30, of which 27 were waited for; matrix products, arithmetic and copies ran while one was open for 12% of the time, Pallas kernels for 0%

commit v1 on v0

v1 whole, which is shorter than its diff:
```python
import functools
import math

import jax
import jax.numpy as jnp
from jax import lax
from jax.experimental import pallas as pl
from jax.experimental.pallas import tpu as pltpu
from jax.sharding import PartitionSpec as P

TEXT_HEAD = 64
CROSS_HEAD = 128
IMAGE_HEAD = 128


EPSILON = 1e-05
MASKED = -1e30


def project(inputs, weight):
    return jnp.dot(inputs, weight, preferred_element_type=jnp.float32)


def project_back(gradient, weight):
    return lax.dot_general(
        gradient,
        weight,
        (((gradient.ndim - 1,), (1,)), ((), ())),
        preferred_element_type=jnp.float32,
    )


def layer_norm(hidden, scales, offsets):
    average = jnp.mean(hidden, -1, keepdims=True)
    centred = hidden - average
    spread = jnp.mean(centred * centred, -1, keepdims=True)
    return centred * lax.rsqrt(spread + EPSILON) * scales + offsets


def norm_back(hidden, scales, offsets, gradient):
    unused, pullback = jax.vjp(layer_norm, hidden, scales, offsets)
    return pullback(gradient)


def gelu_exact(values):
    return jax.nn.gelu(values, approximate=False)


def split_heads(rows, head_size):
    return rows.reshape(rows.shape[0], rows.shape[1], rows.shape[2] // head_size, head_size)


def scores_of(query_heads, key_heads, visible, head_size):
    scores = jnp.einsum(
        "plhe,pmhe->phlm", query_heads, key_heads, preferred_element_type=jnp.float32
    ) / math.sqrt(head_size)
    return jnp.where(visible[:, None, None, :], scores, MASKED)


def attend(queries, key_rows, value_rows, visible, head_size):
    scores = scores_of(
        split_heads(queries, head_size), split_heads(key_rows, head_size), visible, head_size
    )
    highest = jnp.max(scores, -1, keepdims=True)
    log_total = highest + jnp.log(jnp.sum(jnp.exp(scores - highest), -1, keepdims=True))
    probs = jnp.exp(scores - log_total).astype(jnp.bfloat16)
    context = jnp.einsum(
        "phlm,pmhe->plhe",
        probs,
        split_heads(value_rows, head_size),
        preferred_element_type=jnp.float32,
    )
    return (context.reshape(queries.shape).astype(jnp.bfloat16), log_total)


def attend_back(queries, key_rows, value_rows, visible, head_size, log_total, context_grad):
    query_heads = split_heads(queries, head_size)
    key_heads = split_heads(key_rows, head_size)
    value_heads = split_heads(value_rows, head_size)
    grad_heads = split_heads(context_grad, head_size)
    probs = jnp.exp(scores_of(query_heads, key_heads, visible, head_size) - log_total)
    value_grad = jnp.einsum(
        "phlm,plhe->pmhe",
        probs.astype(jnp.bfloat16),
        grad_heads,
        preferred_element_type=jnp.float32,
    )
    prob_grad = jnp.einsum(
        "plhe,pmhe->phlm", grad_heads, value_heads, preferred_element_type=jnp.float32
    )
    inner = jnp.sum(probs * prob_grad, -1, keepdims=True)
    score_grad = (probs * (prob_grad - inner)).astype(jnp.bfloat16)
    query_grad = jnp.einsum(
        "phlm,pmhe->plhe", score_grad, key_heads, preferred_element_type=jnp.float32
    ) / math.sqrt(head_size)
    key_grad = jnp.einsum(
        "phlm,plhe->pmhe", score_grad, query_heads, preferred_element_type=jnp.float32
    ) / math.sqrt(head_size)
    return (
        query_grad.reshape(queries.shape).astype(jnp.bfloat16),
        key_grad.reshape(key_rows.shape).astype(jnp.bfloat16),
        value_grad.reshape(value_rows.shape).astype(jnp.bfloat16),
    )


def project_three(group_rows, weights):
    return tuple((project(group_rows, weights[number]).astype(jnp.bfloat16) for number in range(3)))


def input_part(grads, weights):
    return (
        project_back(grads[0], weights[0])
        + project_back(grads[1], weights[1])
        + project_back(grads[2], weights[2])
    )


def cross_forward(text_group, image_group, text_cross, image_cross, text_mask, image_mask):
    text_proj = project_three(text_group, text_cross)
    image_proj = project_three(image_group, image_cross)
    text_context, text_total = attend(
        text_proj[0], image_proj[1], image_proj[2], image_mask, CROSS_HEAD
    )
    image_context, image_total = attend(
        image_proj[0], text_proj[1], text_proj[2], text_mask, CROSS_HEAD
    )
    return (text_proj, image_proj, (text_context, image_context), (text_total, image_total))


def ffn_forward(group_rows, up_weight, down_weight):
    upper = project(group_rows, up_weight)
    middle = gelu_exact(upper).astype(jnp.bfloat16)
    return (upper, middle, project(middle, down_weight))


def ffn_back(upper, up_weight, down_weight, coming):
    middle_grad = project_back(coming, down_weight)
    unused, pullback = jax.vjp(gelu_exact, upper)
    upper_grad = pullback(middle_grad)[0].astype(jnp.bfloat16)
    return (upper_grad, project_back(upper_grad, up_weight))


def self_forward(group_rows, weights, out_weight, visible, head_size):
    proj = project_three(group_rows, weights)
    context, log_total = attend(proj[0], proj[1], proj[2], visible, head_size)
    return (proj, context, log_total, project(context, out_weight))


def self_back(saved, weights, out_weight, visible, head_size, coming):
    proj, context, log_total = (saved[0], saved[1], saved[2])
    context_grad = project_back(coming, out_weight).astype(jnp.bfloat16)
    grads = attend_back(proj[0], proj[1], proj[2], visible, head_size, log_total, context_grad)
    return (grads, input_part(grads, weights))


MESH_ID = pl.DeviceIdType.MESH


def flip(index, step):
    return index + step * (1 - 2 * ((index // step) % 2))


def position():
    data, model = lax.axis_index("dp"), lax.axis_index("mp")
    return data, model, data % 2, (data // 2) % 2, (data // 4) % 2


def greet(data, model):
    barrier = pltpu.get_barrier_semaphore()
    partners = [(flip(data, step), model) for step in (1, 2, 4)]
    partners += [(data, flip(model, step)) for step in (1, 2)]
    for partner in partners:
        pl.semaphore_signal(barrier, inc=1, device_id=partner, device_id_type=MESH_ID)
    pl.semaphore_wait(barrier, len(partners))


def view_of(ref, kind, shard, width, y, x, c):
    if kind == "col3":
        columns = pl.ds(pl.multiple_of(shard * width, 128), width)
        return ref.at[:, y, x, c, :, columns]
    if kind == "col":
        columns = pl.ds(pl.multiple_of(shard * width, 128), width)
        return ref.at[y, x, c, :, columns]
    if kind == "row":
        return ref.at[shard, y, x, c]
    return ref.at[shard, :, y, x, c]


def local_of(ref, kind, y, x, c):
    if kind in ("col3", "split3"):
        return ref.at[:, y, x, c]
    return ref.at[y, x, c]


def gather_kernel(kinds, widths, streams, *refs):
    count = len(kinds)
    ins, outs = refs[:count], refs[count : 2 * count]
    own_sem, send_sem, recv_sem = refs[2 * count :]
    data, model, c, x, y = position()
    every = slice(None)
    near, far = flip(model, 1), flip(model, 2)
    corner = flip(near, 2)
    owns = []
    for k in range(count):
        own = pltpu.make_async_copy(
            ins[k], view_of(outs[k], kinds[k], model, widths[k], every, every, every), own_sem.at[k]
        )
        own.start()
        owns.append(own)
    greet(data, model)

    def send(k, slot, source, target, partner):
        copy = pltpu.make_async_remote_copy(
            src_ref=source,
            dst_ref=target,
            send_sem=send_sem.at[k, slot],
            recv_sem=recv_sem.at[k, slot],
            device_id=partner,
            device_id_type=MESH_ID,
        )
        copy.start()
        return copy

    def piece(k, shard, y, x, c):
        return view_of(outs[k], kinds[k], shard, widths[k], y, x, c)

    copies = {}
    for k in range(count):
        mine = local_of(ins[k], kinds[k], y, x, c)
        copies[k, 0] = send(k, 0, mine, piece(k, model, y, x, c), (data, far))

    def pair_up(k):
        mine = local_of(ins[k], kinds[k], y, x, c)
        copies[k, 1] = send(k, 1, mine, piece(k, model, y, x, c), (data, near))
        copies[k, 0].wait_recv()
        block = piece(k, far, y, x, c)
        copies[k, 2] = send(k, 2, block, block, (data, near))

    def spread(k, stage):
        first_x = streams[k] == (stage == 0)
        if stage == 2:
            where, partner = (every, every, c), (flip(data, 1), model)
        elif stage == 0:
            where = (y, x, c)
            partner = (flip(data, 2 if first_x else 4), model)
        else:
            where = (y, every, c) if streams[k] else (every, x, c)
            partner = (flip(data, 2 if first_x else 4), model)
        base = 3 + 3 * stage
        for number, shard in enumerate((far, near, corner)):
            if stage == 0:
                if number > 0:
                    copies[k, number].wait_recv()
            else:
                copies[k, base - 3 + number].wait_recv()
            block = piece(k, shard, *where)
            copies[k, base + number] = send(k, base + number, block, block, partner)

    for step in range(count + 3):
        if step < count:
            pair_up(step)
        for stage in range(3):
            k = step - 1 - stage
            if 0 <= k < count:
                spread(k, stage)
    for k in range(count):
        for number in range(3):
            copies[k, 9 + number].wait_recv()
        owns[k].wait()
        for slot in range(12):
            copies[k, slot].wait_send()


def gather_all(arrays, kinds, streams, mp):
    ins, outs, widths, finals = [], [], [], []
    for array, kind in zip(arrays, kinds):
        widths.append(array.shape[-1])
        rows, width = array.shape[-2] // 8, array.shape[-1]
        if kind in ("col3", "split3"):
            ins.append(array.reshape(array.shape[0], 2, 2, 2, rows, width))
        else:
            ins.append(array.reshape(2, 2, 2, rows, width))
        if kind == "col3":
            shape, final = (array.shape[0], 2, 2, 2, rows, mp * width), (array.shape[0], 8 * rows, mp * width)
        elif kind == "col":
            shape, final = (2, 2, 2, rows, mp * width), (8 * rows, mp * width)
        elif kind == "row":
            shape, final = (mp, 2, 2, 2, rows, width), (mp * 8 * rows, width)
        else:
            shape = (mp, array.shape[0], 2, 2, 2, rows, width)
            final = (mp, array.shape[0], 8 * rows, width)
        outs.append(jax.ShapeDtypeStruct(shape, array.dtype))
        finals.append(final)
    count = len(arrays)
    results = pl.pallas_call(
        functools.partial(gather_kernel, tuple(kinds), tuple(widths), tuple(streams)),
        out_shape=outs,
        in_specs=[pl.BlockSpec(memory_space=pltpu.VMEM)] * count,
        out_specs=[pl.BlockSpec(memory_space=pl.ANY)] * count,
        scratch_shapes=[
            pltpu.SemaphoreType.DMA((count,)),
            pltpu.SemaphoreType.DMA((count, 12)),
            pltpu.SemaphoreType.DMA((count, 12)),
        ],
        compiler_params=pltpu.CompilerParams(
            collective_id=0, has_side_effects=True, vmem_limit_bytes=32 * 1024 * 1024
        ),
        name="gather_weights",
    )(*ins)
    return [result.reshape(final) for result, final in zip(results, finals)]


def steps_up(k, marks):
    total = 0
    for mark in marks:
        total = total + jnp.where(k >= mark, 1, 0)
    return total


TEXT_MARKS = (3, 4, 7, 10)
IMAGE_MARKS = (3, 4, 5, 6, 9)


def reduce_kernel(
    text_left, text_right, text_extra, image_left, image_right, norms,
    text_out, image_out, norm_out,
    text_send, image_send,
    text_r0, text_r1, text_r2, text_r3, text_r4,
    image_r0, image_r1, image_r2, image_r3, image_r4,
    norm_buf,
    text_ss, text_rs, image_ss, image_rs, norm_ss, norm_rs,
):
    data, model, c, x, y = position()
    low, high = model % 2, (model // 2) % 2
    f32, bf16 = jnp.float32, jnp.bfloat16
    core = (flip(data, 1), model)
    along_x = (flip(data, 2), model)
    along_y = (flip(data, 4), model)
    near = (data, flip(model, 1))
    far = (data, flip(model, 2))
    greet(data, model)

    def stream(left, right, extra, out, outgoing, bufs, send_sem, recv_sem, marks, x_first):
        r0, r1, r2, r3, r4 = bufs
        total = right.shape[0]
        rows = left.shape[-2]

        def copy(k, stage):
            if stage == 0:
                pair = (outgoing.at[k % 2], r0.at[k], core)
            elif stage == 1:
                source = r0.at[k, :, 1 - x] if x_first else r0.at[k, 1 - y]
                pair = (source, r1.at[k], along_x if x_first else along_y)
            elif stage == 2:
                source = r1.at[k, 1 - y] if x_first else r1.at[k, 1 - x]
                pair = (source, r2.at[k], along_y if x_first else along_x)
            elif stage == 3:
                pair = (r2.at[k, :, 1 - low], r3.at[k], near)
            else:
                pair = (r3.at[k, 1 - high], r4.at[k], far)
            return pltpu.make_async_remote_copy(
                src_ref=pair[0], dst_ref=pair[1],
                send_sem=send_sem.at[k, stage], recv_sem=recv_sem.at[k, stage],
                device_id=pair[2], device_id_type=MESH_ID,
            )

        def products(k, half, put):
            lhs = left[half, steps_up(k, marks)].reshape(4 * rows, left.shape[-1])

            def plain():
                for z in range(4):
                    value = jnp.dot(lhs, right[k, z], preferred_element_type=f32)
                    put(z, value.reshape(2, 2, rows, 256))

            if extra is None:
                plain()
                return
            pl.when(k != total - 1)(plain)

            @pl.when(k == total - 1)
            def _():
                more = left[half, 5].reshape(4 * rows, left.shape[-1])
                for z in range(4):
                    value = jnp.dot(lhs, right[k, z], preferred_element_type=f32)
                    value += jnp.dot(more, extra[z], preferred_element_type=f32)
                    put(z, value.reshape(2, 2, rows, 256))

        def begin(k):
            @pl.when(k >= 2)
            def _():
                copy(k - 2, 0).wait_send()

            def put(z, value):
                outgoing[k % 2, :, :, z // 2, z % 2] = value.astype(bf16)

            products(k, 1 - c, put)
            copy(k, 0).start()

        def join(k):
            copy(k, 0).wait_recv()

            def put(z, value):
                held = r0[k, :, :, z // 2, z % 2].astype(f32)
                r0[k, :, :, z // 2, z % 2] = (held + value).astype(bf16)

            products(k, c, put)
            copy(k, 1).start()

        def add_into(target, k, kept):
            target[k] = (target[k].astype(f32) + kept.astype(f32)).astype(bf16)

        def second(k):
            copy(k, 1).wait_recv()
            add_into(r1, k, r0[k, :, x] if x_first else r0[k, y])
            copy(k, 2).start()

        def third(k):
            copy(k, 2).wait_recv()
            add_into(r2, k, r1[k, y] if x_first else r1[k, x])
            copy(k, 3).start()

        def fourth(k):
            copy(k, 3).wait_recv()
            add_into(r3, k, r2[k, :, low])
            copy(k, 4).start()

        def last(k):
            copy(k, 4).wait_recv()
            out[k] = r4[k].astype(f32) + r3[k, high].astype(f32)

        def finish():
            def body(k, carry):
                for stage in range(1, 5):
                    copy(k, stage).wait_send()
                return carry

            lax.fori_loop(0, total, body, 0)
            copy(total - 2, 0).wait_send()
            copy(total - 1, 0).wait_send()

        return total, (begin, join, second, third, fourth, last), finish

    text_total, text_stages, text_finish = stream(
        text_left, text_right, text_extra, text_out, text_send,
        (text_r0, text_r1, text_r2, text_r3, text_r4), text_ss, text_rs, TEXT_MARKS, True,
    )
    image_total, image_stages, image_finish = stream(
        image_left, image_right, None, image_out, image_send,
        (image_r0, image_r1, image_r2, image_r3, image_r4), image_ss, image_rs, IMAGE_MARKS, False,
    )
    lags = (0, 1, 3, 5, 6, 7)
    partners = (core, along_x, along_y, near, far)

    def norm_copy(stage):
        return pltpu.make_async_remote_copy(
            src_ref=norms if stage == 0 else norm_buf.at[stage - 1],
            dst_ref=norm_buf.at[stage],
            send_sem=norm_ss.at[stage], recv_sem=norm_rs.at[stage],
            device_id=partners[stage], device_id_type=MESH_ID,
        )

    def turn(t, carry):
        for lag, text_stage, image_stage in zip(lags, text_stages, image_stages):
            k = t - lag
            pl.when((k >= 0) & (k < text_total))(functools.partial(text_stage, k))
            pl.when((k >= 0) & (k < image_total))(functools.partial(image_stage, k))
        for stage in range(6):

            @pl.when(t == 2 * stage)
            def _(stage=stage):
                if stage > 0:
                    norm_copy(stage - 1).wait_recv()
                    held = norms[...] if stage == 1 else norm_buf[stage - 2]
                    if stage < 5:
                        norm_buf[stage - 1] += held
                    else:
                        norm_out[...] = norm_buf[stage - 1] + held
                if stage < 5:
                    norm_copy(stage).start()

        return carry

    lax.fori_loop(0, max(text_total, image_total) + lags[-1], turn, 0)
    text_finish()
    image_finish()
    for stage in range(5):
        norm_copy(stage).wait_send()


def reduce_all(text_left, text_right, text_extra, image_left, image_right, norms):
    bf16, f32 = jnp.bfloat16, jnp.float32

    def buffers(right, left):
        total, rows = right.shape[0], left.shape[-2]
        tail = (rows, 256)
        return [
            pltpu.VMEM((total, 2, 2, 2, 2) + tail, bf16),
            pltpu.VMEM((total, 2, 2, 2) + tail, bf16),
            pltpu.VMEM((total, 2, 2) + tail, bf16),
            pltpu.VMEM((total, 2) + tail, bf16),
            pltpu.VMEM((total,) + tail, bf16),
        ]

    def outgoing(left):
        return pltpu.VMEM((2, 2, 2, 2, 2, left.shape[-2], 256), bf16)

    texts, images = text_right.shape[0], image_right.shape[0]
    sems = []
    for total in (texts, images):
        sems += [pltpu.SemaphoreType.DMA((total, 5))] * 2
    sems += [pltpu.SemaphoreType.DMA((5,))] * 2
    return pl.pallas_call(
        reduce_kernel,
        out_shape=[
            jax.ShapeDtypeStruct((texts, text_left.shape[-2], 256), f32),
            jax.ShapeDtypeStruct((images, image_left.shape[-2], 256), f32),
            jax.ShapeDtypeStruct(norms.shape, f32),
        ],
        in_specs=[pl.BlockSpec(memory_space=pltpu.VMEM)] * 6,
        out_specs=[pl.BlockSpec(memory_space=pltpu.VMEM)] * 3,
        scratch_shapes=[outgoing(text_left), outgoing(image_left)]
        + buffers(text_right, text_left)
        + buffers(image_right, image_left)
        + [pltpu.VMEM((5,) + norms.shape, f32)]
        + sems,
        compiler_params=pltpu.CompilerParams(
            collective_id=1, has_side_effects=True, vmem_limit_bytes=67043328
        ),
        name="reduce_gradients",
    )(text_left, text_right, text_extra, image_left, image_right, norms)


def weight_kinds():
    return (
        ("col3", True), ("col3", False), ("row", True), ("row", False), ("col", True), ("row", True),
        ("col", False), ("row", False), ("split3", True), ("row", True), ("col3", False), ("row", False),
    )


def shards(
    text_tokens, image_regions, lengths, region_counts, text_cross, image_cross, text_cross_out,
    image_cross_out, text_up, text_down, image_up, image_down, text_self, text_self_out, image_self,
    image_self_out, text_gains, text_shifts, image_gains, image_shifts, text_cotangent, image_cotangent,
):
    mp, dp = lax.axis_size("mp"), lax.axis_size("dp")
    bf16, f32 = jnp.bfloat16, jnp.float32
    kinds = [kind for kind, unused in weight_kinds()]
    streams = [by_x for unused, by_x in weight_kinds()]
    (
        text_cross, image_cross, text_cross_out, image_cross_out, text_up, text_down, image_up,
        image_down, text_self, text_self_out, image_self, image_self_out,
    ) = gather_all(
        (
            text_cross, image_cross, text_cross_out, image_cross_out, text_up, text_down, image_up,
            image_down, text_self, text_self_out, image_self, image_self_out,
        ),
        kinds, streams, mp,
    )
    text_self = text_self.transpose(1, 2, 0, 3).reshape(3, text_self.shape[2], -1)
    slot_count = text_tokens.shape[1]
    region_total = image_regions.shape[1]
    text_mask = jnp.arange(slot_count, dtype=jnp.int32)[None, :] < lengths[:, None]
    image_mask = jnp.arange(region_total, dtype=jnp.int32)[None, :] < region_counts[:, None]
    text_input = text_tokens.astype(f32)
    image_input = image_regions.astype(f32)
    text_proj, image_proj, contexts, totals = cross_forward(
        text_tokens, image_regions, text_cross, image_cross, text_mask, image_mask
    )
    text_hidden_a = text_input + project(contexts[0], text_cross_out)
    image_hidden_a = image_input + project(contexts[1], image_cross_out)
    text_mid = layer_norm(text_hidden_a, text_gains[0], text_shifts[0])
    image_mid = layer_norm(image_hidden_a, image_gains[0], image_shifts[0])
    text_second, image_second = text_mid.astype(bf16), image_mid.astype(bf16)
    text_upper, text_middle, text_part = ffn_forward(text_second, text_up, text_down)
    image_upper, image_middle, image_part = ffn_forward(image_second, image_up, image_down)
    text_hidden_b = text_mid + text_part
    image_hidden_b = image_mid + image_part
    text_mixed = layer_norm(text_hidden_b, text_gains[1], text_shifts[1])
    image_mixed = layer_norm(image_hidden_b, image_gains[1], image_shifts[1])
    text_third, image_third = text_mixed.astype(bf16), image_mixed.astype(bf16)
    text_saved = self_forward(text_third, text_self, text_self_out, text_mask, TEXT_HEAD)
    image_saved = self_forward(image_third, image_self, image_self_out, image_mask, IMAGE_HEAD)
    text_hidden_c = text_mixed + text_saved[3]
    image_hidden_c = image_mixed + image_saved[3]
    text_result = layer_norm(text_hidden_c, text_gains[2], text_shifts[2])
    image_result = layer_norm(image_hidden_c, image_gains[2], image_shifts[2])
    text_grad_c, text_gain_c, text_shift_c = norm_back(
        text_hidden_c, text_gains[2], text_shifts[2], text_cotangent.astype(f32)
    )
    image_grad_c, image_gain_c, image_shift_c = norm_back(
        image_hidden_c, image_gains[2], image_shifts[2], image_cotangent.astype(f32)
    )
    text_coming_c, image_coming_c = text_grad_c.astype(bf16), image_grad_c.astype(bf16)
    text_self_grads, text_part = self_back(
        text_saved, text_self, text_self_out, text_mask, TEXT_HEAD, text_coming_c
    )
    image_self_grads, image_part = self_back(
        image_saved, image_self, image_self_out, image_mask, IMAGE_HEAD, image_coming_c
    )
    text_grad_b, text_gain_b, text_shift_b = norm_back(
        text_hidden_b, text_gains[1], text_shifts[1], text_grad_c + text_part
    )
    image_grad_b, image_gain_b, image_shift_b = norm_back(
        image_hidden_b, image_gains[1], image_shifts[1], image_grad_c + image_part
    )
    text_coming_b, image_coming_b = text_grad_b.astype(bf16), image_grad_b.astype(bf16)
    text_upper_grad, text_part = ffn_back(text_upper, text_up, text_down, text_coming_b)
    image_upper_grad, image_part = ffn_back(image_upper, image_up, image_down, image_coming_b)
    text_grad_a, text_gain_a, text_shift_a = norm_back(
        text_hidden_a, text_gains[0], text_shifts[0], text_grad_b + text_part
    )
    image_grad_a, image_gain_a, image_shift_a = norm_back(
        image_hidden_a, image_gains[0], image_shifts[0], image_grad_b + image_part
    )
    text_coming_a, image_coming_a = text_grad_a.astype(bf16), image_grad_a.astype(bf16)
    text_ctx_grad = project_back(text_coming_a, text_cross_out).astype(bf16)
    image_ctx_grad = project_back(image_coming_a, image_cross_out).astype(bf16)
    text_query_grad, image_key_grad, image_value_grad = attend_back(
        text_proj[0], image_proj[1], image_proj[2], image_mask, CROSS_HEAD, totals[0], text_ctx_grad
    )
    image_query_grad, text_key_grad, text_value_grad = attend_back(
        image_proj[0], text_proj[1], text_proj[2], text_mask, CROSS_HEAD, totals[1], image_ctx_grad
    )
    text_cross_grads = (text_query_grad, text_key_grad, text_value_grad)
    image_cross_grads = (image_query_grad, image_key_grad, image_value_grad)
    text_input_grad = text_grad_a + input_part(text_cross_grads, text_cross)
    image_input_grad = image_grad_a + input_part(image_cross_grads, image_cross)

    more = dp // 8

    def lefts(arrays, pad):
        tiles = []
        for array in arrays:
            flat = array.reshape(-1, array.shape[-1])
            flat = jnp.pad(flat, ((0, pad), (0, 0))).T
            rows = flat.shape[0] // dp
            parts = flat.reshape(more, 2, 2, 2, rows, flat.shape[1]).transpose(3, 1, 2, 0, 4, 5)
            tiles.append(parts.reshape(2, 2, 2, more * rows, flat.shape[1]))
        return jnp.stack(tiles, 1)

    def cut(arrays, pad):
        tiles = []
        for array in arrays:
            flat = jnp.pad(array.reshape(-1, array.shape[-1]), ((0, pad), (0, 0)))
            tiles.append(flat.reshape(flat.shape[0], mp, -1))
        joined = jnp.concatenate(tiles, -1)
        chunked = joined.reshape(joined.shape[0], mp, -1, 256)
        return chunked.transpose(2, 1, 0, 3)

    text_left = lefts(
        (text_tokens, text_coming_a, text_second, text_coming_b, text_third, text_coming_c), 0
    )
    text_context = text_saved[1]
    text_right = cut(
        text_cross_grads + (contexts[0], text_upper_grad, text_middle) + text_self_grads
        + (jnp.zeros_like(text_context),), 0
    )
    extra = text_context.reshape(-1, mp, text_context.shape[-1] // mp)
    text_extra = jnp.pad(extra, ((0, 0), (0, 0), (256 - extra.shape[-1], 0))).transpose(1, 0, 2)
    image_rows = image_regions.shape[0] * region_total
    pad = 128 * math.ceil(image_rows / 128) - image_rows
    image_left = lefts(
        (image_regions, image_coming_a, image_second, image_coming_b, image_third, image_coming_c), pad
    )
    image_right = cut(
        image_cross_grads + (contexts[1], image_upper_grad, image_middle) + image_self_grads
        + (image_saved[1],), pad
    )
    norms = jnp.concatenate(
        [
            text_gain_a, text_gain_b, text_gain_c, text_shift_a, text_shift_b, text_shift_c,
            image_gain_a, image_gain_b, image_gain_c, image_shift_a, image_shift_b, image_shift_c,
        ]
    ).reshape(-1, 128)
    text_sums, image_sums, norm_sums = reduce_all(
        text_left, text_right, text_extra, image_left, image_right, norms
    )
    if more > 1:
        norm_sums = lax.psum(norm_sums, "dp") / 8
        text_sums, image_sums = outer_sum(text_sums, more), outer_sum(image_sums, more)
    text_sums = text_sums.transpose(1, 0, 2).reshape(text_sums.shape[1], -1)
    image_sums = image_sums.transpose(1, 0, 2).reshape(image_sums.shape[1], -1)

    def columns(sums, widths):
        parts, start = [], 0
        for width in widths:
            parts.append(sums[:, start : start + width])
            start += width
        return parts

    def triple(parts):
        return jnp.stack(parts[:3])

    text_widths = [array.shape[-1] // mp for array in text_cross_grads + (contexts[0],)]
    text_widths += [text_upper_grad.shape[-1] // mp, text_middle.shape[-1] // mp]
    text_widths += [array.shape[-1] // mp for array in text_self_grads + (text_context,)]
    image_widths = [array.shape[-1] // mp for array in image_cross_grads + (contexts[1],)]
    image_widths += [image_upper_grad.shape[-1] // mp, image_middle.shape[-1] // mp]
    image_widths += [array.shape[-1] // mp for array in image_self_grads + (image_saved[1],)]
    text_parts = columns(text_sums, text_widths)
    image_parts = columns(image_sums, image_widths)
    flat_norms = norm_sums.reshape(-1)
    text_size, image_size = text_gains.size, image_gains.size
    text_end = 2 * text_size
    return (
        text_result,
        image_result,
        text_input_grad,
        image_input_grad,
        triple(text_parts[:3]),
        triple(image_parts[:3]),
        text_parts[3].T,
        image_parts[3].T,
        text_parts[4],
        text_parts[5].T,
        image_parts[4],
        image_parts[5].T,
        triple(text_parts[6:9]),
        text_parts[9].T,
        triple(image_parts[6:9]),
        image_parts[9].T,
        flat_norms[:text_size].reshape(text_gains.shape),
        flat_norms[text_size:text_end].reshape(text_shifts.shape),
        flat_norms[text_end : text_end + image_size].reshape(image_gains.shape),
        flat_norms[text_end + image_size :].reshape(image_shifts.shape),
    )


def outer_sum(sums, more):
    chunks, rows, width = sums.shape
    apart = sums.reshape(chunks, more, rows // more, width)
    low = lax.axis_index("dp") % 8
    spread = jnp.zeros((chunks, more, 8, rows // more, width), sums.dtype)
    spread = lax.dynamic_update_slice(spread, apart[:, :, None], (0, 0, low, 0, 0))
    spread = spread.reshape(chunks, more * 8 * (rows // more), width)
    return lax.psum_scatter(spread, "dp", scatter_dimension=1, tiled=True)


def solution(mesh):
    in_specs = (
        P(("dp", "mp"), None, None),
        P(("dp", "mp"), None, None),
        P(("dp", "mp")),
        P(("dp", "mp")),
        P(None, None, "mp"),
        P(None, None, "mp"),
        P("mp", None),
        P("mp", None),
        P(None, "mp"),
        P("mp", None),
        P(None, "mp"),
        P("mp", None),
        P(None, None, "mp"),
        P("mp", None),
        P(None, None, "mp"),
        P("mp", None),
        P(),
        P(),
        P(),
        P(),
        P(("dp", "mp"), None, None),
        P(("dp", "mp"), None, None),
    )
    out_specs = (
        P(("dp", "mp"), None, None),
        P(("dp", "mp"), None, None),
        P(("dp", "mp"), None, None),
        P(("dp", "mp"), None, None),
        P(None, "dp", "mp"),
        P(None, "dp", "mp"),
        P("mp", "dp"),
        P("mp", "dp"),
        P("dp", "mp"),
        P("mp", "dp"),
        P("dp", "mp"),
        P("mp", "dp"),
        P(None, "dp", "mp"),
        P("mp", "dp"),
        P(None, "dp", "mp"),
        P("mp", "dp"),
        P(),
        P(),
        P(),
        P(),
    )
    return jax.shard_map(shards, mesh=mesh, in_specs=in_specs, out_specs=out_specs, check_vma=False)
```

time: 1210 us -> 832 us (0.69)
  waiting for transfers between devices: 782 us -> 0 us
  Pallas kernels: 0 us -> 410 us
  local copies, waits for them, and re-layouts: 58.4 us -> 269 us
  blocking collectives: 189 us -> 0 us
  other arithmetic: 53.1 us -> 31.2 us
  matrix products: 93 us -> 109 us
  between operations: 17.6 us -> 3.05 us
    reduce_scatter x21 -> x0, waiting for transfers between devices: 611 us -> none  [the longest x3 72.8 us: sum_branch(): lax.psum_scatter(text_part.astype(jnp.bfloat16), 'mp', scatter_dimension=...]
    pallas_call x0 -> x2, Pallas kernels: none -> 410 us  [the longest x1 205 us: gather_all(): pl.pallas_call(functools.partial(gather_kernel, tuple(kinds), tuple(width...]
    all_gather x7 -> x0, blocking collectives: 148 us -> none  [the longest x3 65.9 us: gather_grads(): lax.all_gather(image_grad, 'mp', axis=0, tiled=True)]
    all_gather x6 -> x0, waiting for transfers between devices: 104 us -> none  [the longest x2 48.9 us: gather_layer(): lax.all_gather(text_low, 'mp', axis=0, tiled=True)]
    unnamed x33 -> x0, waiting for transfers between devices: 66.9 us -> none
    reshape x0 -> x25, local copies, waits for them, and re-layouts: none -> 50.2 us  [the longest x4 16.6 us: cut(): tiles.append(flat.reshape(flat.shape[0], mp, -1))]
    psum x1 -> x0, blocking collectives: 41 us -> none  [shards(): lax.psum((jnp.stack([text_gain_a, text_gain_b, text_gain_c]), jnp.stack([...]
    unnamed x422 -> x435, local copies, waits for them, and re-layouts: 56 us -> 89.7 us
  transfers between devices with their start and end apart: 30 -> 0, of which waited for: 27 -> 0; matrix products, arithmetic and copies ran while one was open for 12% -> 0% of each run, Pallas kernels for 0% -> 0%
where the time goes in v1:
time: 832 us; the launch traced here: 823 us
  Pallas kernels  410 us (49%)
  local copies, waits for them, and re-layouts  269 us (32%)
  matrix products  109 us (13%)
  other arithmetic  31.2 us (4%)
    pallas_call x1, Pallas kernels, gather_all(): pl.pallas_call(functools.partial(gather_kernel, tuple(kinds), tuple(width...  205 us
    pallas_call x1, Pallas kernels, reduce_all(): pl.pallas_call(reduce_kernel, out_shape=[jax.ShapeDtypeStruct((texts, tex...  204 us
    unnamed x435, local copies, waits for them, and re-layouts  89.7 us
    dot_general x20, matrix products, project(): return jnp.dot(inputs, weight, preferred_element_type=jnp.float32)  47.3 us
    dot_general x20, matrix products, project_back(): lax.dot_general(gradient, weight, (((gradient.ndim - 1,), (1,)), ((), ())...  43 us
    slice x3, local copies, waits for them, and re-layouts, project_three(): weights[number]  17.3 us
    concatenate x12, local copies, waits for them, and re-layouts, cut(): joined = jnp.concatenate(tiles, -1)  17.2 us

profile of v1, /device:TPU:0, one launch (start us, length us, event | category | flops | bytes accessed | tf_op | source)
XLA Modules:
  0.0 822.6 jit_solution(4508281505443375848)
XLA Ops:
  26.0 205.4 %gather_weights.1 = (bf16[3,2,2,2,96,1024]{5,4,3,2,1,0:T(8,128)(2,1)}, bf16[3,2,2,2,128,1024]{5,4,3,2,1,0:T(8,128)(2,1)}, bf16[4,2,2,2,32,768]{5,4,3,2,1,0:T(8,1...) custom-call(bf16[3,2,2,2,96,256]{5,4,3,2,1,0:T(8,128)(2,1)S(1)} %bit, ...), custom_call_target="tpu_custom_call" | custom-call | tf_op jit(solution)/shard_map/gather_weights/pallas_call | solution.py:295
  235.4 9.4 %fusion.106 = (bf16[1,2,2,2,128,1024]{5,4,3,2,1,0:T(8,128)(2,1)}, bf16[1,2,2,2,128,1024]{5,4,3,2,1,0:T(8,128)(2,1)}, bf16[1,2,2,2,128,1024]{5,4,3,2,1,0:T(8,128)...) fusion(bf16[3,2,2,2,128,1024]{5,4,3,2,1,0:T(8,128)(2,1)} %get-t, ...), kind=kLoop, calls=%fused_computation.350 | loop fusion | bytes 25165824 | tf_op jit(solution)/shard_map/slice | solution.py:107
  249.0 2.7 fusion.30
  253.4 2.7 fusion.31
  257.1 6.6 copy.120
  263.7 3.8 fusion.109
  267.5 4.1 fusion.108
  286.5 1.8 copy.225
  288.3 2.1 fusion.83
  296.0 1.8 copy.256
  297.8 2.2 fusion.121
  303.9 1.8 copy.229
  305.7 2.8 convolution_convert_fusion.18
  310.1 2.8 convolution_convert_fusion.19
  314.5 2.8 convolution_convert_fusion.20
  321.4 1.8 copy.365
  324.9 1.8 copy.260
  328.4 2.4 fusion.123
  337.3 1.9 copy.263
  342.4 1.8 copy.231
  354.1 1.8 copy.257
  361.0 1.8 copy.258
  367.8 1.8 copy.259
  373.0 2.6 fusion.126
  378.8 3.5 multiply_reduce_fusion.8
  384.4 2.2 multiply_reduce_fusion.9
  388.9 2.0 fusion.101
  406.0 1.8 bitcast_dynamic-update-slice_fusion.10
  417.9 1.8 copy.251
  421.3 2.5 fusion.127
  426.3 2.2 reshape.824
  429.8 2.2 reshape.825
  437.0 2.2 reshape.826
  439.2 1.9 fusion.115
  443.9 4.6 fusion.39
  448.6 8.0 multiply_convert_fusion
  456.6 5.2 fusion.116
  461.8 4.3 reshape.757
  466.2 4.2 copy.216
  474.0 2.5 convolution_convert_fusion.9
  476.5 1.9 copy.126
  478.4 2.5 convolution_convert_fusion.10
  481.0 2.5 convolution_convert_fusion.11
  483.5 1.9 copy.122
  491.1 2.0 convert_element_type.494
  493.1 2.0 copy.219
  495.2 2.1 pad_bitcast_fusion.text_extra
  497.3 1.9 fusion.118
  504.1 2.1 copy.202
  506.1 2.2 convolution_convert_fusion.6
  510.3 2.0 convert_element_type.493
  519.2 2.0 convert_element_type.491
  521.2 2.2 convolution_add_fusion.3
  523.5 2.3 multiply_reduce_fusion.1
  528.4 6.2 add_convert_fusion
  535.8 5.5 multiply_reduce_fusion.2
  541.2 4.3 reshape.756
  545.6 3.8 copy.215
  554.4 1.8 bitcast_dynamic-update-slice_fusion.4
  568.8 1.9 constant_dynamic-update-slice_fusion.10
  573.1 3.1 convolution_add_fusion.9
  578.0 1.9 fusion.14
  595.0 10.2 %copy.217 = bf16[256,4,13,256]{3,0,1,2:T(8,128)(2,1)} copy(bf16[256,4,13,256]{0,3,2,1:T(8,128)(2,1)} %bitcast.150) | data formatting | bytes 13631488 | tf_op jit(solution)/shard_map/reshape | solution.py:647
  605.2 204.3 %reduce_gradients.1 = (f32[13,96,256]{2,1,0:T(8,128)}, f32[10,128,256]{2,1,0:T(8,128)}, f32[84,128]{1,0:T(8,128)}) custom-call(bf16[2,6,2,2,96,256]{5,4,3,2,1,0:T(8,128)(2,1)} %bitcast_dynamic-update-slice_fusion.text_left, bf16[13,4,256,256]{3,2,1,0:T(8,128)(2,1)} %bitcast.496, bf16[4,256,256]{2,1,0:T(8,128)(2,1)} %pad_bitcast_fusion.text_extra, ...), custom_call_target="tpu_custom_call" | custom-call | tf_op jit(solution)/shard_map/reduce_gradients/pallas_call | solution.py:512
  (623 shorter events, 225.3 us)
Async XLA Ops:
  0.7 8.3 %copy-start.113 = (bf16[3,768,192]{1,2,0:T(8,128)(2,1)S(1)}, bf16[3,768,192]{1,2,0:T(8,128)(2,1)}, u32[]{:S(2)}) copy-start(bf16[3,768,192]{1,2,0:T(8,128)(2,1)} %param.34) | copy-start | bytes 2654212
  1.5 271.9 %copy-start.181 = (pred[2,128]{1,0:T(4,128)(4,1)}, pred[2,128]{1,0:T(4,128)(4,1)S(1)}, u32[]{:S(2)}) copy-start(pred[2,128]{1,0:T(4,128)(4,1)S(1)} %iota_compare_fusion) | copy-start | bytes 772
  5.1 278.4 %copy-start.131 = (f32[1,1024]{1,0:T(1,128)}, f32[1,1024]{1,0:T(1,128)S(1)}, u32[]{:S(2)}) copy-start(f32[1,1024]{1,0:T(1,128)S(1)} %get-tuple-element.176) | copy-start | bytes 12292
  6.6 465.1 %copy-start.121 = (f32[768]{0:T(1024)}, f32[768]{0:T(1024)S(1)}, u32[]{:S(2)}) copy-start(f32[768]{0:T(1024)S(1)} %get-tuple-element.219) | copy-start | bytes 9220
  235.4 9.4 %copy-start.4 = (bf16[4,2,2,2,32,768]{5,4,3,2,1,0:T(8,128)(2,1)}, bf16[4,2,2,2,32,768]{5,4,3,2,1,0:T(8,128)(2,1)S(1)}, u32[]{:S(2)}) copy-start(bf16[4,2,2,2,32,768]{5,4,3,2,1,0:T(8,128)(2,1)S(1)} %get-tuple-element.37) | copy-start | bytes 4718596
  235.4 10.8 %copy-start.114 = (bf16[2,36,1024]{2,0,1:T(2,128)(2,1)S(1)}, bf16[2,36,1024]{2,0,1:T(2,128)(2,1)}, u32[]{:S(2)}) copy-start(bf16[2,36,1024]{2,0,1:T(2,128)(2,1)} %param.23) | copy-start | bytes 442372
  257.1 16.2 %copy-start.90 = (bf16[2,36,8,128]{3,2,1,0:T(8,128)(2,1)}, bf16[2,36,8,128]{3,2,1,0:T(8,128)(2,1)S(1)}, u32[]{:S(2)}) copy-start(bf16[2,36,8,128]{3,2,1,0:T(8,128)(2,1)S(1)} %reshape.809) | copy-start | bytes 442372
  283.5 4.8 copy-start.169
  317.3 11.1 %copy-start.136 = (f32[2,36]{1,0:T(2,128)S(1)}, f32[2,36]{1,0:T(2,128)}, u32[]{:S(2)}) copy-start(f32[2,36]{1,0:T(2,128)} %copy-done.135) | copy-start | bytes 868
  317.3 11.1 %copy-start.142 = (f32[2,36]{1,0:T(2,128)S(1)}, f32[2,36]{1,0:T(2,128)}, u32[]{:S(2)}) copy-start(f32[2,36]{1,0:T(2,128)} %copy-done.141) | copy-start | bytes 868
  321.4 9.4 %copy-start.72 = (bf16[2,36,1024]{2,0,1:T(2,128)(2,1)S(1)}, bf16[2,36,1024]{2,0,1:T(2,128)(2,1)}, u32[]{:S(2)}) copy-start(bf16[2,36,1024]{2,0,1:T(2,128)(2,1)} %param.43) | copy-start | bytes 442372
  328.4 5.8 copy-start.3
  373.0 5.8 copy-start.161
  373.0 5.8 copy-start.163
  390.9 7.9 copy-start.164
  398.8 5.1 copy-start.34
  401.4 6.5 copy-start.111
  406.0 7.7 copy-start.101
  406.0 15.3 %copy-start.41 = (bf16[1,2,2,2,128,1024]{5,4,3,2,1,0:T(8,128)(2,1)S(1)}, bf16[1,2,2,2,128,1024]{5,4,3,2,1,0:T(8,128)(2,1)}, u32[]{:S(2)}) copy-start(bf16[1,2,2,2,128,1024]{5,4,3,2,1,0:T(8,128)(2,1)} %get-tuple-element.218) | copy-start | bytes 6291460
  413.7 10.1 %copy-start.91 = (bf16[2,36,8,128]{3,2,1,0:T(8,128)(2,1)S(1)}, bf16[2,36,8,128]{3,2,1,0:T(8,128)(2,1)}, u32[]{:S(2)}) copy-start(bf16[2,36,8,128]{3,2,1,0:T(8,128)(2,1)} %copy-done.90) | copy-start | bytes 442372
  423.8 8.2 copy-start.48
  428.5 5.2 copy-start.88
  428.5 5.2 copy-start.184
  433.7 5.6 copy-start.5
  434.0 7.1 copy-start.35
  434.5 6.6 copy-start.119
  437.0 5.0 copy-start.132
  437.0 5.0 copy-start.159
  441.1 15.4 %copy-start.144 = (f32[2,128]{1,0:T(2,128)}, f32[2,128]{1,0:T(2,128)S(1)}, u32[]{:S(2)}) copy-start(f32[2,128]{1,0:T(2,128)S(1)} %broadcast_multiply_fusion.5) | copy-start | bytes 3076
  441.4 7.1 copy-start.171
  442.0 14.6 %copy-start.166 = (f32[2,128]{1,0:T(2,128)}, f32[2,128]{1,0:T(2,128)S(1)}, u32[]{:S(2)}) copy-start(f32[2,128]{1,0:T(2,128)S(1)} %fusion.90) | copy-start | bytes 3076
  448.5 8.0 copy-start.70
  448.5 8.0 copy-start.27
  456.6 5.3 copy-start.54
  461.8 35.4 %copy-start.129 = (f32[2,128]{1,0:T(2,128)}, f32[2,128]{1,0:T(2,128)S(1)}, u32[]{:S(2)}) copy-start(f32[2,128]{1,0:T(2,128)S(1)} %broadcast_multiply_fusion.4) | copy-start | bytes 3076
  466.2 5.6 copy-start.134
  471.7 6.8 copy-start.175
  471.7 25.6 %copy-start.137 = (f32[2,128]{1,0:T(2,128)}, f32[2,128]{1,0:T(2,128)S(1)}, u32[]{:S(2)}) copy-start(f32[2,128]{1,0:T(2,128)S(1)} %fusion.91) | copy-start | bytes 3076
  478.4 8.2 copy-start.182
  490.0 7.3 copy-start.122
  493.1 6.0 copy-start.52
  493.1 6.0 copy-start.124
  504.1 8.2 copy-start.21
  504.1 8.2 copy-start.69
  518.0 5.5 copy-start.22
  518.0 5.5 copy-start.24
  518.0 5.5 copy-start.53
  518.0 5.5 copy-start.123
  518.0 5.5 copy-start.125
  518.0 5.5 copy-start.130
  518.0 5.5 copy-start.138
  528.3 7.5 copy-start.28
  528.3 7.5 copy-start.133
  528.3 7.4 copy-start.145
  528.3 7.4 copy-start.167
  528.3 7.4 copy-start.180
  553.5 5.3 copy-start.85
  553.5 7.9 copy-start.36
  553.5 7.9 copy-start.120
  554.4 7.2 copy-start.93
  563.2 4.8 copy-start.109
  568.8 9.2 %copy-start.40 = (bf16[1,2,2,2,128,1024]{5,4,3,2,1,0:T(8,128)(2,1)S(1)}, bf16[1,2,2,2,128,1024]{5,4,3,2,1,0:T(8,128)(2,1)}, u32[]{:S(2)}) copy-start(bf16[1,2,2,2,128,1024]{5,4,3,2,1,0:T(8,128)(2,1)} %copy-done.39) | copy-start | bytes 6291460
  568.8 9.2 %copy-start.71 = (f32[2,36,1024]{2,1,0:T(8,128)S(1)}, f32[2,36,1024]{2,1,0:T(8,128)}, u32[]{:S(2)}) copy-start(f32[2,36,1024]{2,1,0:T(8,128)} %get-tuple-element.123) | copy-start | bytes 884740
  568.8 9.2 %copy-start.165 = (f32[2,36]{1,0:T(2,128)S(1)}, f32[2,36]{1,0:T(2,128)}, u32[]{:S(2)}) copy-start(f32[2,36]{1,0:T(2,128)} %copy-done.164) | copy-start | bytes 868
  (121 other events, 283.3 us)

commit v2 on v1

v2 whole, which is shorter than its diff:
```python
import functools
import math

import jax
import jax.numpy as jnp
from jax import lax
from jax.experimental import pallas as pl
from jax.experimental.pallas import tpu as pltpu
from jax.sharding import PartitionSpec as P

TEXT_HEAD = 64
CROSS_HEAD = 128
IMAGE_HEAD = 128


EPSILON = 1e-05
MASKED = -1e30
MESH_ID = pl.DeviceIdType.MESH


def flip(index, step):
    return index + step * (1 - 2 * ((index // step) % 2))


def position(unit):
    data, model = lax.axis_index("dp"), lax.axis_index("mp")
    return data, model, (data // unit) % 2, (data // (2 * unit)) % 2, (data // (4 * unit)) % 2


def greet(data, model, unit):
    barrier = pltpu.get_barrier_semaphore()
    partners = [(flip(data, step * unit), model) for step in (1, 2, 4)]
    partners += [(data, flip(model, step)) for step in (1, 2)]
    for partner in partners:
        pl.semaphore_signal(barrier, inc=1, device_id=partner, device_id_type=MESH_ID)
    pl.semaphore_wait(barrier, len(partners))


def view_of(ref, kind, shard, width, y, x, c):
    if kind == "col3":
        columns = pl.ds(pl.multiple_of(shard * width, 128), width)
        return ref.at[:, y, x, c, :, columns]
    if kind == "col":
        columns = pl.ds(pl.multiple_of(shard * width, 128), width)
        return ref.at[y, x, c, :, columns]
    if kind == "row":
        return ref.at[shard, y, x, c]
    return ref.at[shard, :, y, x, c]


def local_of(ref, kind, y, x, c):
    if kind in ("col3", "split3"):
        return ref.at[:, y, x, c]
    return ref.at[y, x, c]


def gather_kernel(unit, kinds, widths, streams, *refs):
    count = len(kinds)
    ins, outs = refs[:count], refs[count : 2 * count]
    own_sem, send_sem, recv_sem = refs[2 * count :]
    data, model, c, x, y = position(unit)
    every = slice(None)
    near, far = flip(model, 1), flip(model, 2)
    corner = flip(near, 2)
    owns = []
    for k in range(count):
        own = pltpu.make_async_copy(
            ins[k], view_of(outs[k], kinds[k], model, widths[k], every, every, every), own_sem.at[k]
        )
        own.start()
        owns.append(own)
    greet(data, model, unit)

    def send(k, slot, source, target, partner):
        copy = pltpu.make_async_remote_copy(
            src_ref=source,
            dst_ref=target,
            send_sem=send_sem.at[k, slot],
            recv_sem=recv_sem.at[k, slot],
            device_id=partner,
            device_id_type=MESH_ID,
        )
        copy.start()
        return copy

    def piece(k, shard, y, x, c):
        return view_of(outs[k], kinds[k], shard, widths[k], y, x, c)

    copies = {}
    for k in range(count):
        mine = local_of(ins[k], kinds[k], y, x, c)
        copies[k, 0] = send(k, 0, mine, piece(k, model, y, x, c), (data, far))

    def pair_up(k):
        mine = local_of(ins[k], kinds[k], y, x, c)
        copies[k, 1] = send(k, 1, mine, piece(k, model, y, x, c), (data, near))
        copies[k, 0].wait_recv()
        block = piece(k, far, y, x, c)
        copies[k, 2] = send(k, 2, block, block, (data, near))

    def spread(k, stage):
        first_x = streams[k] == (stage == 0)
        if stage == 2:
            where, partner = (every, every, c), (flip(data, unit), model)
        elif stage == 0:
            where = (y, x, c)
            partner = (flip(data, (2 if first_x else 4) * unit), model)
        else:
            where = (y, every, c) if streams[k] else (every, x, c)
            partner = (flip(data, (2 if first_x else 4) * unit), model)
        base = 3 + 3 * stage
        for number, shard in enumerate((far, near, corner)):
            if stage == 0:
                if number > 0:
                    copies[k, number].wait_recv()
            else:
                copies[k, base - 3 + number].wait_recv()
            block = piece(k, shard, *where)
            copies[k, base + number] = send(k, base + number, block, block, partner)

    for step in range(count + 3):
        if step < count:
            pair_up(step)
        for stage in range(3):
            k = step - 1 - stage
            if 0 <= k < count:
                spread(k, stage)
    for k in range(count):
        for number in range(3):
            copies[k, 9 + number].wait_recv()
        owns[k].wait()
        for slot in range(12):
            copies[k, slot].wait_send()


def gather_all(arrays, kinds, streams, mp, unit):
    ins, outs, widths, finals = [], [], [], []
    for array, kind in zip(arrays, kinds):
        widths.append(array.shape[-1])
        rows, width = array.shape[-2] // 8, array.shape[-1]
        if kind in ("col3", "split3"):
            ins.append(array.reshape(array.shape[0], 2, 2, 2, rows, width))
        else:
            ins.append(array.reshape(2, 2, 2, rows, width))
        if kind == "col3":
            shape, final = (array.shape[0], 2, 2, 2, rows, mp * width), (array.shape[0], 8 * rows, mp * width)
        elif kind == "col":
            shape, final = (2, 2, 2, rows, mp * width), (8 * rows, mp * width)
        elif kind == "row":
            shape, final = (mp, 2, 2, 2, rows, width), (mp * 8 * rows, width)
        else:
            shape = (mp, array.shape[0], 2, 2, 2, rows, width)
            final = (mp, array.shape[0], 8 * rows, width)
        outs.append(jax.ShapeDtypeStruct(shape, array.dtype))
        finals.append(final)
    count = len(arrays)
    results = pl.pallas_call(
        functools.partial(gather_kernel, unit, tuple(kinds), tuple(widths), tuple(streams)),
        out_shape=outs,
        in_specs=[pl.BlockSpec(memory_space=pltpu.VMEM)] * count,
        out_specs=[pl.BlockSpec(memory_space=pl.ANY)] * count,
        scratch_shapes=[
            pltpu.SemaphoreType.DMA((count,)),
            pltpu.SemaphoreType.DMA((count, 12)),
            pltpu.SemaphoreType.DMA((count, 12)),
        ],
        compiler_params=pltpu.CompilerParams(
            collective_id=0, has_side_effects=True, vmem_limit_bytes=32 * 1024 * 1024
        ),
        name="gather_weights",
    )(*ins)
    return [result.reshape(final) for result, final in zip(results, finals)]


def steps_up(k, marks):
    total = 0
    for mark in marks:
        total = total + jnp.where(k >= mark, 1, 0)
    return total


TEXT_MARKS = (3, 4, 7, 10)
IMAGE_MARKS = (3, 4, 5, 6, 9)


def reduce_kernel(
    unit,
    text_left, text_right, text_extra, image_left, image_right, norms,
    text_out, image_out, norm_out,
    text_send, image_send,
    text_r0, text_r1, text_r2, text_r3, text_r4,
    image_r0, image_r1, image_r2, image_r3, image_r4,
    norm_buf,
    text_ss, text_rs, image_ss, image_rs, norm_ss, norm_rs,
):
    data, model, c, x, y = position(unit)
    low, high = model % 2, (model // 2) % 2
    f32, bf16 = jnp.float32, jnp.bfloat16
    core = (flip(data, unit), model)
    along_x = (flip(data, 2 * unit), model)
    along_y = (flip(data, 4 * unit), model)
    near = (data, flip(model, 1))
    far = (data, flip(model, 2))
    greet(data, model, unit)

    def stream(left, right, extra, out, outgoing, bufs, send_sem, recv_sem, marks, x_first):
        r0, r1, r2, r3, r4 = bufs
        total = right.shape[0]
        rows = left.shape[-2]

        def copy(k, stage):
            if stage == 0:
                pair = (outgoing.at[k % 2], r0.at[k], core)
            elif stage == 1:
                source = r0.at[k, :, 1 - x] if x_first else r0.at[k, 1 - y]
                pair = (source, r1.at[k], along_x if x_first else along_y)
            elif stage == 2:
                source = r1.at[k, 1 - y] if x_first else r1.at[k, 1 - x]
                pair = (source, r2.at[k], along_y if x_first else along_x)
            elif stage == 3:
                pair = (r2.at[k, :, 1 - low], r3.at[k], near)
            else:
                pair = (r3.at[k, 1 - high], r4.at[k], far)
            return pltpu.make_async_remote_copy(
                src_ref=pair[0], dst_ref=pair[1],
                send_sem=send_sem.at[k, stage], recv_sem=recv_sem.at[k, stage],
                device_id=pair[2], device_id_type=MESH_ID,
            )

        def products(k, half, put):
            lhs = left[half, steps_up(k, marks)].reshape(4 * rows, left.shape[-1])

            def plain():
                for z in range(4):
                    value = jnp.dot(lhs, right[k, z], preferred_element_type=f32)
                    put(z, value.reshape(2, 2, rows, 256))

            if extra is None:
                plain()
                return
            pl.when(k != total - 1)(plain)

            @pl.when(k == total - 1)
            def _():
                more = left[half, 5].reshape(4 * rows, left.shape[-1])
                for z in range(4):
                    value = jnp.dot(lhs, right[k, z], preferred_element_type=f32)
                    value += jnp.dot(more, extra[z], preferred_element_type=f32)
                    put(z, value.reshape(2, 2, rows, 256))

        def begin(k):
            @pl.when(k >= 2)
            def _():
                copy(k - 2, 0).wait_send()

            def put(z, value):
                outgoing[k % 2, :, :, z // 2, z % 2] = value.astype(bf16)

            products(k, 1 - c, put)
            copy(k, 0).start()

        def join(k):
            copy(k, 0).wait_recv()

            def put(z, value):
                held = r0[k, :, :, z // 2, z % 2].astype(f32)
                r0[k, :, :, z // 2, z % 2] = (held + value).astype(bf16)

            products(k, c, put)
            copy(k, 1).start()

        def add_into(target, k, kept):
            target[k] = (target[k].astype(f32) + kept.astype(f32)).astype(bf16)

        def second(k):
            copy(k, 1).wait_recv()
            add_into(r1, k, r0[k, :, x] if x_first else r0[k, y])
            copy(k, 2).start()

        def third(k):
            copy(k, 2).wait_recv()
            add_into(r2, k, r1[k, y] if x_first else r1[k, x])
            copy(k, 3).start()

        def fourth(k):
            copy(k, 3).wait_recv()
            add_into(r3, k, r2[k, :, low])
            copy(k, 4).start()

        def last(k):
            copy(k, 4).wait_recv()
            out[k] = r4[k].astype(f32) + r3[k, high].astype(f32)

        def finish():
            def body(k, carry):
                for stage in range(1, 5):
                    copy(k, stage).wait_send()
                return carry

            lax.fori_loop(0, total, body, 0)
            copy(total - 2, 0).wait_send()
            copy(total - 1, 0).wait_send()

        return total, (begin, join, second, third, fourth, last), finish

    text_total, text_stages, text_finish = stream(
        text_left, text_right, text_extra, text_out, text_send,
        (text_r0, text_r1, text_r2, text_r3, text_r4), text_ss, text_rs, TEXT_MARKS, True,
    )
    image_total, image_stages, image_finish = stream(
        image_left, image_right, None, image_out, image_send,
        (image_r0, image_r1, image_r2, image_r3, image_r4), image_ss, image_rs, IMAGE_MARKS, False,
    )
    lags = (0, 1, 3, 5, 6, 7)
    partners = (core, along_x, along_y, near, far)

    def norm_copy(stage):
        return pltpu.make_async_remote_copy(
            src_ref=norms if stage == 0 else norm_buf.at[stage - 1],
            dst_ref=norm_buf.at[stage],
            send_sem=norm_ss.at[stage], recv_sem=norm_rs.at[stage],
            device_id=partners[stage], device_id_type=MESH_ID,
        )

    def turn(t, carry):
        for lag, text_stage, image_stage in zip(lags, text_stages, image_stages):
            k = t - lag
            pl.when((k >= 0) & (k < text_total))(functools.partial(text_stage, k))
            pl.when((k >= 0) & (k < image_total))(functools.partial(image_stage, k))
        for stage in range(6):

            @pl.when(t == 2 * stage)
            def _(stage=stage):
                if stage > 0:
                    norm_copy(stage - 1).wait_recv()
                    held = norms[...] if stage == 1 else norm_buf[stage - 2]
                    if stage < 5:
                        norm_buf[stage - 1] += held
                    else:
                        norm_out[...] = norm_buf[stage - 1] + held
                if stage < 5:
                    norm_copy(stage).start()

        return carry

    lax.fori_loop(0, max(text_total, image_total) + lags[-1], turn, 0)
    text_finish()
    image_finish()
    for stage in range(5):
        norm_copy(stage).wait_send()


def reduce_all(text_left, text_right, text_extra, image_left, image_right, norms, unit):
    bf16, f32 = jnp.bfloat16, jnp.float32

    def buffers(right, left):
        total, rows = right.shape[0], left.shape[-2]
        tail = (rows, 256)
        return [
            pltpu.VMEM((total, 2, 2, 2, 2) + tail, bf16),
            pltpu.VMEM((total, 2, 2, 2) + tail, bf16),
            pltpu.VMEM((total, 2, 2) + tail, bf16),
            pltpu.VMEM((total, 2) + tail, bf16),
            pltpu.VMEM((total,) + tail, bf16),
        ]

    def outgoing(left):
        return pltpu.VMEM((2, 2, 2, 2, 2, left.shape[-2], 256), bf16)

    texts, images = text_right.shape[0], image_right.shape[0]
    sems = []
    for total in (texts, images):
        sems += [pltpu.SemaphoreType.DMA((total, 5))] * 2
    sems += [pltpu.SemaphoreType.DMA((5,))] * 2
    return pl.pallas_call(
        functools.partial(reduce_kernel, unit),
        out_shape=[
            jax.ShapeDtypeStruct((texts, text_left.shape[-2], 256), f32),
            jax.ShapeDtypeStruct((images, image_left.shape[-2], 256), f32),
            jax.ShapeDtypeStruct(norms.shape, f32),
        ],
        in_specs=[pl.BlockSpec(memory_space=pltpu.VMEM)] * 6,
        out_specs=[pl.BlockSpec(memory_space=pltpu.VMEM)] * 3,
        scratch_shapes=[outgoing(text_left), outgoing(image_left)]
        + buffers(text_right, text_left)
        + buffers(image_right, image_left)
        + [pltpu.VMEM((5,) + norms.shape, f32)]
        + sems,
        compiler_params=pltpu.CompilerParams(
            collective_id=1, has_side_effects=True, vmem_limit_bytes=67043328
        ),
        name="reduce_gradients",
    )(text_left, text_right, text_extra, image_left, image_right, norms)


ROOT_HALF = math.sqrt(0.5)
DENSITY = 1.0 / math.sqrt(2.0 * math.pi)
TILE = 256
BLOCK = 32


def dot_nn(a, b):
    return jnp.dot(a, b, preferred_element_type=jnp.float32)


def dot_nt(a, b):
    return lax.dot_general(a, b, (((1,), (1,)), ((), ())), preferred_element_type=jnp.float32)


def dot_tn(a, b):
    return lax.dot_general(a, b, (((0,), (0,)), ((), ())), preferred_element_type=jnp.float32)


def row_blocks(rows, body):
    def step(i, carry):
        body(pl.ds(pl.multiple_of(i * BLOCK, BLOCK), BLOCK))
        return carry

    lax.fori_loop(0, rows // BLOCK, step, 0)


def tile_at(j):
    return pl.ds(pl.multiple_of(j * TILE, TILE), TILE)


def probabilities(query, keys, mask, head_size):
    scores = dot_nt(query, keys) * (1.0 / math.sqrt(head_size))
    scores = jnp.where(mask > 0.5, scores, MASKED)
    lifted = jnp.exp(scores - jnp.max(scores, -1, keepdims=True))
    return lifted / jnp.sum(lifted, -1, keepdims=True)


def head_forward(query, keys, values, mask, head_size):
    probs = probabilities(query, keys, mask, head_size)
    return dot_nn(probs.astype(jnp.bfloat16), values).astype(jnp.bfloat16)


def head_back(query, keys, values, mask, head_size, context_grad):
    bf16 = jnp.bfloat16
    probs = probabilities(query, keys, mask, head_size)
    value_grad = dot_tn(probs.astype(bf16), context_grad)
    prob_grad = dot_nt(context_grad, values)
    inner = jnp.sum(probs * prob_grad, -1, keepdims=True)
    score_grad = (probs * (prob_grad - inner)).astype(bf16)
    scale = 1.0 / math.sqrt(head_size)
    query_grad = dot_nn(score_grad, keys) * scale
    key_grad = dot_tn(score_grad, query) * scale
    return query_grad.astype(bf16), key_grad.astype(bf16), value_grad.astype(bf16)


def norm_forward(number, res, acc, xhat, rstd, gains, shifts, lows):
    def block(rows):
        hidden = res[rows, :] + acc[rows, :]
        centred = hidden - jnp.mean(hidden, -1, keepdims=True)
        scale = lax.rsqrt(jnp.mean(centred * centred, -1, keepdims=True) + EPSILON)
        unit = centred * scale
        xhat[number, rows, :] = unit
        rstd[number, rows, :] = jnp.broadcast_to(scale, (BLOCK, 128))
        out = unit * gains[number : number + 1, :] + shifts[number : number + 1, :]
        res[rows, :] = out
        if lows is not None:
            lows[rows, :] = out.astype(jnp.bfloat16)

    row_blocks(res.shape[0], block)


def norm_backward(number, grad, acc, xhat, rstd, gains, low, norms):
    count = gains.shape[0]
    width = grad.shape[1]

    def step(i, carry):
        gain_sum, shift_sum = carry
        rows = pl.ds(pl.multiple_of(i * BLOCK, BLOCK), BLOCK)
        coming = grad[rows, :] if acc is None else grad[rows, :] + acc[rows, :]
        unit = xhat[number, rows, :]
        gain_sum += jnp.sum(coming * unit, 0, keepdims=True)
        shift_sum += jnp.sum(coming, 0, keepdims=True)
        scaled = coming * gains[number : number + 1, :]
        mean = jnp.mean(scaled, -1, keepdims=True)
        slope = jnp.mean(scaled * unit, -1, keepdims=True)
        out = (scaled - mean - unit * slope) * rstd[number, rows, 0:1]
        grad[rows, :] = out
        low[rows, :] = out.astype(jnp.bfloat16)
        return gain_sum, shift_sum

    zero = jnp.zeros((1, width), jnp.float32)
    gain_sum, shift_sum = lax.fori_loop(0, grad.shape[0] // BLOCK, step, (zero, zero))
    norms[number : number + 1, :] = gain_sum
    norms[count + number : count + number + 1, :] = shift_sum


def turn_over(left, tokens, rows):
    part = left.shape[4]
    for number, source in enumerate((tokens, rows.at[2], rows.at[0], rows.at[3], rows.at[1], rows.at[4])):
        turned = source[...].T
        for y in range(2):
            for x in range(2):
                for c in range(2):
                    first = (4 * y + 2 * x + c) * part
                    left[c, number, y, x] = turned[first : first + part]


def layer_kernel(
    lengths, counts, text_tokens, image_tokens, text_cot, image_cot,
    text_gains, text_shifts, image_gains, image_shifts,
    text_cross, image_cross, text_cross_out, image_cross_out, text_up, text_down,
    image_up, image_down, text_self, image_self, image_self_out,
    text_output, image_output, text_grad, image_grad,
    text_left, image_left, text_right, text_extra, image_right, text_norms, image_norms,
    slot, load_sem, text_acc, image_acc, text_xhat, image_xhat, text_rstd, image_rstd,
    text_slope, image_slope, text_qkv, image_qkv, text_sqkv, image_sqkv,
    mask_ti, mask_it, mask_tt, mask_ii, text_rows, image_rows,
):
    f32, bf16 = jnp.float32, jnp.bfloat16
    rows_t, rows_i = text_tokens.shape[0], image_tokens.shape[0]
    width_t, width_i = text_tokens.shape[1], image_tokens.shape[1]
    pairs = lengths.shape[0]
    per_t, per_i = rows_t // pairs, rows_i // pairs
    zs = text_right.shape[1]
    inner = zs * TILE
    ups = text_up.shape[1] // (zs * TILE)

    def whole(ref, row):
        flat = ref
        return [(flat, slice(None), row, ref.shape[-2], ref.shape[-1])]

    def three(ref):
        return [(ref.at[n], slice(None), n * ref.shape[1], ref.shape[1], ref.shape[2]) for n in range(ref.shape[0])]

    wide = slot.shape[2]
    loads = {
        "tc": three(text_cross),
        "ic": three(image_cross),
        "out": whole(text_cross_out, 0) + whole(image_cross_out, inner),
        "tu": [
            (text_up, pl.ds(n * wide, wide), n * width_t, width_t, wide)
            for n in range(text_up.shape[1] // wide)
        ],
        "td": whole(text_down, 0),
        "if": whole(image_up, 0) + whole(image_down, width_i),
        "ts": three(text_self),
        "is": three(image_self),
        "io": whole(image_self_out, 0),
    }
    order = ["tc", "ic", "out", "tu", "td", "if", "ts", "is", "io"]
    order += ["td", "if", "tu", "out", "tc", "ic"]
    slots = [0, 1, 2, 0, 1, 2, 0, 1, 2, 2, 0, 1, 2, 0, 1]

    def copies(number):
        where = slots[number]
        return [
            pltpu.make_async_copy(
                ref.at[:, cols] if isinstance(cols, slice) is False else ref,
                slot.at[where, pl.ds(row, rows), pl.ds(0, width)],
                load_sem.at[number, part],
            )
            for part, (ref, cols, row, rows, width) in enumerate(loads[order[number]])
        ]

    def start(number):
        for copy in copies(number):
            copy.start()

    def ready(number):
        for copy in copies(number):
            copy.wait()
        return slot.at[slots[number]]

    for number in range(3):
        start(number)

    def set_mask(ref, query_per, key_per, limits):
        query = lax.broadcasted_iota(jnp.int32, ref.shape, 0)
        key = lax.broadcasted_iota(jnp.int32, ref.shape, 1)
        seen = jnp.zeros(ref.shape, f32)
        for pair in range(pairs):
            inside = (query >= pair * query_per) & (query < (pair + 1) * query_per)
            inside &= (key >= pair * key_per) & (key < pair * key_per + limits[pair])
            seen = jnp.where(inside, 1.0, seen)
        ref[...] = seen

    set_mask(mask_ti, per_t, per_i, counts)
    set_mask(mask_it, per_i, per_t, lengths)
    set_mask(mask_tt, per_t, per_t, lengths)
    set_mask(mask_ii, per_i, per_i, counts)
    text_output[...] = text_tokens[...].astype(f32)
    image_output[...] = image_tokens[...].astype(f32)

    def clear():
        text_acc[...] = jnp.zeros(text_acc.shape, f32)
        image_acc[...] = jnp.zeros(image_acc.shape, f32)

    clear()

    def project_tiles(rows_ref, weights, width, kept):
        def body(z, carry):
            for n in range(3):
                tile = dot_nn(rows_ref[...], weights[n * width : (n + 1) * width, tile_at(z)])
                kept[n, :, tile_at(z)] = tile.astype(bf16)
            return carry

        lax.fori_loop(0, zs, body, 0)

    def halves(tile):
        return tile[:, :128], tile[:, 128:]

    def pair_heads(fn, count, *tiles):
        size = TILE // count if count == 2 else 64
        results = []
        for h in range(count):
            results.append(fn(*[tile[:, h * size : (h + 1) * size] for tile in tiles]))
        return results

    project_tiles(text_tokens, ready(0), width_t, text_qkv)
    project_tiles(image_tokens, ready(1), width_i, image_qkv)
    start(3)
    start(4)
    outs = ready(2)

    def cross_forward_tile(z, carry):
        tq, tk, tv = [text_qkv[n, :, tile_at(z)] for n in range(3)]
        iq, ik, iv = [image_qkv[n, :, tile_at(z)] for n in range(3)]
        text_heads = pair_heads(
            lambda q, k, v: head_forward(q, k, v, mask_ti[...], CROSS_HEAD), 2, tq, ik, iv
        )
        image_heads = pair_heads(
            lambda q, k, v: head_forward(q, k, v, mask_it[...], CROSS_HEAD), 2, iq, tk, tv
        )
        text_context = jnp.concatenate(text_heads, -1)
        image_context = jnp.concatenate(image_heads, -1)
        text_right[3, z] = text_context
        image_right[3, z] = image_context
        text_acc[...] += dot_nn(text_context, outs[tile_at(z), 0:width_t])
        offset = pl.ds(pl.multiple_of(inner + z * TILE, TILE), TILE)
        image_acc[...] += dot_nn(image_context, outs[offset, 0:width_i])
        return carry

    lax.fori_loop(0, zs, cross_forward_tile, 0)
    start(5)
    norm_forward(0, text_output, text_acc, text_xhat, text_rstd, text_gains, text_shifts, text_rows.at[0])
    norm_forward(0, image_output, image_acc, image_xhat, image_rstd, image_gains, image_shifts, image_rows.at[0])

    def gelu_tile(upper):
        normal = 0.5 * (1.0 + lax.erf(upper * ROOT_HALF))
        slope = normal + upper * (DENSITY * jnp.exp(-0.5 * upper * upper))
        return (upper * normal).astype(bf16), slope

    up_t = ready(3)
    per_wide = wide // TILE

    def text_up_tile(j, carry):
        rows = pl.ds(pl.multiple_of((j // per_wide) * width_t, 8), width_t)
        upper = dot_nn(text_rows[0], up_t[rows, tile_at(j % per_wide)])
        middle, slope = gelu_tile(upper)
        text_slope[j] = slope
        text_right[7 + j % ups, j // ups] = middle
        return carry

    lax.fori_loop(0, zs * ups, text_up_tile, 0)
    start(6)
    down_t = ready(4)
    clear()

    def text_down_tile(j, carry):
        text_acc[...] += dot_nn(text_right[7 + j % ups, j // ups], down_t[tile_at(j), 0:width_t])
        return carry

    lax.fori_loop(0, zs * ups, text_down_tile, 0)
    start(7)
    both_i = ready(5)

    def image_up_tile(z, carry):
        middle, slope = gelu_tile(dot_nn(image_rows[0], both_i[0:width_i, tile_at(z)]))
        image_slope[z] = slope
        image_right[5, z] = middle
        offset = pl.ds(pl.multiple_of(width_i + z * TILE, TILE), TILE)
        image_acc[...] += dot_nn(middle, both_i[offset, 0:width_i])
        return carry

    lax.fori_loop(0, zs, image_up_tile, 0)
    start(8)
    norm_forward(1, text_output, text_acc, text_xhat, text_rstd, text_gains, text_shifts, text_rows.at[1])
    norm_forward(1, image_output, image_acc, image_xhat, image_rstd, image_gains, image_shifts, image_rows.at[1])

    clear()
    self_t = ready(6)
    project_tiles(text_rows.at[1], self_t, width_t, text_sqkv)
    self_i = ready(7)
    project_tiles(image_rows.at[1], self_i, width_i, image_sqkv)
    out_i = ready(8)
    share = TILE - TEXT_HEAD
    heads_t = share // TEXT_HEAD

    def self_forward_tile(z, carry):
        text_tiles = [text_sqkv[n, :, tile_at(z)] for n in range(3)]
        heads = pair_heads(
            lambda q, k, v: head_forward(q, k, v, mask_tt[...], TEXT_HEAD), heads_t, *text_tiles
        )
        blank = jnp.zeros((rows_t, TEXT_HEAD), bf16)
        text_extra[z] = jnp.concatenate([blank] + heads, -1)
        context = jnp.concatenate(heads + [blank], -1)
        text_acc[...] += dot_nt(context, self_t[3 * width_t : 4 * width_t, tile_at(z)])
        image_tiles = [image_sqkv[n, :, tile_at(z)] for n in range(3)]
        image_heads = pair_heads(
            lambda q, k, v: head_forward(q, k, v, mask_ii[...], IMAGE_HEAD), 2, *image_tiles
        )
        image_context = jnp.concatenate(image_heads, -1)
        image_right[9, z] = image_context
        image_acc[...] += dot_nn(image_context, out_i[tile_at(z), 0:width_i])
        return carry

    lax.fori_loop(0, zs, self_forward_tile, 0)
    norm_forward(2, text_output, text_acc, text_xhat, text_rstd, text_gains, text_shifts, None)
    norm_forward(2, image_output, image_acc, image_xhat, image_rstd, image_gains, image_shifts, None)

    text_grad[...] = text_cot[...].astype(f32)
    image_grad[...] = image_cot[...].astype(f32)
    norm_backward(2, text_grad, None, text_xhat, text_rstd, text_gains, text_rows.at[4], text_norms)
    norm_backward(2, image_grad, None, image_xhat, image_rstd, image_gains, image_rows.at[4], image_norms)
    clear()

    def self_back_tile(z, carry):
        text_tiles = [text_sqkv[n, :, tile_at(z)] for n in range(3)]
        context_grad = dot_nt_rows(text_rows[4], self_t, z)
        grads = pair_heads(
            lambda q, k, v, d: head_back(q, k, v, mask_tt[...], TEXT_HEAD, d),
            heads_t, *text_tiles, context_grad,
        )
        blank = jnp.zeros((rows_t, TEXT_HEAD), bf16)
        dq, dk, dv = [[grads[h][n] for h in range(heads_t)] for n in range(3)]
        pieces = dq + dk + dv
        text_right[10, z] = jnp.concatenate(pieces[0:4], -1)
        text_right[11, z] = jnp.concatenate(pieces[4:8], -1)
        text_right[12, z] = jnp.concatenate(pieces[8:9] + [blank] * 3, -1)
        total = jnp.zeros((rows_t, width_t), f32)
        for n, parts in enumerate((dq, dk, dv)):
            joined = jnp.concatenate(parts + [blank], -1)
            total += dot_nt(joined, self_t[n * width_t : (n + 1) * width_t, tile_at(z)])
        text_acc[...] += total
        return carry

    def dot_nt_rows(coming, weights, z):
        return dot_nn(coming, weights[3 * width_t : 4 * width_t, tile_at(z)]).astype(bf16)

    def self_back_image(z, carry):
        image_tiles = [image_sqkv[n, :, tile_at(z)] for n in range(3)]
        context_grad = dot_nt(image_rows[4], out_i[tile_at(z), 0:width_i]).astype(bf16)
        grads = pair_heads(
            lambda q, k, v, d: head_back(q, k, v, mask_ii[...], IMAGE_HEAD, d),
            2, *image_tiles, context_grad,
        )
        total = jnp.zeros((rows_i, width_i), f32)
        for n in range(3):
            joined = jnp.concatenate([grads[0][n], grads[1][n]], -1)
            image_right[6 + n, z] = joined
            total += dot_nt(joined, self_i[n * width_i : (n + 1) * width_i, tile_at(z)])
        image_acc[...] += total
        return carry

    lax.fori_loop(0, zs, self_back_image, 0)
    start(9)
    lax.fori_loop(0, zs, self_back_tile, 0)
    start(10)
    start(11)
    norm_backward(1, text_grad, text_acc, text_xhat, text_rstd, text_gains, text_rows.at[3], text_norms)
    norm_backward(1, image_grad, image_acc, image_xhat, image_rstd, image_gains, image_rows.at[3], image_norms)
    clear()

    back_down = ready(9)

    def text_down_back(j, carry):
        middle_grad = dot_nt(text_rows[3], back_down[tile_at(j), 0:width_t])
        text_right[4 + j % ups, j // ups] = (middle_grad * text_slope[j]).astype(bf16)
        return carry

    lax.fori_loop(0, zs * ups, text_down_back, 0)
    start(12)
    back_i = ready(10)

    def image_ffn_back(z, carry):
        offset = pl.ds(pl.multiple_of(width_i + z * TILE, TILE), TILE)
        middle_grad = dot_nt(image_rows[3], back_i[offset, 0:width_i])
        upper_grad = (middle_grad * image_slope[z]).astype(bf16)
        image_right[4, z] = upper_grad
        image_acc[...] += dot_nt(upper_grad, back_i[0:width_i, tile_at(z)])
        return carry

    lax.fori_loop(0, zs, image_ffn_back, 0)
    start(13)
    back_up = ready(11)

    def text_up_back(j, carry):
        rows = pl.ds(pl.multiple_of((j // per_wide) * width_t, 8), width_t)
        text_acc[...] += dot_nt(text_right[4 + j % ups, j // ups], back_up[rows, tile_at(j % per_wide)])
        return carry

    lax.fori_loop(0, zs * ups, text_up_back, 0)
    start(14)
    norm_backward(0, text_grad, text_acc, text_xhat, text_rstd, text_gains, text_rows.at[2], text_norms)
    norm_backward(0, image_grad, image_acc, image_xhat, image_rstd, image_gains, image_rows.at[2], image_norms)
    clear()

    back_out = ready(12)
    cross_t = ready(13)
    cross_i = ready(14)

    def cross_back_tile(z, carry):
        tq, tk, tv = [text_qkv[n, :, tile_at(z)] for n in range(3)]
        iq, ik, iv = [image_qkv[n, :, tile_at(z)] for n in range(3)]
        text_ctx_grad = dot_nt(text_rows[2], back_out[tile_at(z), 0:width_t]).astype(bf16)
        offset = pl.ds(pl.multiple_of(inner + z * TILE, TILE), TILE)
        image_ctx_grad = dot_nt(image_rows[2], back_out[offset, 0:width_i]).astype(bf16)
        text_side = pair_heads(
            lambda q, k, v, d: head_back(q, k, v, mask_ti[...], CROSS_HEAD, d), 2, tq, ik, iv, text_ctx_grad
        )
        image_side = pair_heads(
            lambda q, k, v, d: head_back(q, k, v, mask_it[...], CROSS_HEAD, d), 2, iq, tk, tv, image_ctx_grad
        )

        def joined(side, n):
            return jnp.concatenate([side[0][n], side[1][n]], -1)

        text_parts = (joined(text_side, 0), joined(image_side, 1), joined(image_side, 2))
        image_parts = (joined(image_side, 0), joined(text_side, 1), joined(text_side, 2))
        total_t = jnp.zeros((rows_t, width_t), f32)
        total_i = jnp.zeros((rows_i, width_i), f32)
        for n in range(3):
            text_right[n, z] = text_parts[n]
            image_right[n, z] = image_parts[n]
            total_t += dot_nt(text_parts[n], cross_t[n * width_t : (n + 1) * width_t, tile_at(z)])
            total_i += dot_nt(image_parts[n], cross_i[n * width_i : (n + 1) * width_i, tile_at(z)])
        text_acc[...] += total_t
        image_acc[...] += total_i
        return carry

    lax.fori_loop(0, zs, cross_back_tile, 0)
    text_grad[...] += text_acc[...]
    image_grad[...] += image_acc[...]
    turn_over(text_left, text_tokens, text_rows)
    turn_over(image_left, image_tokens, image_rows)


def layer(lengths, counts, rows, params, weights, mp):
    f32, bf16 = jnp.float32, jnp.bfloat16
    text_tokens, image_tokens = rows[0], rows[1]
    rows_t, width_t = text_tokens.shape
    rows_i, width_i = image_tokens.shape
    text_up = weights[4]
    text_tiles = text_up.shape[1] // TILE
    inner = mp * TILE

    vmem = pl.BlockSpec(memory_space=pltpu.VMEM)
    out_shape = [
        jax.ShapeDtypeStruct((rows_t, width_t), f32),
        jax.ShapeDtypeStruct((rows_i, width_i), f32),
        jax.ShapeDtypeStruct((rows_t, width_t), f32),
        jax.ShapeDtypeStruct((rows_i, width_i), f32),
        jax.ShapeDtypeStruct((2, 6, 2, 2, width_t // 8, rows_t), bf16),
        jax.ShapeDtypeStruct((2, 6, 2, 2, width_i // 8, rows_i), bf16),
        jax.ShapeDtypeStruct((13, mp, rows_t, TILE), bf16),
        jax.ShapeDtypeStruct((mp, rows_t, TILE), bf16),
        jax.ShapeDtypeStruct((10, mp, rows_i, TILE), bf16),
        jax.ShapeDtypeStruct((2 * params[0].shape[0], width_t), f32),
        jax.ShapeDtypeStruct((2 * params[0].shape[0], width_i), f32),
    ]
    return pl.pallas_call(
        layer_kernel,
        out_shape=out_shape,
        in_specs=[pl.BlockSpec(memory_space=pltpu.SMEM)] * 2
        + [vmem] * 8
        + [pl.BlockSpec(memory_space=pl.ANY)] * len(weights),
        out_specs=[vmem] * len(out_shape),
        scratch_shapes=[
            pltpu.VMEM((3, 3 * width_i, inner), bf16),
            pltpu.SemaphoreType.DMA((15, 4)),
            pltpu.VMEM((rows_t, width_t), f32),
            pltpu.VMEM((rows_i, width_i), f32),
            pltpu.VMEM((3, rows_t, width_t), f32),
            pltpu.VMEM((3, rows_i, width_i), f32),
            pltpu.VMEM((3, rows_t, 128), f32),
            pltpu.VMEM((3, rows_i, 128), f32),
            pltpu.VMEM((text_tiles, rows_t, TILE), f32),
            pltpu.VMEM((mp, rows_i, TILE), f32),
            pltpu.VMEM((3, rows_t, inner), bf16),
            pltpu.VMEM((3, rows_i, inner), bf16),
            pltpu.VMEM((3, rows_t, inner), bf16),
            pltpu.VMEM((3, rows_i, inner), bf16),
            pltpu.VMEM((rows_t, rows_i), f32),
            pltpu.VMEM((rows_i, rows_t), f32),
            pltpu.VMEM((rows_t, rows_t), f32),
            pltpu.VMEM((rows_i, rows_i), f32),
            pltpu.VMEM((5, rows_t, width_t), bf16),
            pltpu.VMEM((5, rows_i, width_i), bf16),
        ],
        compiler_params=pltpu.CompilerParams(vmem_limit_bytes=67043328),
        name="layer",
    )(lengths, counts, *rows, *params, *weights)


def weight_kinds():
    return (
        ("col3", True), ("col3", False), ("row", True), ("row", False), ("col", True), ("row", True),
        ("col", False), ("row", False), ("col3", True), ("col3", False), ("row", False),
    )


def shards(
    text_tokens, image_regions, lengths, region_counts, text_cross, image_cross, text_cross_out,
    image_cross_out, text_up, text_down, image_up, image_down, text_self, text_self_out, image_self,
    image_self_out, text_gains, text_shifts, image_gains, image_shifts, text_cotangent, image_cotangent,
):
    mp, dp = lax.axis_size("mp"), lax.axis_size("dp")
    more = dp // 8
    text_out_turned = text_self_out.T[None]
    text_four = jnp.concatenate([text_self, text_out_turned])
    spare = 256 - text_four.shape[-1]
    text_four = jnp.pad(text_four, ((0, 0), (0, 0), (0, spare)))
    kinds = [kind for kind, unused in weight_kinds()]
    streams = [by_x for unused, by_x in weight_kinds()]
    weights = gather_all(
        (
            text_cross, image_cross, text_cross_out, image_cross_out, text_up, text_down, image_up,
            image_down, text_four, image_self, image_self_out,
        ),
        kinds, streams, mp, more,
    )
    pairs, regions = image_regions.shape[0], image_regions.shape[1]
    padding = (-regions) % 16

    def pad_regions(array):
        return jnp.pad(array, ((0, 0), (0, padding), (0, 0))).reshape(-1, array.shape[-1])

    def flat(array):
        return array.reshape(-1, array.shape[-1])

    (
        text_result, image_result, text_input_grad, image_input_grad,
        text_left, image_left, text_right, text_extra, image_right, text_norms, image_norms,
    ) = layer(
        lengths, region_counts,
        (flat(text_tokens), pad_regions(image_regions), flat(text_cotangent), pad_regions(image_cotangent)),
        (text_gains, text_shifts, image_gains, image_shifts),
        weights, mp,
    )
    text_result, text_input_grad = [
        array.reshape(text_tokens.shape) for array in (text_result, text_input_grad)
    ]
    image_result, image_input_grad = [
        array.reshape(pairs, regions + padding, -1)[:, :regions]
        for array in (image_result, image_input_grad)
    ]
    norms = jnp.concatenate([text_norms.reshape(-1, 128), image_norms.reshape(-1, 128)])
    text_sums, image_sums, norm_sums = reduce_all(
        text_left, text_right, text_extra, image_left, image_right, norms, more
    )
    if more > 1:
        norm_sums = lax.psum(norm_sums, "dp") / 8
        text_sums, image_sums = outer_sum(text_sums, more), outer_sum(image_sums, more)
    text_sums = text_sums.transpose(1, 0, 2).reshape(text_sums.shape[1], -1)
    image_sums = image_sums.transpose(1, 0, 2).reshape(image_sums.shape[1], -1)

    def columns(sums, widths):
        parts, start = [], 0
        for width in widths:
            parts.append(sums[:, start : start + width])
            start += width
        return parts

    def triple(parts):
        return jnp.stack(parts[:3])

    text_widths = [text_cross.shape[-1]] * 3 + [text_cross_out.shape[0]]
    text_widths += [text_up.shape[-1], text_down.shape[0]]
    text_widths += [text_self.shape[-1]] * 3 + [text_self_out.shape[0]]
    image_widths = [image_cross.shape[-1]] * 3 + [image_cross_out.shape[0]]
    image_widths += [image_up.shape[-1], image_down.shape[0]]
    image_widths += [image_self.shape[-1]] * 3 + [image_self_out.shape[0]]
    text_parts = columns(text_sums, text_widths)
    image_parts = columns(image_sums, image_widths)
    flat_norms = norm_sums.reshape(-1)
    text_size, image_size = text_gains.size, image_gains.size
    text_end = 2 * text_size
    return (
        text_result,
        image_result,
        text_input_grad,
        image_input_grad,
        triple(text_parts[:3]),
        triple(image_parts[:3]),
        text_parts[3].T,
        image_parts[3].T,
        text_parts[4],
        text_parts[5].T,
        image_parts[4],
        image_parts[5].T,
        triple(text_parts[6:9]),
        text_parts[9].T,
        triple(image_parts[6:9]),
        image_parts[9].T,
        flat_norms[:text_size].reshape(text_gains.shape),
        flat_norms[text_size:text_end].reshape(text_shifts.shape),
        flat_norms[text_end : text_end + image_size].reshape(image_gains.shape),
        flat_norms[text_end + image_size :].reshape(image_shifts.shape),
    )


def outer_sum(sums, more):
    chunks, rows, width = sums.shape
    apart = sums.reshape(chunks, 1, more, rows // more, width)
    low = lax.axis_index("dp") // more
    spread = jnp.zeros((chunks, 8, more, rows // more, width), sums.dtype)
    spread = lax.dynamic_update_slice(spread, apart, (0, low, 0, 0, 0))
    spread = spread.reshape(chunks, 8 * rows, width)
    return lax.psum_scatter(spread, "dp", scatter_dimension=1, tiled=True)


def solution(mesh):
    in_specs = (
        P(("dp", "mp"), None, None),
        P(("dp", "mp"), None, None),
        P(("dp", "mp")),
        P(("dp", "mp")),
        P(None, None, "mp"),
        P(None, None, "mp"),
        P("mp", None),
        P("mp", None),
        P(None, "mp"),
        P("mp", None),
        P(None, "mp"),
        P("mp", None),
        P(None, None, "mp"),
        P("mp", None),
        P(None, None, "mp"),
        P("mp", None),
        P(),
        P(),
        P(),
        P(),
        P(("dp", "mp"), None, None),
        P(("dp", "mp"), None, None),
    )
    out_specs = (
        P(("dp", "mp"), None, None),
        P(("dp", "mp"), None, None),
        P(("dp", "mp"), None, None),
        P(("dp", "mp"), None, None),
        P(None, "dp", "mp"),
        P(None, "dp", "mp"),
        P("mp", "dp"),
        P("mp", "dp"),
        P("dp", "mp"),
        P("mp", "dp"),
        P("dp", "mp"),
        P("mp", "dp"),
        P(None, "dp", "mp"),
        P("mp", "dp"),
        P(None, "dp", "mp"),
        P("mp", "dp"),
        P(),
        P(),
        P(),
        P(),
    )
    return jax.shard_map(shards, mesh=mesh, in_specs=in_specs, out_specs=out_specs, check_vma=False)
```

time: 832 us -> 543 us (0.65); the launches traced: 823 us -> 543 us
  local copies, waits for them, and re-layouts: 269 us -> 36.8 us
  matrix products: 109 us -> 0 us
  Pallas kernels: 410 us -> 502 us
  other arithmetic: 31.2 us -> 3.29 us
    dot_general x64 -> x0, matrix products: 109 us -> none  [the longest x20 47.3 us: project(): return jnp.dot(inputs, weight, preferred_element_type=jnp.float32)]
    pallas_call x2 -> x3, Pallas kernels: 410 us -> 502 us  [the longest x1 204 us: reduce_all(): pl.pallas_call(functools.partial(reduce_kernel, unit), out_shape=[jax.Sha...]
    unnamed x435 -> x45, local copies, waits for them, and re-layouts: 89.7 us -> 22.2 us
    reshape x28 -> x2, local copies, waits for them, and re-layouts: 57.8 us -> 1.5 us  [the longest x1 0.76 us: shards(): image_norms.reshape(-1, 128)]
    convert_element_type x37 -> x0, local copies, waits for them, and re-layouts: 44.1 us -> none  [the longest x9 11.2 us: attend(): return (context.reshape(queries.shape).astype(jnp.bfloat16), log_total)]
    slice x6 -> x2, local copies, waits for them, and re-layouts: 21.1 us -> 1.99 us  [shards(): array.reshape(pairs, regions + padding, -1)[:, :regions]]
    convert_element_type x16 -> x0, other arithmetic: 17.5 us -> none  [the longest x2 8.77 us: ffn_forward(): middle = gelu_exact(upper).astype(jnp.bfloat16)]
    concatenate x13 -> x0, local copies, waits for them, and re-layouts: 17.2 us -> none  [the longest x12 17.2 us: cut(): joined = jnp.concatenate(tiles, -1)]
where the time goes in v2:
time: 543 us
  Pallas kernels  502 us (92%)
  local copies, waits for them, and re-layouts  36.8 us (7%)
    pallas_call x1, Pallas kernels, reduce_all(): pl.pallas_call(functools.partial(reduce_kernel, unit), out_shape=[jax.Sha...  204 us
    pallas_call x1, Pallas kernels, gather_all(): pl.pallas_call(functools.partial(gather_kernel, unit, tuple(kinds), tuple...  202 us
    pallas_call x1, Pallas kernels, layer(): pl.pallas_call(layer_kernel, out_shape=out_shape, in_specs=[pl.BlockSpec(...  96 us
    unnamed x45, local copies, waits for them, and re-layouts  22.2 us

profile of v2, /device:TPU:0, one launch (start us, length us, event | category | flops | bytes accessed | tf_op | source)
XLA Modules:
  0.0 542.7 jit_solution(3741830505333456011)
XLA Ops:
  0.7 0.0 copy-start.16
  0.7 0.0 copy-start.15
  0.7 1.0 copy.68
  1.7 0.7 pad.11.clone
  2.4 0.9 copy.69
  3.3 0.7 pad.12.clone
  4.0 0.0 copy-done.16
  4.0 0.0 copy-done.15
  4.0 0.0 copy-start.9
  4.1 1.1 pad_maximum_fusion
  5.2 0.0 copy-start.7
  5.2 0.0 copy-start.8
  5.2 2.7 copy.70
  7.9 0.0 copy-start.5
  7.9 0.0 copy-start.6
  7.9 1.8 pad.13.clone
  9.7 0.0 copy-done.9
  9.7 0.0 copy-done.7
  9.7 0.0 copy-done.8
  9.8 0.0 copy-done.5
  9.8 0.5 copy-done.6
  10.3 0.0 copy-start.10
  10.3 1.0 copy-done.10
  11.3 0.0 copy-start.11
  11.3 1.0 copy-done.11
  12.3 0.0 copy-start.12
  12.3 1.0 copy-done.12
  13.4 1.0 copy-done.13
  14.4 1.0 copy-done.14
  15.4 201.8 %gather_weights.1 = (bf16[3,2,2,2,96,1024]{5,4,3,2,1,0:T(8,128)(2,1)}, bf16[3,2,2,2,128,1024]{5,4,3,2,1,0:T(8,128)(2,1)}, bf16[4,2,2,2,32,768]{5,4,3,2,1,0:T(8,1...) custom-call(bf16[3,2,2,2,96,256]{5,4,3,2,1,0:T(8,128)(2,1)S(1)} %bit, ...), custom_call_target="tpu_custom_call" | custom-call | tf_op jit(solution)/shard_map/gather_weights/pallas_call | solution.py:157
  217.2 0.0 copy-start
  217.2 1.4 copy-done
  218.6 1.3 copy-done.1
  219.9 1.4 copy-done.2
  221.3 1.4 copy-done.3
  222.7 1.1 copy-done.4
  223.8 96.0 %layer.1 = (f32[256,768]{1,0:T(8,128)}, f32[96,1024]{1,0:T(8,128)}, f32[256,768]{1,0:T(8,128)}, f32[96,1024]{1,0:T(8,128)}, bf16[2,6,2,2,96,256]{5,4,3,2,1,0:T(8...) custom-call(s32[2]{0:T(128)} %lengths.1, ...), custom_call_target="tpu_custom_call" | custom-call | tf_op jit(solution)/shard_map/layer/pallas_call | solution.py:866
  319.8 1.0 slice.108
  320.8 0.9 copy.66
  321.7 0.7 reshape.193
  322.5 0.8 reshape.194
  323.2 0.6 pad_maximum_fusion.5.norms
  323.8 204.1 %reduce_gradients.1 = (f32[13,96,256]{2,1,0:T(8,128)}, f32[10,128,256]{2,1,0:T(8,128)}, f32[84,128]{1,0:T(8,128)}) custom-call(bf16[2,6,2,2,96,256]{5,4,3,2,1,0:T(8,128)(2,1)} %get-tuple-element.60.text_left, bf16[13,4,256,256]{3,2,1,0:T(8,128)(2,1)} %get-tuple-element.61.text_right, bf16[4,256,256]{2,1,0:T(8,128)(2,1)} %get-tuple-element.62.text_extra, ...), custom_call_target="tpu_custom_call" | custom-call | tf_op jit(solution)/shard_map/reduce_gradients/pallas_call | solution.py:375
  527.9 1.4 copy.71
  529.3 1.7 copy.61
  531.0 0.0 copy-start.17
  531.0 0.8 slice_bitcast_fusion.1
  531.8 0.0 copy-done.17
  531.8 0.6 reshape.198
  532.5 0.6 reshape.200
  533.1 0.6 reshape.197
  533.7 0.6 reshape.199
  534.3 0.8 copy.63
  535.0 1.0 slice.109
  536.0 0.9 copy.67
  537.0 0.1 slice_bitcast_fusion.10
  537.1 0.7 copy.64
  537.8 0.7 pad_maximum_fusion.4
  538.6 0.7 slice_bitcast_fusion.14
  539.3 0.8 slice_bitcast_fusion
  540.1 0.7 pad_maximum_fusion.3
  540.8 0.1 pad_maximum_fusion.1
  540.9 0.9 copy.62
  541.8 0.9 copy.65
  (8 shorter events, 0.0 us)
Async XLA Ops:
  0.7 3.4 copy-start.16
  0.7 3.4 copy-start.15
  4.0 5.7 %copy-start.9 = (bf16[768,768]{1,0:T(8,128)(2,1)S(1)}, bf16[768,768]{1,0:T(8,128)(2,1)}, u32[]{:S(2)}) copy-start(bf16[768,768]{1,0:T(8,128)(2,1)} %param.31) | copy-start | bytes 3538948
  5.2 4.5 copy-start.7
  5.2 4.6 copy-start.8
  7.9 1.9 copy-start.5
  7.9 2.4 copy-start.6
  10.3 1.0 copy-start.10
  11.3 1.0 copy-start.11
  12.3 1.0 copy-start.12
  13.4 1.0 copy-start.13
  14.4 1.0 copy-start.14
  217.2 1.4 copy-start
  218.6 1.3 copy-start.1
  219.9 1.4 copy-start.2
  221.3 1.4 copy-start.3
  222.7 1.1 copy-start.4
  531.0 0.8 copy-start.17

commit v3 on v2

--- a/solution.py
+++ b/solution.py
@@ -36,25 +36,17 @@
     pl.semaphore_wait(barrier, len(partners))
 
 
-def view_of(ref, kind, shard, width, y, x, c):
-    if kind == "col3":
-        columns = pl.ds(pl.multiple_of(shard * width, 128), width)
-        return ref.at[:, y, x, c, :, columns]
-    if kind == "col":
-        columns = pl.ds(pl.multiple_of(shard * width, 128), width)
-        return ref.at[y, x, c, :, columns]
-    if kind == "row":
+def view_of(ref, matrix, shard, width, y, x, c):
+    if matrix is None:
         return ref.at[shard, y, x, c]
-    return ref.at[shard, :, y, x, c]
-
-
-def local_of(ref, kind, y, x, c):
-    if kind in ("col3", "split3"):
-        return ref.at[:, y, x, c]
-    return ref.at[y, x, c]
-
-
-def gather_kernel(unit, kinds, widths, streams, *refs):
+    return ref.at[matrix, y, x, c, :, pl.ds(pl.multiple_of(shard * width, 128), width)]
+
+
+LEAD = 2
+LAGS = (0, 2, 4, 6, 8)
+
+
+def gather_kernel(unit, kinds, widths, chunks, *refs):
     count = len(kinds)
     ins, outs = refs[:count], refs[count : 2 * count]
     own_sem, send_sem, recv_sem = refs[2 * count :]
@@ -64,105 +56,118 @@
     corner = flip(near, 2)
     owns = []
     for k in range(count):
-        own = pltpu.make_async_copy(
-            ins[k], view_of(outs[k], kinds[k], model, widths[k], every, every, every), own_sem.at[k]
-        )
-        own.start()
-        owns.append(own)
+        for matrix in range(ins[k].shape[0]) if kinds[k] == "cols" else (None,):
+            source = ins[k] if matrix is None else ins[k].at[matrix]
+            target = view_of(outs[k], matrix, model, widths[k], every, every, every)
+            own = pltpu.make_async_copy(source, target, own_sem.at[len(owns)])
+            own.start()
+            owns.append(own)
     greet(data, model, unit)
-
-    def send(k, slot, source, target, partner):
-        copy = pltpu.make_async_remote_copy(
+    copies = {}
+
+    def send(n, slot, source, target, partner):
+        copies[n, slot] = pltpu.make_async_remote_copy(
             src_ref=source,
             dst_ref=target,
-            send_sem=send_sem.at[k, slot],
-            recv_sem=recv_sem.at[k, slot],
+            send_sem=send_sem.at[n, slot],
+            recv_sem=recv_sem.at[n, slot],
             device_id=partner,
             device_id_type=MESH_ID,
         )
-        copy.start()
-        return copy
-
-    def piece(k, shard, y, x, c):
-        return view_of(outs[k], kinds[k], shard, widths[k], y, x, c)
-
-    copies = {}
-    for k in range(count):
-        mine = local_of(ins[k], kinds[k], y, x, c)
-        copies[k, 0] = send(k, 0, mine, piece(k, model, y, x, c), (data, far))
-
-    def pair_up(k):
-        mine = local_of(ins[k], kinds[k], y, x, c)
-        copies[k, 1] = send(k, 1, mine, piece(k, model, y, x, c), (data, near))
-        copies[k, 0].wait_recv()
-        block = piece(k, far, y, x, c)
-        copies[k, 2] = send(k, 2, block, block, (data, near))
-
-    def spread(k, stage):
-        first_x = streams[k] == (stage == 0)
-        if stage == 2:
-            where, partner = (every, every, c), (flip(data, unit), model)
-        elif stage == 0:
-            where = (y, x, c)
-            partner = (flip(data, (2 if first_x else 4) * unit), model)
+        copies[n, slot].start()
+
+    def piece(n, shard, where):
+        k, matrix, unused, unused = chunks[n]
+        return view_of(outs[k], matrix, shard, widths[k], *where)
+
+    def mine(n, where):
+        k, matrix, unused, unused = chunks[n]
+        return ins[k].at[where] if matrix is None else ins[k].at[(matrix,) + where]
+
+    x_side = (flip(data, 2 * unit), model)
+    y_side = (flip(data, 4 * unit), model)
+    z_side = (data, near)
+    single = (y, x, c)
+
+    def relay(n, slot, shard, where, partner):
+        block = piece(n, shard, where)
+        send(n, slot, block, block, partner)
+
+    def advance(n, stage):
+        x_first, early = chunks[n][2:]
+        first, second = (x_side, y_side) if x_first else (y_side, x_side)
+        double = (y, every, c) if x_first else (every, x, c)
+        if stage == 0:
+            send(n, 0, mine(n, single), piece(n, model, single), (data, far))
+        elif stage == 1 and not early:
+            send(n, 1, mine(n, single), piece(n, model, single), z_side)
+            copies[n, 0].wait_recv()
+            relay(n, 2, far, single, z_side)
+        elif stage == 2 and not early:
+            relay(n, 3, far, single, first)
+            copies[n, 1].wait_recv()
+            relay(n, 4, near, single, first)
+            copies[n, 2].wait_recv()
+            relay(n, 5, corner, single, first)
+        elif stage == 1:
+            copies[n, 0].wait_recv()
+            relay(n, 3, far, single, first)
+        elif stage == 2:
+            send(n, 1, mine(n, double), piece(n, model, double), z_side)
+            copies[n, 3].wait_recv()
+            relay(n, 2, far, double, z_side)
+        elif stage == 3:
+            before = (None, 1, 2) if early else (3, 4, 5)
+            for number, shard in enumerate((far, near, corner)):
+                if before[number] is not None:
+                    copies[n, before[number]].wait_recv()
+                relay(n, 6 + number, shard, double, second)
         else:
-            where = (y, every, c) if streams[k] else (every, x, c)
-            partner = (flip(data, (2 if first_x else 4) * unit), model)
-        base = 3 + 3 * stage
-        for number, shard in enumerate((far, near, corner)):
-            if stage == 0:
-                if number > 0:
-                    copies[k, number].wait_recv()
-            else:
-                copies[k, base - 3 + number].wait_recv()
-            block = piece(k, shard, *where)
-            copies[k, base + number] = send(k, base + number, block, block, partner)
-
-    for step in range(count + 3):
-        if step < count:
-            pair_up(step)
-        for stage in range(3):
-            k = step - 1 - stage
-            if 0 <= k < count:
-                spread(k, stage)
-    for k in range(count):
-        for number in range(3):
-            copies[k, 9 + number].wait_recv()
-        owns[k].wait()
-        for slot in range(12):
-            copies[k, slot].wait_send()
-
-
-def gather_all(arrays, kinds, streams, mp, unit):
-    ins, outs, widths, finals = [], [], [], []
+            for number, shard in enumerate((far, near, corner)):
+                copies[n, 6 + number].wait_recv()
+                relay(n, 9 + number, shard, (every, every, c), (flip(data, unit), model))
+
+    total = len(chunks)
+    for step in range(total + LAGS[-1]):
+        for stage, lag in enumerate(LAGS):
+            if 0 <= step - lag < total:
+                advance(step - lag, stage)
+    for n in range(total):
+        for slot in range(9, 12):
+            copies[n, slot].wait_recv()
+    for own in owns:
+        own.wait()
+    for copy in copies.values():
+        copy.wait_send()
+
+
+def gather_all(arrays, kinds, chunks, mp, unit):
+    ins, outs, widths, finals, owned = [], [], [], [], 0
     for array, kind in zip(arrays, kinds):
-        widths.append(array.shape[-1])
         rows, width = array.shape[-2] // 8, array.shape[-1]
-        if kind in ("col3", "split3"):
-            ins.append(array.reshape(array.shape[0], 2, 2, 2, rows, width))
+        widths.append(width)
+        if kind == "cols":
+            lead = array.size // (8 * rows * width)
+            ins.append(array.reshape(lead, 2, 2, 2, rows, width))
+            shape = (lead, 2, 2, 2, rows, mp * width)
+            finals.append(array.shape[:-1] + (mp * width,))
+            owned += lead
         else:
             ins.append(array.reshape(2, 2, 2, rows, width))
-        if kind == "col3":
-            shape, final = (array.shape[0], 2, 2, 2, rows, mp * width), (array.shape[0], 8 * rows, mp * width)
-        elif kind == "col":
-            shape, final = (2, 2, 2, rows, mp * width), (8 * rows, mp * width)
-        elif kind == "row":
-            shape, final = (mp, 2, 2, 2, rows, width), (mp * 8 * rows, width)
-        else:
-            shape = (mp, array.shape[0], 2, 2, 2, rows, width)
-            final = (mp, array.shape[0], 8 * rows, width)
+            shape = (mp, 2, 2, 2, rows, width)
+            finals.append((mp * 8 * rows, width))
+            owned += 1
         outs.append(jax.ShapeDtypeStruct(shape, array.dtype))
-        finals.append(final)
     count = len(arrays)
     results = pl.pallas_call(
-        functools.partial(gather_kernel, unit, tuple(kinds), tuple(widths), tuple(streams)),
+        functools.partial(gather_kernel, unit, tuple(kinds), tuple(widths), tuple(chunks)),
         out_shape=outs,
         in_specs=[pl.BlockSpec(memory_space=pltpu.VMEM)] * count,
         out_specs=[pl.BlockSpec(memory_space=pl.ANY)] * count,
         scratch_shapes=[
-            pltpu.SemaphoreType.DMA((count,)),
-            pltpu.SemaphoreType.DMA((count, 12)),
-            pltpu.SemaphoreType.DMA((count, 12)),
+            pltpu.SemaphoreType.DMA((owned,)),
+            pltpu.SemaphoreType.DMA((len(chunks), 12)),
+            pltpu.SemaphoreType.DMA((len(chunks), 12)),
         ],
         compiler_params=pltpu.CompilerParams(
             collective_id=0, has_side_effects=True, vmem_limit_bytes=32 * 1024 * 1024
@@ -172,6 +177,19 @@
     return [result.reshape(final) for result, final in zip(results, finals)]
 
 
+KINDS = ("cols", "cols", "rows", "rows", "cols", "rows", "cols", "rows", "cols", "cols", "rows")
+SEQUENCE = (
+    (0, 0), (1, 0), (0, 1), (1, 1), (0, 2), (1, 2), (2, None), (3, None), (4, 0), (6, 0), (5, None), (7, None),
+    (8, 0), (9, 0), (8, 1), (9, 1), (8, 2), (9, 2), (8, 3), (10, None),
+)
+
+
+def chunk_plan():
+    return tuple(
+        (k, matrix, n % 4 in (0, 3), n % 2 == 1) for n, (k, matrix) in enumerate(SEQUENCE)
+    )
+
+
 def steps_up(k, marks):
     total = 0
     for mark in marks:
@@ -179,6 +197,7 @@
     return total
 
 
+STAGE_LAGS = (0, 2, 4, 6, 8, 10)
 TEXT_MARKS = (3, 4, 7, 10)
 IMAGE_MARKS = (3, 4, 5, 6, 9)
 
@@ -203,22 +222,27 @@
     far = (data, flip(model, 2))
     greet(data, model, unit)
 
-    def stream(left, right, extra, out, outgoing, bufs, send_sem, recv_sem, marks, x_first):
+    def stream(left, right, extra, out, outgoing, bufs, send_sem, recv_sem, marks, turn_first):
         r0, r1, r2, r3, r4 = bufs
         total = right.shape[0]
         rows = left.shape[-2]
 
+        def order(k):
+            by_y = (k + turn_first) % 2
+            by_x = 1 - by_y
+            first, second = x * by_x + y * by_y, y * by_x + x * by_y
+            return by_x, first, second
+
         def copy(k, stage):
+            by_x, first, second = order(k)
             if stage == 0:
                 pair = (outgoing.at[k % 2], r0.at[k], core)
             elif stage == 1:
-                source = r0.at[k, :, 1 - x] if x_first else r0.at[k, 1 - y]
-                pair = (source, r1.at[k], along_x if x_first else along_y)
+                pair = (r0.at[k, 1 - first], r1.at[k], (flip(data, (4 - 2 * by_x) * unit), model))
             elif stage == 2:
-                source = r1.at[k, 1 - y] if x_first else r1.at[k, 1 - x]
-                pair = (source, r2.at[k], along_y if x_first else along_x)
+                pair = (r1.at[k, :, :, 1 - low], r2.at[k], near)
             elif stage == 3:
-                pair = (r2.at[k, :, 1 - low], r3.at[k], near)
+                pair = (r2.at[k, 1 - second], r3.at[k], (flip(data, (2 + 2 * by_x) * unit), model))
             else:
                 pair = (r3.at[k, 1 - high], r4.at[k], far)
             return pltpu.make_async_remote_copy(
@@ -248,13 +272,21 @@
                     value += jnp.dot(more, extra[z], preferred_element_type=f32)
                     put(z, value.reshape(2, 2, rows, 256))
 
+        def places(k):
+            by_x, unused, unused = order(k)
+            for y_side in range(2):
+                for x_side in range(2):
+                    first = x_side * by_x + y_side * (1 - by_x)
+                    yield y_side, x_side, first, y_side + x_side - first
+
         def begin(k):
             @pl.when(k >= 2)
             def _():
                 copy(k - 2, 0).wait_send()
 
             def put(z, value):
-                outgoing[k % 2, :, :, z // 2, z % 2] = value.astype(bf16)
+                for y_side, x_side, first, second in places(k):
+                    outgoing[k % 2, first, second, z // 2, z % 2] = value[y_side, x_side].astype(bf16)
 
             products(k, 1 - c, put)
             copy(k, 0).start()
@@ -263,8 +295,9 @@
             copy(k, 0).wait_recv()
 
             def put(z, value):
-                held = r0[k, :, :, z // 2, z % 2].astype(f32)
-                r0[k, :, :, z // 2, z % 2] = (held + value).astype(bf16)
+                for y_side, x_side, first, second in places(k):
+                    held = r0[k, first, second, z // 2, z % 2].astype(f32)
+                    r0[k, first, second, z // 2, z % 2] = (held + value[y_side, x_side]).astype(bf16)
 
             products(k, c, put)
             copy(k, 1).start()
@@ -274,17 +307,17 @@
 
         def second(k):
             copy(k, 1).wait_recv()
-            add_into(r1, k, r0[k, :, x] if x_first else r0[k, y])
+            add_into(r1, k, r0[k, order(k)[1]])
             copy(k, 2).start()
 
         def third(k):
             copy(k, 2).wait_recv()
-            add_into(r2, k, r1[k, y] if x_first else r1[k, x])
+            add_into(r2, k, r1[k, :, :, low])
             copy(k, 3).start()
 
         def fourth(k):
             copy(k, 3).wait_recv()
-            add_into(r3, k, r2[k, :, low])
+            add_into(r3, k, r2[k, order(k)[2]])
             copy(k, 4).start()
 
         def last(k):
@@ -305,13 +338,13 @@
 
     text_total, text_stages, text_finish = stream(
         text_left, text_right, text_extra, text_out, text_send,
-        (text_r0, text_r1, text_r2, text_r3, text_r4), text_ss, text_rs, TEXT_MARKS, True,
+        (text_r0, text_r1, text_r2, text_r3, text_r4), text_ss, text_rs, TEXT_MARKS, 0,
     )
     image_total, image_stages, image_finish = stream(
         image_left, image_right, None, image_out, image_send,
-        (image_r0, image_r1, image_r2, image_r3, image_r4), image_ss, image_rs, IMAGE_MARKS, False,
+        (image_r0, image_r1, image_r2, image_r3, image_r4), image_ss, image_rs, IMAGE_MARKS, 1,
     )
-    lags = (0, 1, 3, 5, 6, 7)
+    lags = STAGE_LAGS
     partners = (core, along_x, along_y, near, far)
 
     def norm_copy(stage):
@@ -897,13 +930,6 @@
     )(lengths, counts, *rows, *params, *weights)
 
 
-def weight_kinds():
-    return (
-        ("col3", True), ("col3", False), ("row", True), ("row", False), ("col", True), ("row", True),
-        ("col", False), ("row", False), ("col3", True), ("col3", False), ("row", False),
-    )
-
-
 def shards(
     text_tokens, image_regions, lengths, region_counts, text_cross, image_cross, text_cross_out,
     image_cross_out, text_up, text_down, image_up, image_down, text_self, text_self_out, image_self,
@@ -915,14 +941,12 @@
     text_four = jnp.concatenate([text_self, text_out_turned])
     spare = 256 - text_four.shape[-1]
     text_four = jnp.pad(text_four, ((0, 0), (0, 0), (0, spare)))
-    kinds = [kind for kind, unused in weight_kinds()]
-    streams = [by_x for unused, by_x in weight_kinds()]
     weights = gather_all(
         (
             text_cross, image_cross, text_cross_out, image_cross_out, text_up, text_down, image_up,
             image_down, text_four, image_self, image_self_out,
         ),
-        kinds, streams, mp, more,
+        KINDS, chunk_plan(), mp, more,
     )
     pairs, regions = image_regions.shape[0], image_regions.shape[1]
     padding = (-regions) % 16

time: 543 us -> 465 us (0.86)
  Pallas kernels: 502 us -> 424 us
    pallas_call x1, Pallas kernels: 202 us -> 154 us  [gather_all(): pl.pallas_call(functools.partial(gather_kernel, unit, tuple(kinds), tuple...]
    pallas_call x1, Pallas kernels: 204 us -> 174 us  [reduce_all(): pl.pallas_call(functools.partial(reduce_kernel, unit), out_shape=[jax.Sha...]
where the time goes in v3:
time: 465 us
  Pallas kernels  424 us (91%)
  local copies, waits for them, and re-layouts  36.8 us (8%)
    pallas_call x1, Pallas kernels, reduce_all(): pl.pallas_call(functools.partial(reduce_kernel, unit), out_shape=[jax.Sha...  174 us
    pallas_call x1, Pallas kernels, gather_all(): pl.pallas_call(functools.partial(gather_kernel, unit, tuple(kinds), tuple...  154 us
    pallas_call x1, Pallas kernels, layer(): pl.pallas_call(layer_kernel, out_shape=out_shape, in_specs=[pl.BlockSpec(...  96 us
    unnamed x45, local copies, waits for them, and re-layouts  22.2 us

profile of v3, /device:TPU:0, one launch (start us, length us, event | category | flops | bytes accessed | tf_op | source)
XLA Modules:
  0.0 464.5 jit_solution(3104191013823648279)
XLA Ops:
  0.7 0.0 copy-start.16
  0.7 0.0 copy-start.15
  0.7 1.0 copy.68
  1.7 0.7 pad.11.clone
  2.4 0.9 copy.69
  3.3 0.7 pad.12.clone
  4.0 0.0 copy-done.16
  4.0 0.0 copy-done.15
  4.0 0.0 copy-start.9
  4.1 1.1 pad_maximum_fusion
  5.2 0.0 copy-start.7
  5.2 0.0 copy-start.8
  5.2 2.7 copy.70
  7.9 0.0 copy-start.5
  7.9 0.0 copy-start.6
  7.9 1.8 pad.13.clone
  9.7 0.0 copy-done.9
  9.7 0.0 copy-done.7
  9.7 0.0 copy-done.8
  9.8 0.0 copy-done.5
  9.8 0.5 copy-done.6
  10.3 0.0 copy-start.10
  10.3 1.0 copy-done.10
  11.3 0.0 copy-start.11
  11.3 1.0 copy-done.11
  12.3 0.0 copy-start.12
  12.3 1.0 copy-done.12
  13.4 1.0 copy-done.13
  14.4 1.0 copy-done.14
  15.4 153.6 %gather_weights.1 = (bf16[3,2,2,2,96,1024]{5,4,3,2,1,0:T(8,128)(2,1)}, bf16[3,2,2,2,128,1024]{5,4,3,2,1,0:T(8,128)(2,1)}, bf16[4,2,2,2,32,768]{5,4,3,2,1,0:T(8,1...) custom-call(bf16[3,2,2,2,96,256]{5,4,3,2,1,0:T(8,128)(2,1)S(1)} %bit, ...), custom_call_target="tpu_custom_call" | custom-call | tf_op jit(solution)/shard_map/gather_weights/pallas_call | solution.py:162
  169.0 0.0 copy-start
  169.0 1.4 copy-done
  170.4 1.3 copy-done.1
  171.7 1.4 copy-done.2
  173.1 1.4 copy-done.3
  174.4 1.1 copy-done.4
  175.6 96.0 %layer.1 = (f32[256,768]{1,0:T(8,128)}, f32[96,1024]{1,0:T(8,128)}, f32[256,768]{1,0:T(8,128)}, f32[96,1024]{1,0:T(8,128)}, bf16[2,6,2,2,96,256]{5,4,3,2,1,0:T(8...) custom-call(s32[2]{0:T(128)} %lengths.1, ...), custom_call_target="tpu_custom_call" | custom-call | tf_op jit(solution)/shard_map/layer/pallas_call | solution.py:899
  271.6 1.0 slice.108
  272.6 0.9 copy.66
  273.5 0.7 reshape.193
  274.3 0.8 reshape.194
  275.0 0.6 pad_maximum_fusion.5.norms
  275.6 174.0 %reduce_gradients.1 = (f32[13,96,256]{2,1,0:T(8,128)}, f32[10,128,256]{2,1,0:T(8,128)}, f32[84,128]{1,0:T(8,128)}) custom-call(bf16[2,6,2,2,96,256]{5,4,3,2,1,0:T(8,128)(2,1)} %get-tuple-element.60.text_left, bf16[13,4,256,256]{3,2,1,0:T(8,128)(2,1)} %get-tuple-element.61.text_right, bf16[4,256,256]{2,1,0:T(8,128)(2,1)} %get-tuple-element.62.text_extra, ...), custom_call_target="tpu_custom_call" | custom-call | tf_op jit(solution)/shard_map/reduce_gradients/pallas_call | solution.py:408
  449.7 1.4 copy.71
  451.1 1.7 copy.61
  452.8 0.0 copy-start.17
  452.8 0.8 slice_bitcast_fusion.1
  453.6 0.0 copy-done.17
  453.6 0.6 reshape.198
  454.2 0.6 reshape.200
  454.8 0.6 reshape.197
  455.5 0.6 reshape.199
  456.1 0.8 copy.63
  456.8 1.0 slice.109
  457.8 0.9 copy.67
  458.8 0.1 slice_bitcast_fusion.10
  458.9 0.7 copy.64
  459.6 0.7 pad_maximum_fusion.4
  460.4 0.7 slice_bitcast_fusion.14
  461.0 0.8 slice_bitcast_fusion
  461.9 0.7 pad_maximum_fusion.3
  462.6 0.1 pad_maximum_fusion.1
  462.7 0.9 copy.62
  463.6 0.9 copy.65
  (8 shorter events, 0.0 us)
Async XLA Ops:
  0.7 3.4 copy-start.16
  0.7 3.4 copy-start.15
  4.0 5.7 %copy-start.9 = (bf16[768,768]{1,0:T(8,128)(2,1)S(1)}, bf16[768,768]{1,0:T(8,128)(2,1)}, u32[]{:S(2)}) copy-start(bf16[768,768]{1,0:T(8,128)(2,1)} %param.31) | copy-start | bytes 3538948
  5.2 4.5 copy-start.7
  5.2 4.6 copy-start.8
  7.9 1.9 copy-start.5
  7.9 2.4 copy-start.6
  10.3 1.0 copy-start.10
  11.3 1.0 copy-start.11
  12.3 1.0 copy-start.12
  13.4 1.0 copy-start.13
  14.4 1.0 copy-start.14
  169.0 1.4 copy-start
  170.4 1.3 copy-start.1
  171.7 1.4 copy-start.2
  173.1 1.4 copy-start.3
  174.4 1.1 copy-start.4
  452.8 0.8 copy-start.17

commit v4 on v3

--- a/solution.py
+++ b/solution.py
@@ -36,33 +36,13 @@
     pl.semaphore_wait(barrier, len(partners))
 
 
-def view_of(ref, matrix, shard, width, y, x, c):
-    if matrix is None:
-        return ref.at[shard, y, x, c]
-    return ref.at[matrix, y, x, c, :, pl.ds(pl.multiple_of(shard * width, 128), width)]
-
-
-LEAD = 2
 LAGS = (0, 2, 4, 6, 8)
 
 
-def gather_kernel(unit, kinds, widths, chunks, *refs):
-    count = len(kinds)
-    ins, outs = refs[:count], refs[count : 2 * count]
-    own_sem, send_sem, recv_sem = refs[2 * count :]
+def gather_steps(unit, kinds, chunks, ins, outs, send_sem, recv_sem):
     data, model, c, x, y = position(unit)
-    every = slice(None)
     near, far = flip(model, 1), flip(model, 2)
     corner = flip(near, 2)
-    owns = []
-    for k in range(count):
-        for matrix in range(ins[k].shape[0]) if kinds[k] == "cols" else (None,):
-            source = ins[k] if matrix is None else ins[k].at[matrix]
-            target = view_of(outs[k], matrix, model, widths[k], every, every, every)
-            own = pltpu.make_async_copy(source, target, own_sem.at[len(owns)])
-            own.start()
-            owns.append(own)
-    greet(data, model, unit)
     copies = {}
 
     def send(n, slot, source, target, partner):
@@ -76,27 +56,39 @@
         )
         copies[n, slot].start()
 
-    def piece(n, shard, where):
+    def rows_of(height, first, base, span):
+        start, count = span
+        return pl.ds(pl.multiple_of(base + start * (height // 8), 8), count * (height // 8))
+
+    def mine(n, span):
         k, matrix, unused, unused = chunks[n]
-        return view_of(outs[k], matrix, shard, widths[k], *where)
-
-    def mine(n, where):
+        if kinds[k] == "cols":
+            return ins[k].at[matrix, rows_of(ins[k].shape[1], 0, 0, span), :]
+        return ins[k].at[rows_of(ins[k].shape[0], 0, 0, span), :]
+
+    def piece(n, shard, span):
         k, matrix, unused, unused = chunks[n]
-        return ins[k].at[where] if matrix is None else ins[k].at[(matrix,) + where]
+        if kinds[k] == "cols":
+            width = ins[k].shape[2]
+            columns = pl.ds(pl.multiple_of(shard * width, 128), width)
+            return outs[k].at[matrix, rows_of(ins[k].shape[1], 0, 0, span), columns]
+        height = ins[k].shape[0]
+        return outs[k].at[rows_of(height, 0, shard * height, span), :]
 
     x_side = (flip(data, 2 * unit), model)
     y_side = (flip(data, 4 * unit), model)
     z_side = (data, near)
-    single = (y, x, c)
-
-    def relay(n, slot, shard, where, partner):
-        block = piece(n, shard, where)
+
+    def relay(n, slot, shard, span, partner):
+        block = piece(n, shard, span)
         send(n, slot, block, block, partner)
 
     def advance(n, stage):
         x_first, early = chunks[n][2:]
         first, second = (x_side, y_side) if x_first else (y_side, x_side)
-        double = (y, every, c) if x_first else (every, x, c)
+        low_bit, middle_bit = (x, y) if x_first else (y, x)
+        single = (4 * c + 2 * middle_bit + low_bit, 1)
+        double = (4 * c + 2 * middle_bit, 2)
         if stage == 0:
             send(n, 0, mine(n, single), piece(n, model, single), (data, far))
         elif stage == 1 and not early:
@@ -125,56 +117,29 @@
         else:
             for number, shard in enumerate((far, near, corner)):
                 copies[n, 6 + number].wait_recv()
-                relay(n, 9 + number, shard, (every, every, c), (flip(data, unit), model))
+                relay(n, 9 + number, shard, (4 * c, 4), (flip(data, unit), model))
 
     total = len(chunks)
-    for step in range(total + LAGS[-1]):
-        for stage, lag in enumerate(LAGS):
-            if 0 <= step - lag < total:
-                advance(step - lag, stage)
-    for n in range(total):
-        for slot in range(9, 12):
-            copies[n, slot].wait_recv()
-    for own in owns:
-        own.wait()
-    for copy in copies.values():
-        copy.wait_send()
-
-
-def gather_all(arrays, kinds, chunks, mp, unit):
-    ins, outs, widths, finals, owned = [], [], [], [], 0
-    for array, kind in zip(arrays, kinds):
-        rows, width = array.shape[-2] // 8, array.shape[-1]
-        widths.append(width)
-        if kind == "cols":
-            lead = array.size // (8 * rows * width)
-            ins.append(array.reshape(lead, 2, 2, 2, rows, width))
-            shape = (lead, 2, 2, 2, rows, mp * width)
-            finals.append(array.shape[:-1] + (mp * width,))
-            owned += lead
-        else:
-            ins.append(array.reshape(2, 2, 2, rows, width))
-            shape = (mp, 2, 2, 2, rows, width)
-            finals.append((mp * 8 * rows, width))
-            owned += 1
-        outs.append(jax.ShapeDtypeStruct(shape, array.dtype))
-    count = len(arrays)
-    results = pl.pallas_call(
-        functools.partial(gather_kernel, unit, tuple(kinds), tuple(widths), tuple(chunks)),
-        out_shape=outs,
-        in_specs=[pl.BlockSpec(memory_space=pltpu.VMEM)] * count,
-        out_specs=[pl.BlockSpec(memory_space=pl.ANY)] * count,
-        scratch_shapes=[
-            pltpu.SemaphoreType.DMA((owned,)),
-            pltpu.SemaphoreType.DMA((len(chunks), 12)),
-            pltpu.SemaphoreType.DMA((len(chunks), 12)),
-        ],
-        compiler_params=pltpu.CompilerParams(
-            collective_id=0, has_side_effects=True, vmem_limit_bytes=32 * 1024 * 1024
-        ),
-        name="gather_weights",
-    )(*ins)
-    return [result.reshape(final) for result, final in zip(results, finals)]
+    done = [0]
+
+    def run(limit):
+        while done[0] < min(limit, total + LAGS[-1]):
+            for stage, lag in enumerate(LAGS):
+                if 0 <= done[0] - lag < total:
+                    advance(done[0] - lag, stage)
+            done[0] += 1
+
+    def arrived(numbers):
+        run(max(numbers) + LAGS[-1] + 1)
+        for n in numbers:
+            for slot in range(9, 12):
+                copies[n, slot].wait_recv()
+
+    def finish():
+        for copy in copies.values():
+            copy.wait_send()
+
+    return run, arrived, finish
 
 
 KINDS = ("cols", "cols", "rows", "rows", "cols", "rows", "cols", "rows", "cols", "cols", "rows")
@@ -534,13 +499,14 @@
 
 
 def layer_kernel(
+    unit,
     lengths, counts, text_tokens, image_tokens, text_cot, image_cot,
     text_gains, text_shifts, image_gains, image_shifts,
-    text_cross, image_cross, text_cross_out, image_cross_out, text_up, text_down,
-    image_up, image_down, text_self, image_self, image_self_out,
+    in_a, in_b, in_c, in_d, in_e, in_f, in_g, in_h, in_i, in_j, in_k,
     text_output, image_output, text_grad, image_grad,
     text_left, image_left, text_right, text_extra, image_right, text_norms, image_norms,
-    slot, load_sem, text_acc, image_acc, text_xhat, image_xhat, text_rstd, image_rstd,
+    full_a, full_b, full_c, full_d, full_e, full_f, full_g, full_h, full_i, full_j, full_k,
+    send_sem, recv_sem, slot, load_sem, text_acc, image_acc, text_xhat, image_xhat, text_rstd, image_rstd,
     text_slope, image_slope, text_qkv, image_qkv, text_sqkv, image_sqkv,
     mask_ti, mask_it, mask_tt, mask_ii, text_rows, image_rows,
 ):
@@ -551,46 +517,59 @@
     per_t, per_i = rows_t // pairs, rows_i // pairs
     zs = text_right.shape[1]
     inner = zs * TILE
-    ups = text_up.shape[1] // (zs * TILE)
-
-    def whole(ref, row):
-        flat = ref
-        return [(flat, slice(None), row, ref.shape[-2], ref.shape[-1])]
-
-    def three(ref):
-        return [(ref.at[n], slice(None), n * ref.shape[1], ref.shape[1], ref.shape[2]) for n in range(ref.shape[0])]
-
-    wide = slot.shape[2]
+    ins = (in_a, in_b, in_c, in_d, in_e, in_f, in_g, in_h, in_i, in_j, in_k)
+    fulls = (full_a, full_b, full_c, full_d, full_e, full_f, full_g, full_h, full_i, full_j, full_k)
+    ups = in_e.shape[2] // TILE
+    data, model, unused, unused, unused = position(unit)
+    greet(data, model, unit)
+    run, arrived, finish = gather_steps(unit, KINDS, chunk_plan(), ins, fulls, send_sem, recv_sem)
+    run(6)
+
+    def three(k):
+        return [(k, n, n * ins[k].shape[1], False) for n in range(ins[k].shape[0])]
+
     loads = {
-        "tc": three(text_cross),
-        "ic": three(image_cross),
-        "out": whole(text_cross_out, 0) + whole(image_cross_out, inner),
-        "tu": [
-            (text_up, pl.ds(n * wide, wide), n * width_t, width_t, wide)
-            for n in range(text_up.shape[1] // wide)
-        ],
-        "td": whole(text_down, 0),
-        "if": whole(image_up, 0) + whole(image_down, width_i),
-        "ts": three(text_self),
-        "is": three(image_self),
-        "io": whole(image_self_out, 0),
+        "tc": three(0),
+        "ic": three(1),
+        "out": [(2, None, 0, False), (3, None, inner, False)],
+        "tu": [(4, 0, 0, True)],
+        "td": [(5, None, 0, False)],
+        "if": [(6, 0, 0, False), (7, None, width_i, False)],
+        "ts": three(8),
+        "is": three(9),
+        "io": [(10, None, 0, False)],
     }
     order = ["tc", "ic", "out", "tu", "td", "if", "ts", "is", "io"]
     order += ["td", "if", "tu", "out", "tc", "ic"]
     slots = [0, 1, 2, 0, 1, 2, 0, 1, 2, 2, 0, 1, 2, 0, 1]
 
     def copies(number):
-        where = slots[number]
-        return [
-            pltpu.make_async_copy(
-                ref.at[:, cols] if isinstance(cols, slice) is False else ref,
-                slot.at[where, pl.ds(row, rows), pl.ds(0, width)],
-                load_sem.at[number, part],
-            )
-            for part, (ref, cols, row, rows, width) in enumerate(loads[order[number]])
-        ]
+        where, found = slots[number], []
+        for k, matrix, row, stacked in loads[order[number]]:
+            for turn in range(zs):
+                shard = (model + turn) % zs
+                if matrix is None:
+                    height, width = ins[k].shape
+                    source = fulls[k].at[pl.ds(pl.multiple_of(shard * height, 8), height), :]
+                    source = ins[k] if turn == 0 else source
+                    rows = pl.ds(pl.multiple_of(row + shard * height, 8), height)
+                    target = slot.at[where, rows, pl.ds(0, width)]
+                else:
+                    unused, height, width = ins[k].shape
+                    columns = pl.ds(pl.multiple_of(shard * width, 128), width)
+                    source = ins[k].at[matrix] if turn == 0 else fulls[k].at[matrix, :, columns]
+                    if stacked:
+                        rows = pl.ds(pl.multiple_of(row + shard * height, 8), height)
+                        target = slot.at[where, rows, pl.ds(0, width)]
+                    else:
+                        target = slot.at[where, pl.ds(row, height), columns]
+                found.append(pltpu.make_async_copy(source, target, load_sem.at[number, len(found)]))
+        return found
 
     def start(number):
+        if number < 9:
+            wanted = {k for k, unused, unused, unused in loads[order[number]]}
+            arrived([n for n, chunk in enumerate(SEQUENCE) if chunk[0] in wanted])
         for copy in copies(number):
             copy.start()
 
@@ -598,9 +577,6 @@
         for copy in copies(number):
             copy.wait()
         return slot.at[slots[number]]
-
-    for number in range(3):
-        start(number)
 
     def set_mask(ref, query_per, key_per, limits):
         query = lax.broadcasted_iota(jnp.int32, ref.shape, 0)
@@ -644,10 +620,13 @@
             results.append(fn(*[tile[:, h * size : (h + 1) * size] for tile in tiles]))
         return results
 
+    start(0)
+    start(1)
+    run(16)
     project_tiles(text_tokens, ready(0), width_t, text_qkv)
+    start(2)
     project_tiles(image_tokens, ready(1), width_i, image_qkv)
-    start(3)
-    start(4)
+    run(18)
     outs = ready(2)
 
     def cross_forward_tile(z, carry):
@@ -668,8 +647,11 @@
         image_acc[...] += dot_nn(image_context, outs[offset, 0:width_i])
         return carry
 
-    lax.fori_loop(0, zs, cross_forward_tile, 0)
-    start(5)
+    lax.fori_loop(0, zs // 2, cross_forward_tile, 0)
+    start(3)
+    run(19)
+    lax.fori_loop(zs // 2, zs, cross_forward_tile, 0)
+    start(4)
     norm_forward(0, text_output, text_acc, text_xhat, text_rstd, text_gains, text_shifts, text_rows.at[0])
     norm_forward(0, image_output, image_acc, image_xhat, image_rstd, image_gains, image_shifts, image_rows.at[0])
 
@@ -678,19 +660,22 @@
         slope = normal + upper * (DENSITY * jnp.exp(-0.5 * upper * upper))
         return (upper * normal).astype(bf16), slope
 
+    start(5)
+    run(21)
     up_t = ready(3)
-    per_wide = wide // TILE
 
     def text_up_tile(j, carry):
-        rows = pl.ds(pl.multiple_of((j // per_wide) * width_t, 8), width_t)
-        upper = dot_nn(text_rows[0], up_t[rows, tile_at(j % per_wide)])
+        rows = pl.ds(pl.multiple_of((j // ups) * width_t, 8), width_t)
+        upper = dot_nn(text_rows[0], up_t[rows, tile_at(j % ups)])
         middle, slope = gelu_tile(upper)
         text_slope[j] = slope
         text_right[7 + j % ups, j // ups] = middle
         return carry
 
-    lax.fori_loop(0, zs * ups, text_up_tile, 0)
-    start(6)
+    lax.fori_loop(0, zs * ups // 2, text_up_tile, 0)
+    run(22)
+    lax.fori_loop(zs * ups // 2, zs * ups, text_up_tile, 0)
+    run(23)
     down_t = ready(4)
     clear()
 
@@ -699,7 +684,7 @@
         return carry
 
     lax.fori_loop(0, zs * ups, text_down_tile, 0)
-    start(7)
+    run(24)
     both_i = ready(5)
 
     def image_up_tile(z, carry):
@@ -711,11 +696,14 @@
         return carry
 
     lax.fori_loop(0, zs, image_up_tile, 0)
-    start(8)
+    run(25)
     norm_forward(1, text_output, text_acc, text_xhat, text_rstd, text_gains, text_shifts, text_rows.at[1])
     norm_forward(1, image_output, image_acc, image_xhat, image_rstd, image_gains, image_shifts, image_rows.at[1])
 
     clear()
+    start(6)
+    start(7)
+    start(8)
     self_t = ready(6)
     project_tiles(text_rows.at[1], self_t, width_t, text_sqkv)
     self_i = ready(7)
@@ -823,8 +811,8 @@
     back_up = ready(11)
 
     def text_up_back(j, carry):
-        rows = pl.ds(pl.multiple_of((j // per_wide) * width_t, 8), width_t)
-        text_acc[...] += dot_nt(text_right[4 + j % ups, j // ups], back_up[rows, tile_at(j % per_wide)])
+        rows = pl.ds(pl.multiple_of((j // ups) * width_t, 8), width_t)
+        text_acc[...] += dot_nt(text_right[4 + j % ups, j // ups], back_up[rows, tile_at(j % ups)])
         return carry
 
     lax.fori_loop(0, zs * ups, text_up_back, 0)
@@ -869,17 +857,17 @@
     lax.fori_loop(0, zs, cross_back_tile, 0)
     text_grad[...] += text_acc[...]
     image_grad[...] += image_acc[...]
+    finish()
     turn_over(text_left, text_tokens, text_rows)
     turn_over(image_left, image_tokens, image_rows)
 
 
-def layer(lengths, counts, rows, params, weights, mp):
+def layer(lengths, counts, rows, params, weights, mp, unit):
     f32, bf16 = jnp.float32, jnp.bfloat16
     text_tokens, image_tokens = rows[0], rows[1]
     rows_t, width_t = text_tokens.shape
     rows_i, width_i = image_tokens.shape
-    text_up = weights[4]
-    text_tiles = text_up.shape[1] // TILE
+    text_tiles = mp * weights[4].shape[2] // TILE
     inner = mp * TILE
 
     vmem = pl.BlockSpec(memory_space=pltpu.VMEM)
@@ -896,16 +884,23 @@
         jax.ShapeDtypeStruct((2 * params[0].shape[0], width_t), f32),
         jax.ShapeDtypeStruct((2 * params[0].shape[0], width_i), f32),
     ]
-    return pl.pallas_call(
-        layer_kernel,
-        out_shape=out_shape,
+    fulls = []
+    for array, kind in zip(weights, KINDS):
+        shape = array.shape[:-1] + (mp * array.shape[-1],) if kind == "cols" else (mp * array.shape[0], array.shape[1])
+        fulls.append(jax.ShapeDtypeStruct(shape, bf16))
+    chunks = len(SEQUENCE)
+    results = pl.pallas_call(
+        functools.partial(layer_kernel, unit),
+        out_shape=out_shape + fulls,
         in_specs=[pl.BlockSpec(memory_space=pltpu.SMEM)] * 2
         + [vmem] * 8
         + [pl.BlockSpec(memory_space=pl.ANY)] * len(weights),
-        out_specs=[vmem] * len(out_shape),
+        out_specs=[vmem] * len(out_shape) + [pl.BlockSpec(memory_space=pl.ANY)] * len(fulls),
         scratch_shapes=[
+            pltpu.SemaphoreType.DMA((chunks, 12)),
+            pltpu.SemaphoreType.DMA((chunks, 12)),
             pltpu.VMEM((3, 3 * width_i, inner), bf16),
-            pltpu.SemaphoreType.DMA((15, 4)),
+            pltpu.SemaphoreType.DMA((15, 4 * mp)),
             pltpu.VMEM((rows_t, width_t), f32),
             pltpu.VMEM((rows_i, width_i), f32),
             pltpu.VMEM((3, rows_t, width_t), f32),
@@ -925,9 +920,12 @@
             pltpu.VMEM((5, rows_t, width_t), bf16),
             pltpu.VMEM((5, rows_i, width_i), bf16),
         ],
-        compiler_params=pltpu.CompilerParams(vmem_limit_bytes=67043328),
+        compiler_params=pltpu.CompilerParams(
+            collective_id=0, has_side_effects=True, vmem_limit_bytes=67043328
+        ),
         name="layer",
     )(lengths, counts, *rows, *params, *weights)
+    return results[: len(out_shape)]
 
 
 def shards(
@@ -941,12 +939,9 @@
     text_four = jnp.concatenate([text_self, text_out_turned])
     spare = 256 - text_four.shape[-1]
     text_four = jnp.pad(text_four, ((0, 0), (0, 0), (0, spare)))
-    weights = gather_all(
-        (
-            text_cross, image_cross, text_cross_out, image_cross_out, text_up, text_down, image_up,
-            image_down, text_four, image_self, image_self_out,
-        ),
-        KINDS, chunk_plan(), mp, more,
+    weights = (
+        text_cross, image_cross, text_cross_out, image_cross_out, text_up[None], text_down,
+        image_up[None], image_down, text_four, image_self, image_self_out,
     )
     pairs, regions = image_regions.shape[0], image_regions.shape[1]
     padding = (-regions) % 16
@@ -964,7 +959,7 @@
         lengths, region_counts,
         (flat(text_tokens), pad_regions(image_regions), flat(text_cotangent), pad_regions(image_cotangent)),
         (text_gains, text_shifts, image_gains, image_shifts),
-        weights, mp,
+        weights, mp, more,
     )
     text_result, text_input_grad = [
         array.reshape(text_tokens.shape) for array in (text_result, text_input_grad)

time: 465 us -> 440 us (0.946)
  local copies, waits for them, and re-layouts: 36.8 us -> 23.5 us
  Pallas kernels: 424 us -> 412 us
    pallas_call x2 -> x1, Pallas kernels: 250 us -> 237 us  [layer(): pl.pallas_call(functools.partial(layer_kernel, unit), out_shape=out_shape...]
    unnamed x45 -> x20, local copies, waits for them, and re-layouts: 22.2 us -> 10.7 us
where the time goes in v4:
time: 440 us
  Pallas kernels  412 us (94%)
  local copies, waits for them, and re-layouts  23.5 us (5%)
    pallas_call x1, Pallas kernels, layer(): pl.pallas_call(functools.partial(layer_kernel, unit), out_shape=out_shape...  237 us
    pallas_call x1, Pallas kernels, reduce_all(): pl.pallas_call(functools.partial(reduce_kernel, unit), out_shape=[jax.Sha...  175 us
    unnamed x20, local copies, waits for them, and re-layouts  10.7 us

profile of v4, /device:TPU:0, one launch (start us, length us, event | category | flops | bytes accessed | tf_op | source)
XLA Modules:
  0.0 439.9 jit_solution(15408421291941042318)
XLA Ops:
  0.7 0.0 copy-start
  0.7 1.0 copy.70
  1.7 0.7 pad.11.clone
  2.4 0.9 copy.71
  3.3 0.7 pad.12.clone
  4.0 1.1 copy.58
  5.2 0.0 copy-done
  5.2 0.6 copy.59
  5.8 1.5 fusion.2.in_i
  7.3 237.0 %layer.1 = (f32[256,768]{1,0:T(8,128)}, f32[96,1024]{1,0:T(8,128)}, f32[256,768]{1,0:T(8,128)}, f32[96,1024]{1,0:T(8,128)}, bf16[2,6,2,2,96,256]{5,4,3,2,1,0:T(8...) custom-call(s32[2]{0:T(128)} %lengths.1, ...), custom_call_target="tpu_custom_call" | custom-call | tf_op jit(solution)/shard_map/layer/pallas_call | solution.py:892
  244.3 1.0 slice.108
  245.3 0.9 copy.68
  246.2 0.7 reshape.105
  246.9 0.8 reshape.106
  247.7 0.6 pad_maximum_fusion.4.norms
  248.3 175.0 %reduce_gradients.1 = (f32[13,96,256]{2,1,0:T(8,128)}, f32[10,128,256]{2,1,0:T(8,128)}, f32[84,128]{1,0:T(8,128)}) custom-call(bf16[2,6,2,2,96,256]{5,4,3,2,1,0:T(8,128)(2,1)} %get-tuple-element.38.text_left, bf16[13,4,256,256]{3,2,1,0:T(8,128)(2,1)} %get-tuple-element.39.text_right, bf16[4,256,256]{2,1,0:T(8,128)(2,1)} %get-tuple-element.40.text_extra, ...), custom_call_target="tpu_custom_call" | custom-call | tf_op jit(solution)/shard_map/reduce_gradients/pallas_call | solution.py:373
  423.3 1.4 copy.72
  424.7 1.7 copy.63
  426.4 0.0 copy-start.3
  426.4 0.8 slice_bitcast_fusion.1
  427.2 0.0 copy-done.3
  427.2 0.6 reshape.110
  427.9 0.6 reshape.112
  428.5 0.6 reshape.109
  429.1 0.6 reshape.111
  429.7 0.8 copy.65
  430.5 1.0 slice.109
  431.5 0.9 copy.69
  432.4 0.1 slice_bitcast_fusion.10
  432.5 0.7 copy.66
  433.3 0.7 pad_maximum_fusion.3
  434.0 0.7 slice_bitcast_fusion.14
  434.7 0.8 slice_bitcast_fusion
  435.5 0.7 pad_maximum_fusion.2
  436.2 0.0 copy-start.2
  436.2 0.1 pad_maximum_fusion
  436.3 0.0 copy-start.1
  436.3 0.9 copy.64
  437.2 0.9 copy.67
  438.1 0.0 copy-done.2
  438.1 0.9 copy.75
  439.0 0.0 copy-done.1
  439.0 0.9 copy.76
  (2 shorter events, 0.0 us)
Async XLA Ops:
  0.7 4.5 %copy-start = (bf16[3,768,192]{1,2,0:T(8,128)(2,1)S(1)}, bf16[3,768,192]{1,2,0:T(8,128)(2,1)}, u32[]{:S(2)}) copy-start(bf16[3,768,192]{1,2,0:T(8,128)(2,1)} %param.34) | copy-start | bytes 2654212
  426.4 0.8 copy-start.3
  436.2 1.9 copy-start.2
  436.3 2.7 copy-start.1

commit v5 on v4

--- a/solution.py
+++ b/solution.py
@@ -394,7 +394,10 @@
 ROOT_HALF = math.sqrt(0.5)
 DENSITY = 1.0 / math.sqrt(2.0 * math.pi)
 TILE = 256
-BLOCK = 32
+
+
+def block_of(rows):
+    return next(size for size in (64, 48, 32, 16) if rows % size == 0)
 
 
 def dot_nn(a, b):
@@ -405,16 +408,23 @@
     return lax.dot_general(a, b, (((1,), (1,)), ((), ())), preferred_element_type=jnp.float32)
 
 
+def joint_nt(parts, weights, width, z):
+    tiles = [weights[n * width : (n + 1) * width, tile_at(z)] for n in range(len(parts))]
+    return dot_nt(jnp.concatenate(parts, -1), jnp.concatenate(tiles, -1))
+
+
 def dot_tn(a, b):
     return lax.dot_general(a, b, (((0,), (0,)), ((), ())), preferred_element_type=jnp.float32)
 
 
 def row_blocks(rows, body):
+    size = block_of(rows)
+
     def step(i, carry):
-        body(pl.ds(pl.multiple_of(i * BLOCK, BLOCK), BLOCK))
-        return carry
-
-    lax.fori_loop(0, rows // BLOCK, step, 0)
+        body(pl.ds(pl.multiple_of(i * size, size), size))
+        return carry
+
+    lax.fori_loop(0, rows // size, step, 0)
 
 
 def tile_at(j):
@@ -453,7 +463,7 @@
         scale = lax.rsqrt(jnp.mean(centred * centred, -1, keepdims=True) + EPSILON)
         unit = centred * scale
         xhat[number, rows, :] = unit
-        rstd[number, rows, :] = jnp.broadcast_to(scale, (BLOCK, 128))
+        rstd[number, rows, :] = jnp.broadcast_to(scale, (scale.shape[0], 128))
         out = unit * gains[number : number + 1, :] + shifts[number : number + 1, :]
         res[rows, :] = out
         if lows is not None:
@@ -465,10 +475,11 @@
 def norm_backward(number, grad, acc, xhat, rstd, gains, low, norms):
     count = gains.shape[0]
     width = grad.shape[1]
+    size = block_of(grad.shape[0])
 
     def step(i, carry):
         gain_sum, shift_sum = carry
-        rows = pl.ds(pl.multiple_of(i * BLOCK, BLOCK), BLOCK)
+        rows = pl.ds(pl.multiple_of(i * size, size), size)
         coming = grad[rows, :] if acc is None else grad[rows, :] + acc[rows, :]
         unit = xhat[number, rows, :]
         gain_sum += jnp.sum(coming * unit, 0, keepdims=True)
@@ -482,7 +493,7 @@
         return gain_sum, shift_sum
 
     zero = jnp.zeros((1, width), jnp.float32)
-    gain_sum, shift_sum = lax.fori_loop(0, grad.shape[0] // BLOCK, step, (zero, zero))
+    gain_sum, shift_sum = lax.fori_loop(0, grad.shape[0] // size, step, (zero, zero))
     norms[number : number + 1, :] = gain_sum
     norms[count + number : count + number + 1, :] = shift_sum
 
@@ -608,7 +619,7 @@
                 kept[n, :, tile_at(z)] = tile.astype(bf16)
             return carry
 
-        lax.fori_loop(0, zs, body, 0)
+        lax.fori_loop(0, zs, body, 0, unroll=True)
 
     def halves(tile):
         return tile[:, :128], tile[:, 128:]
@@ -672,18 +683,20 @@
         text_right[7 + j % ups, j // ups] = middle
         return carry
 
-    lax.fori_loop(0, zs * ups // 2, text_up_tile, 0)
+    lax.fori_loop(0, zs * ups // 2, text_up_tile, 0, unroll=3)
     run(22)
-    lax.fori_loop(zs * ups // 2, zs * ups, text_up_tile, 0)
+    lax.fori_loop(zs * ups // 2, zs * ups, text_up_tile, 0, unroll=3)
     run(23)
     down_t = ready(4)
     clear()
 
     def text_down_tile(j, carry):
-        text_acc[...] += dot_nn(text_right[7 + j % ups, j // ups], down_t[tile_at(j), 0:width_t])
-        return carry
-
-    lax.fori_loop(0, zs * ups, text_down_tile, 0)
+        joined = jnp.concatenate([text_right[7 + part, j] for part in range(ups)], -1)
+        rows = pl.ds(pl.multiple_of(j * ups * TILE, TILE), ups * TILE)
+        text_acc[...] += dot_nn(joined, down_t[rows, 0:width_t])
+        return carry
+
+    lax.fori_loop(0, zs, text_down_tile, 0)
     run(24)
     both_i = ready(5)
 
@@ -695,7 +708,7 @@
         image_acc[...] += dot_nn(middle, both_i[offset, 0:width_i])
         return carry
 
-    lax.fori_loop(0, zs, image_up_tile, 0)
+    lax.fori_loop(0, zs, image_up_tile, 0, unroll=True)
     run(25)
     norm_forward(1, text_output, text_acc, text_xhat, text_rstd, text_gains, text_shifts, text_rows.at[1])
     norm_forward(1, image_output, image_acc, image_xhat, image_rstd, image_gains, image_shifts, image_rows.at[1])
@@ -730,7 +743,7 @@
         image_acc[...] += dot_nn(image_context, out_i[tile_at(z), 0:width_i])
         return carry
 
-    lax.fori_loop(0, zs, self_forward_tile, 0)
+    lax.fori_loop(0, zs, self_forward_tile, 0, unroll=2)
     norm_forward(2, text_output, text_acc, text_xhat, text_rstd, text_gains, text_shifts, None)
     norm_forward(2, image_output, image_acc, image_xhat, image_rstd, image_gains, image_shifts, None)
 
@@ -753,11 +766,8 @@
         text_right[10, z] = jnp.concatenate(pieces[0:4], -1)
         text_right[11, z] = jnp.concatenate(pieces[4:8], -1)
         text_right[12, z] = jnp.concatenate(pieces[8:9] + [blank] * 3, -1)
-        total = jnp.zeros((rows_t, width_t), f32)
-        for n, parts in enumerate((dq, dk, dv)):
-            joined = jnp.concatenate(parts + [blank], -1)
-            total += dot_nt(joined, self_t[n * width_t : (n + 1) * width_t, tile_at(z)])
-        text_acc[...] += total
+        joined = [jnp.concatenate(parts + [blank], -1) for parts in (dq, dk, dv)]
+        text_acc[...] += joint_nt(joined, self_t, width_t, z)
         return carry
 
     def dot_nt_rows(coming, weights, z):
@@ -770,17 +780,15 @@
             lambda q, k, v, d: head_back(q, k, v, mask_ii[...], IMAGE_HEAD, d),
             2, *image_tiles, context_grad,
         )
-        total = jnp.zeros((rows_i, width_i), f32)
+        joined = [jnp.concatenate([grads[0][n], grads[1][n]], -1) for n in range(3)]
         for n in range(3):
-            joined = jnp.concatenate([grads[0][n], grads[1][n]], -1)
-            image_right[6 + n, z] = joined
-            total += dot_nt(joined, self_i[n * width_i : (n + 1) * width_i, tile_at(z)])
-        image_acc[...] += total
-        return carry
-
-    lax.fori_loop(0, zs, self_back_image, 0)
+            image_right[6 + n, z] = joined[n]
+        image_acc[...] += joint_nt(joined, self_i, width_i, z)
+        return carry
+
+    lax.fori_loop(0, zs, self_back_image, 0, unroll=True)
     start(9)
-    lax.fori_loop(0, zs, self_back_tile, 0)
+    lax.fori_loop(0, zs, self_back_tile, 0, unroll=2)
     start(10)
     start(11)
     norm_backward(1, text_grad, text_acc, text_xhat, text_rstd, text_gains, text_rows.at[3], text_norms)
@@ -794,7 +802,7 @@
         text_right[4 + j % ups, j // ups] = (middle_grad * text_slope[j]).astype(bf16)
         return carry
 
-    lax.fori_loop(0, zs * ups, text_down_back, 0)
+    lax.fori_loop(0, zs * ups, text_down_back, 0, unroll=4)
     start(12)
     back_i = ready(10)
 
@@ -806,16 +814,17 @@
         image_acc[...] += dot_nt(upper_grad, back_i[0:width_i, tile_at(z)])
         return carry
 
-    lax.fori_loop(0, zs, image_ffn_back, 0)
+    lax.fori_loop(0, zs, image_ffn_back, 0, unroll=True)
     start(13)
     back_up = ready(11)
 
     def text_up_back(j, carry):
-        rows = pl.ds(pl.multiple_of((j // ups) * width_t, 8), width_t)
-        text_acc[...] += dot_nt(text_right[4 + j % ups, j // ups], back_up[rows, tile_at(j % ups)])
-        return carry
-
-    lax.fori_loop(0, zs * ups, text_up_back, 0)
+        joined = jnp.concatenate([text_right[4 + part, j] for part in range(ups)], -1)
+        rows = pl.ds(pl.multiple_of(j * width_t, 8), width_t)
+        text_acc[...] += dot_nt(joined, back_up[rows, 0 : ups * TILE])
+        return carry
+
+    lax.fori_loop(0, zs, text_up_back, 0)
     start(14)
     norm_backward(0, text_grad, text_acc, text_xhat, text_rstd, text_gains, text_rows.at[2], text_norms)
     norm_backward(0, image_grad, image_acc, image_xhat, image_rstd, image_gains, image_rows.at[2], image_norms)
@@ -843,18 +852,14 @@
 
         text_parts = (joined(text_side, 0), joined(image_side, 1), joined(image_side, 2))
         image_parts = (joined(image_side, 0), joined(text_side, 1), joined(text_side, 2))
-        total_t = jnp.zeros((rows_t, width_t), f32)
-        total_i = jnp.zeros((rows_i, width_i), f32)
         for n in range(3):
             text_right[n, z] = text_parts[n]
             image_right[n, z] = image_parts[n]
-            total_t += dot_nt(text_parts[n], cross_t[n * width_t : (n + 1) * width_t, tile_at(z)])
-            total_i += dot_nt(image_parts[n], cross_i[n * width_i : (n + 1) * width_i, tile_at(z)])
-        text_acc[...] += total_t
-        image_acc[...] += total_i
-        return carry
-
-    lax.fori_loop(0, zs, cross_back_tile, 0)
+        text_acc[...] += joint_nt(text_parts, cross_t, width_t, z)
+        image_acc[...] += joint_nt(image_parts, cross_i, width_i, z)
+        return carry
+
+    lax.fori_loop(0, zs, cross_back_tile, 0, unroll=2)
     text_grad[...] += text_acc[...]
     image_grad[...] += image_acc[...]
     finish()
@@ -975,27 +980,15 @@
     if more > 1:
         norm_sums = lax.psum(norm_sums, "dp") / 8
         text_sums, image_sums = outer_sum(text_sums, more), outer_sum(image_sums, more)
-    text_sums = text_sums.transpose(1, 0, 2).reshape(text_sums.shape[1], -1)
-    image_sums = image_sums.transpose(1, 0, 2).reshape(image_sums.shape[1], -1)
-
-    def columns(sums, widths):
-        parts, start = [], 0
-        for width in widths:
-            parts.append(sums[:, start : start + width])
-            start += width
-        return parts
-
-    def triple(parts):
-        return jnp.stack(parts[:3])
-
-    text_widths = [text_cross.shape[-1]] * 3 + [text_cross_out.shape[0]]
-    text_widths += [text_up.shape[-1], text_down.shape[0]]
-    text_widths += [text_self.shape[-1]] * 3 + [text_self_out.shape[0]]
-    image_widths = [image_cross.shape[-1]] * 3 + [image_cross_out.shape[0]]
-    image_widths += [image_up.shape[-1], image_down.shape[0]]
-    image_widths += [image_self.shape[-1]] * 3 + [image_self_out.shape[0]]
-    text_parts = columns(text_sums, text_widths)
-    image_parts = columns(image_sums, image_widths)
+
+    def wide(sums, first, last):
+        return jnp.concatenate([sums[n] for n in range(first, last)], -1)
+
+    share, ups = text_self.shape[-1], text_up.shape[-1] // 256
+    selfs = wide(text_sums, 4 + 2 * ups, text_sums.shape[0])
+    text_parts = [text_sums[0:3], text_sums[3], wide(text_sums, 4, 4 + ups), wide(text_sums, 4 + ups, 4 + 2 * ups)]
+    text_parts += [jnp.stack([selfs[:, n * share : (n + 1) * share] for n in range(3)]), selfs[:, 3 * share :]]
+    image_parts = [image_sums[0:3], image_sums[3], image_sums[4], image_sums[5], image_sums[6:9], image_sums[9]]
     flat_norms = norm_sums.reshape(-1)
     text_size, image_size = text_gains.size, image_gains.size
     text_end = 2 * text_size
@@ -1004,18 +997,18 @@
         image_result,
         text_input_grad,
         image_input_grad,
-        triple(text_parts[:3]),
-        triple(image_parts[:3]),
+        text_parts[0],
+        image_parts[0],
+        text_parts[1].T,
+        image_parts[1].T,
+        text_parts[2],
         text_parts[3].T,
+        image_parts[2],
         image_parts[3].T,
         text_parts[4],
         text_parts[5].T,
         image_parts[4],
         image_parts[5].T,
-        triple(text_parts[6:9]),
-        text_parts[9].T,
-        triple(image_parts[6:9]),
-        image_parts[9].T,
         flat_norms[:text_size].reshape(text_gains.shape),
         flat_norms[text_size:text_end].reshape(text_shifts.shape),
         flat_norms[text_end : text_end + image_size].reshape(image_gains.shape),

time: 440 us -> 440 us (level); the launches traced: 440 us -> 435 us
  Pallas kernels: 412 us -> 407 us
    pallas_call x1, Pallas kernels: 237 us -> 230 us  [layer(): pl.pallas_call(functools.partial(layer_kernel, unit), out_shape=out_shape...]
    unnamed x20 -> x22, local copies, waits for them, and re-layouts: 10.7 us -> 10.4 us
where the time goes in v5:
time: 440 us; the launch traced here: 435 us
  Pallas kernels  407 us (92%)
  local copies, waits for them, and re-layouts  23.7 us (5%)
    pallas_call x1, Pallas kernels, layer(): pl.pallas_call(functools.partial(layer_kernel, unit), out_shape=out_shape...  230 us
    pallas_call x1, Pallas kernels, reduce_all(): pl.pallas_call(functools.partial(reduce_kernel, unit), out_shape=[jax.Sha...  176 us
    unnamed x22, local copies, waits for them, and re-layouts  10.4 us

profile of v5, /device:TPU:0, one launch (start us, length us, event | category | flops | bytes accessed | tf_op | source)
XLA Modules:
  0.0 435.1 jit_solution(8203744955868726379)
XLA Ops:
  0.7 0.0 copy-start.1
  0.7 1.0 copy.54
  1.7 0.7 pad.11.clone
  2.4 0.9 copy.55
  3.3 0.7 pad.12.clone
  4.0 1.1 copy.44
  5.2 0.0 copy-done.1
  5.2 0.6 copy.45
  5.8 1.5 fusion.2.in_i
  7.3 230.4 %layer.1 = (f32[256,768]{1,0:T(8,128)}, f32[96,1024]{1,0:T(8,128)}, f32[256,768]{1,0:T(8,128)}, f32[96,1024]{1,0:T(8,128)}, bf16[2,6,2,2,96,256]{5,4,3,2,1,0:T(8...) custom-call(s32[2]{0:T(128)} %lengths.1, ...), custom_call_target="tpu_custom_call" | custom-call | tf_op jit(solution)/shard_map/layer/pallas_call | solution.py:897
  237.7 1.0 slice.114
  238.7 0.9 copy.52
  239.7 0.7 reshape.99
  240.4 0.8 reshape.100
  241.2 0.6 pad_maximum_fusion.4.norms
  241.8 176.2 %reduce_gradients.1 = (f32[13,96,256]{2,1,0:T(8,128)}, f32[10,128,256]{2,1,0:T(8,128)}, f32[84,128]{1,0:T(8,128)}) custom-call(bf16[2,6,2,2,96,256]{5,4,3,2,1,0:T(8,128)(2,1)} %get-tuple-element.38.text_left, bf16[13,4,256,256]{3,2,1,0:T(8,128)(2,1)} %get-tuple-element.39.text_right, bf16[4,256,256]{2,1,0:T(8,128)(2,1)} %get-tuple-element.40.text_extra, ...), custom_call_target="tpu_custom_call" | custom-call | tf_op jit(solution)/shard_map/reduce_gradients/pallas_call | solution.py:373
  418.0 0.8 fusion.7
  418.8 0.8 fusion.6
  419.6 0.6 reshape.102
  420.2 0.6 reshape.104
  420.8 0.6 reshape.101
  421.4 0.6 reshape.103
  422.0 1.7 slice.89
  423.7 0.0 copy-start.4
  423.7 2.1 slice_bitcast_fusion.8
  425.8 0.0 copy-start
  425.8 0.1 slice_bitcast_fusion.4
  425.9 0.7 copy.50
  426.7 0.7 pad_maximum_fusion.1
  427.4 0.0 copy-done.4
  427.4 0.9 copy.53
  428.4 0.0 copy-done
  428.4 0.7 slice_bitcast_fusion
  429.1 0.0 copy-start.3
  429.1 0.9 fusion.5
  430.0 0.8 copy.51
  430.7 0.8 copy.49
  431.5 0.0 copy-start.2
  431.5 0.8 copy.48
  432.3 0.8 pad_maximum_fusion
  433.1 0.0 copy-done.3
  433.1 0.9 copy.58
  434.0 0.0 copy-done.2
  434.0 0.9 copy.59
  (1 shorter events, 0.0 us)
Async XLA Ops:
  0.7 4.5 %copy-start.1 = (bf16[3,768,192]{1,2,0:T(8,128)(2,1)S(1)}, bf16[3,768,192]{1,2,0:T(8,128)(2,1)}, u32[]{:S(2)}) copy-start(bf16[3,768,192]{1,2,0:T(8,128)(2,1)} %param.34) | copy-start | bytes 2654212
  423.7 3.7 copy-start.4
  425.8 2.6 copy-start
  429.1 4.0 copy-start.3
  431.5 2.5 copy-start.2

commit v6 on v5

--- a/solution.py
+++ b/solution.py
@@ -683,9 +683,9 @@
         text_right[7 + j % ups, j // ups] = middle
         return carry
 
-    lax.fori_loop(0, zs * ups // 2, text_up_tile, 0, unroll=3)
+    lax.fori_loop(0, zs * ups // 2, text_up_tile, 0, unroll=2)
     run(22)
-    lax.fori_loop(zs * ups // 2, zs * ups, text_up_tile, 0, unroll=3)
+    lax.fori_loop(zs * ups // 2, zs * ups, text_up_tile, 0, unroll=2)
     run(23)
     down_t = ready(4)
     clear()
@@ -743,7 +743,7 @@
         image_acc[...] += dot_nn(image_context, out_i[tile_at(z), 0:width_i])
         return carry
 
-    lax.fori_loop(0, zs, self_forward_tile, 0, unroll=2)
+    lax.fori_loop(0, zs, self_forward_tile, 0)
     norm_forward(2, text_output, text_acc, text_xhat, text_rstd, text_gains, text_shifts, None)
     norm_forward(2, image_output, image_acc, image_xhat, image_rstd, image_gains, image_shifts, None)
 
@@ -786,7 +786,7 @@
         image_acc[...] += joint_nt(joined, self_i, width_i, z)
         return carry
 
-    lax.fori_loop(0, zs, self_back_image, 0, unroll=True)
+    lax.fori_loop(0, zs, self_back_image, 0, unroll=2)
     start(9)
     lax.fori_loop(0, zs, self_back_tile, 0, unroll=2)
     start(10)
@@ -802,7 +802,7 @@
         text_right[4 + j % ups, j // ups] = (middle_grad * text_slope[j]).astype(bf16)
         return carry
 
-    lax.fori_loop(0, zs * ups, text_down_back, 0, unroll=4)
+    lax.fori_loop(0, zs * ups, text_down_back, 0, unroll=2)
     start(12)
     back_i = ready(10)
 
@@ -814,7 +814,7 @@
         image_acc[...] += dot_nt(upper_grad, back_i[0:width_i, tile_at(z)])
         return carry
 
-    lax.fori_loop(0, zs, image_ffn_back, 0, unroll=True)
+    lax.fori_loop(0, zs, image_ffn_back, 0, unroll=2)
     start(13)
     back_up = ready(11)
 

time: 440 us -> 429 us (0.975)
  Pallas kernels: 407 us -> 400 us
    pallas_call x1, Pallas kernels: 230 us -> 224 us  [layer(): pl.pallas_call(functools.partial(layer_kernel, unit), out_shape=out_shape...]
where the time goes in v6:
time: 429 us; the launch traced here: 428 us
  Pallas kernels  400 us (93%)
  local copies, waits for them, and re-layouts  23.7 us (6%)
    pallas_call x1, Pallas kernels, layer(): pl.pallas_call(functools.partial(layer_kernel, unit), out_shape=out_shape...  224 us
    pallas_call x1, Pallas kernels, reduce_all(): pl.pallas_call(functools.partial(reduce_kernel, unit), out_shape=[jax.Sha...  176 us
    unnamed x22, local copies, waits for them, and re-layouts  10.4 us

profile of v6, /device:TPU:0, one launch (start us, length us, event | category | flops | bytes accessed | tf_op | source)
XLA Modules:
  0.0 428.1 jit_solution(8229718156179480920)
XLA Ops:
  0.7 0.0 copy-start.1
  0.7 1.0 copy.54
  1.7 0.7 pad.11.clone
  2.4 0.9 copy.55
  3.3 0.7 pad.12.clone
  4.0 1.1 copy.44
  5.2 0.0 copy-done.1
  5.2 0.6 copy.45
  5.8 1.5 fusion.2.in_i
  7.3 223.6 %layer.1 = (f32[256,768]{1,0:T(8,128)}, f32[96,1024]{1,0:T(8,128)}, f32[256,768]{1,0:T(8,128)}, f32[96,1024]{1,0:T(8,128)}, bf16[2,6,2,2,96,256]{5,4,3,2,1,0:T(8...) custom-call(s32[2]{0:T(128)} %lengths.1, ...), custom_call_target="tpu_custom_call" | custom-call | tf_op jit(solution)/shard_map/layer/pallas_call | solution.py:897
  230.9 1.0 slice.114
  231.9 0.9 copy.52
  232.9 0.7 reshape.99
  233.6 0.8 reshape.100
  234.4 0.6 pad_maximum_fusion.4.norms
  235.0 176.2 %reduce_gradients.1 = (f32[13,96,256]{2,1,0:T(8,128)}, f32[10,128,256]{2,1,0:T(8,128)}, f32[84,128]{1,0:T(8,128)}) custom-call(bf16[2,6,2,2,96,256]{5,4,3,2,1,0:T(8,128)(2,1)} %get-tuple-element.38.text_left, bf16[13,4,256,256]{3,2,1,0:T(8,128)(2,1)} %get-tuple-element.39.text_right, bf16[4,256,256]{2,1,0:T(8,128)(2,1)} %get-tuple-element.40.text_extra, ...), custom_call_target="tpu_custom_call" | custom-call | tf_op jit(solution)/shard_map/reduce_gradients/pallas_call | solution.py:373
  411.2 0.8 fusion.7
  412.0 0.8 fusion.6
  412.8 0.6 reshape.102
  413.4 0.6 reshape.104
  414.0 0.6 reshape.101
  414.6 0.6 reshape.103
  415.3 1.7 slice.89
  417.0 0.0 copy-start.4
  417.0 2.1 slice_bitcast_fusion.8
  419.0 0.0 copy-start
  419.0 0.1 slice_bitcast_fusion.4
  419.1 0.7 copy.50
  419.9 0.7 pad_maximum_fusion.1
  420.6 0.0 copy-done.4
  420.7 0.9 copy.53
  421.6 0.0 copy-done
  421.6 0.7 slice_bitcast_fusion
  422.3 0.0 copy-start.3
  422.3 0.9 fusion.5
  423.2 0.8 copy.51
  424.0 0.8 copy.49
  424.7 0.0 copy-start.2
  424.7 0.8 copy.48
  425.5 0.8 pad_maximum_fusion
  426.3 0.0 copy-done.3
  426.3 0.9 copy.58
  427.2 0.0 copy-done.2
  427.2 0.9 copy.59
  (1 shorter events, 0.0 us)
Async XLA Ops:
  0.7 4.5 %copy-start.1 = (bf16[3,768,192]{1,2,0:T(8,128)(2,1)S(1)}, bf16[3,768,192]{1,2,0:T(8,128)(2,1)}, u32[]{:S(2)}) copy-start(bf16[3,768,192]{1,2,0:T(8,128)(2,1)} %param.34) | copy-start | bytes 2654212
  417.0 3.7 copy-start.4
  419.0 2.6 copy-start
  422.3 4.0 copy-start.3
  424.7 2.5 copy-start.2

commit v7 on v6

--- a/solution.py
+++ b/solution.py
@@ -498,9 +498,9 @@
     norms[count + number : count + number + 1, :] = shift_sum
 
 
-def turn_over(left, tokens, rows):
+def turn_over(left, sources):
     part = left.shape[4]
-    for number, source in enumerate((tokens, rows.at[2], rows.at[0], rows.at[3], rows.at[1], rows.at[4])):
+    for number, source in sources:
         turned = source[...].T
         for y in range(2):
             for x in range(2):
@@ -714,6 +714,10 @@
     norm_forward(1, image_output, image_acc, image_xhat, image_rstd, image_gains, image_shifts, image_rows.at[1])
 
     clear()
+    run(26)
+    turn_over(text_left, ((0, text_tokens), (2, text_rows.at[0]), (4, text_rows.at[1])))
+    run(27)
+    turn_over(image_left, ((0, image_tokens), (2, image_rows.at[0]), (4, image_rows.at[1])))
     start(6)
     start(7)
     start(8)
@@ -863,8 +867,8 @@
     text_grad[...] += text_acc[...]
     image_grad[...] += image_acc[...]
     finish()
-    turn_over(text_left, text_tokens, text_rows)
-    turn_over(image_left, image_tokens, image_rows)
+    for left, rows in ((text_left, text_rows), (image_left, image_rows)):
+        turn_over(left, ((1, rows.at[2]), (3, rows.at[3]), (5, rows.at[4])))
 
 
 def layer(lengths, counts, rows, params, weights, mp, unit):

time: 429 us -> 429 us (level)
  no operation moved by 1% of the time
where the time goes in v7:
time: 429 us; the launch traced here: 428 us
  Pallas kernels  400 us (93%)
  local copies, waits for them, and re-layouts  23.7 us (6%)
    pallas_call x1, Pallas kernels, layer(): pl.pallas_call(functools.partial(layer_kernel, unit), out_shape=out_shape...  223 us
    pallas_call x1, Pallas kernels, reduce_all(): pl.pallas_call(functools.partial(reduce_kernel, unit), out_shape=[jax.Sha...  176 us
    unnamed x22, local copies, waits for them, and re-layouts  10.4 us

profile of v7, /device:TPU:0, one launch (start us, length us, event | category | flops | bytes accessed | tf_op | source)
XLA Modules:
  0.0 428.0 jit_solution(379055021302704625)
XLA Ops:
  0.7 0.0 copy-start.1
  0.7 1.0 copy.54
  1.7 0.7 pad.11.clone
  2.4 0.9 copy.55
  3.3 0.7 pad.12.clone
  4.0 1.1 copy.44
  5.2 0.0 copy-done.1
  5.2 0.6 copy.45
  5.8 1.5 fusion.2.in_i
  7.3 223.4 %layer.1 = (f32[256,768]{1,0:T(8,128)}, f32[96,1024]{1,0:T(8,128)}, f32[256,768]{1,0:T(8,128)}, f32[96,1024]{1,0:T(8,128)}, bf16[2,6,2,2,96,256]{5,4,3,2,1,0:T(8...) custom-call(s32[2]{0:T(128)} %lengths.1, ...), custom_call_target="tpu_custom_call" | custom-call | tf_op jit(solution)/shard_map/layer/pallas_call | solution.py:901
  230.7 1.0 slice.114
  231.7 0.9 copy.52
  232.7 0.7 reshape.99
  233.4 0.8 reshape.100
  234.2 0.6 pad_maximum_fusion.4.norms
  234.8 176.3 %reduce_gradients.1 = (f32[13,96,256]{2,1,0:T(8,128)}, f32[10,128,256]{2,1,0:T(8,128)}, f32[84,128]{1,0:T(8,128)}) custom-call(bf16[2,6,2,2,96,256]{5,4,3,2,1,0:T(8,128)(2,1)} %get-tuple-element.38.text_left, bf16[13,4,256,256]{3,2,1,0:T(8,128)(2,1)} %get-tuple-element.39.text_right, bf16[4,256,256]{2,1,0:T(8,128)(2,1)} %get-tuple-element.40.text_extra, ...), custom_call_target="tpu_custom_call" | custom-call | tf_op jit(solution)/shard_map/reduce_gradients/pallas_call | solution.py:373
  411.1 0.8 fusion.7
  411.9 0.8 fusion.6
  412.7 0.6 reshape.102
  413.3 0.6 reshape.104
  413.9 0.6 reshape.101
  414.5 0.6 reshape.103
  415.1 1.7 slice.89
  416.8 0.0 copy-start.4
  416.8 2.1 slice_bitcast_fusion.8
  418.9 0.0 copy-start
  418.9 0.1 slice_bitcast_fusion.4
  419.0 0.7 copy.50
  419.8 0.7 pad_maximum_fusion.1
  420.5 0.0 copy-done.4
  420.5 0.9 copy.53
  421.5 0.0 copy-done
  421.5 0.7 slice_bitcast_fusion
  422.2 0.0 copy-start.3
  422.2 0.9 fusion.5
  423.1 0.8 copy.51
  423.8 0.8 copy.49
  424.6 0.0 copy-start.2
  424.6 0.8 copy.48
  425.4 0.8 pad_maximum_fusion
  426.2 0.0 copy-done.3
  426.2 0.9 copy.58
  427.1 0.0 copy-done.2
  427.1 0.9 copy.59
  (1 shorter events, 0.0 us)
Async XLA Ops:
  0.7 4.5 %copy-start.1 = (bf16[3,768,192]{1,2,0:T(8,128)(2,1)S(1)}, bf16[3,768,192]{1,2,0:T(8,128)(2,1)}, u32[]{:S(2)}) copy-start(bf16[3,768,192]{1,2,0:T(8,128)(2,1)} %param.34) | copy-start | bytes 2654212
  416.8 3.7 copy-start.4
  418.9 2.6 copy-start
  422.2 4.0 copy-start.3
  424.6 2.5 copy-start.2
